TPU v7x, 32 devices: a whole 2x2x4 slice. The times are simulated.
32 devices in a mesh: groups: 2 (over x), seq: 8 (over z, y), segment: 2 (over core).
Axes of the slice: x: 2, y: 2, z: 4, core: 2. Of those that a mesh axis runs over, the one named last changes fastest.
Arguments:
- queue_frames: bfloat16 [32, 32, 5120], P(('groups', 'segment'), 'seq'), parts along dimension 0, may hold values from -450 to 450
- fresh_frames: bfloat16 [2, 32, 5120], P('groups', 'seq'), parts along dimension 0, may hold values from -450 to 450
- slot_level: int32 [32], P(('groups', 'segment')), parts along dimension 0, may hold values from 0 to 49
- window_start: int32 [32], P(('groups', 'segment')), parts along dimension 0, may hold values from 0 to 3
- shift_table: float32 [50, 5120], replicated, may hold values from -3 to 3
- scale_table: float32 [50, 5120], replicated, may hold values from -1.5 to 1.5
- gate_table: float32 [50, 5120], replicated, may hold values from -10 to 10
- w_query: bfloat16 [5120, 4096], P(None, 'seq'), may hold values from -3.5 to 3.5
- w_key: bfloat16 [5120, 4096], P(None, 'seq'), may hold values from -3.5 to 3.5
- w_value: bfloat16 [5120, 4096], P(None, 'seq'), may hold values from -0.078125 to 0.078125
- w_out: bfloat16 [4096, 5120], P('seq'), may hold values from -0.5 to 0.5
- query_gain: float32 [4096], P('seq'), may hold values from 0.1 to 1.9
- key_gain: float32 [4096], P('seq'), may hold values from 0.1 to 1.9
Outputs:
- queue_out: bfloat16 [32, 32, 5120], P(('groups', 'segment'), 'seq'), parts along dimension 0
- departed: bfloat16 [4, 1, 32, 5120], P(('groups', 'segment'), None, 'seq'), parts along dimension 0
There are 2 independent parts, one for each index of `groups`. A program takes and returns all parts, laid end to end along the dimension named above; an argument that names none is the same for every part. Nothing has to cross between parts.
All inputs are finite; a program needn't handle non-finite values.
Results may differ from a plain program's by a relative error of at most 0.02.
Values may be sent and summed in bfloat16 or wider, within the bound.
No kernel may reach another device: no remote copies, remote signals or barrier semaphores. Data moves between devices by JAX's collectives and lax.ppermute only.
A program may use at most 128 MiB of HBM per device.

v0:
```python
import jax
import jax.numpy as jnp
from jax import lax
from jax.sharding import PartitionSpec as P

HD = 128
HEADS = 32
KEYWIN = 4


epsilon = 1e-06
masked_score = -1e30


def from_behind(block, axis, distance):
    devices = range(lax.axis_size(axis))
    route = [(i - distance, i) for i in devices if i - distance in devices]
    return lax.ppermute(block, axis, route)


def extended(x, sides, width):
    for axis, dim in sides:
        peers, length = (lax.axis_size(axis), x.shape[dim])
        up = [(i, (i + 1) % peers) for i in range(peers - 1)]
        down = [(j, i) for i, j in up]
        last = lax.slice_in_dim(x, length - width, length, axis=dim)
        leading = lax.slice_in_dim(x, 0, width, axis=dim)
        before = lax.ppermute(last, axis, up)
        after = lax.ppermute(leading, axis, down)
        x = jnp.concatenate([before, x, after], axis=dim)
    return x


def modulate(level_ids, lookup):
    onehot = (level_ids[:, None] == jnp.arange(lookup.shape[0], dtype=jnp.int32)[None, :]).astype(
        jnp.float32
    )
    return jnp.dot(onehot, lookup, precision=lax.Precision.HIGHEST)


def scaled(raw, total_squares, gain):
    inverse = lax.rsqrt(total_squares / (HEADS * HD) + epsilon)
    return (raw * inverse[:, :, None] * gain).astype(jnp.bfloat16)


def attend(queries, keys, value_rows, window_start, segment_idx, queue_len):
    rim_width = KEYWIN - 1
    frames = queries.shape[0]
    token_count = queries.shape[1]
    local_width = queries.shape[2]
    heads_local = local_width // HD
    begins = jnp.arange(frames, dtype=jnp.int32) + rim_width - window_start

    def window(source):

        def take(begin):
            return lax.dynamic_slice_in_dim(source, begin, KEYWIN, 0)

        return jax.vmap(take)(begins).reshape(frames, KEYWIN * token_count, heads_local, HD)

    key_rows = window(keys)
    value_win = window(value_rows)
    frame_ids = (
        segment_idx * frames
        + begins[:, None]
        - rim_width
        + jnp.arange(KEYWIN, dtype=jnp.int32)[None, :]
    )
    usable = jnp.repeat((frame_ids >= 0) & (frame_ids < queue_len), token_count, axis=1)
    query_heads = queries.reshape(frames, token_count, heads_local, HD)
    scores = jnp.einsum(
        "fqhd,fkhd->fhqk", query_heads, key_rows, preferred_element_type=jnp.float32
    ) * HD ** (-0.5)
    scores = jnp.where(usable[:, None, None, :], scores, masked_score)
    largest = jnp.max(scores, axis=3, keepdims=True)
    lifted = jnp.exp(scores - largest)
    totals = jnp.sum(lifted, axis=3, keepdims=True)
    weights = (lifted / totals).astype(jnp.bfloat16)
    outputs = jnp.einsum("fhqk,fkhd->qfhd", weights, value_win, preferred_element_type=jnp.float32)
    return outputs.astype(jnp.bfloat16).reshape(token_count, frames, local_width)


def handoff(updated, incoming):
    handed = from_behind(updated[0], "segment", -1)
    last_segment = lax.axis_index("segment") == lax.axis_size("segment") - 1
    arriving = jnp.where(last_segment, incoming, handed)
    return jnp.concatenate([updated[1:], arriving[None]], axis=0)


def shards(
    queue_frames,
    fresh_frames,
    slot_level,
    window_start,
    shift_table,
    scale_table,
    gate_table,
    w_query,
    w_key,
    w_value,
    w_out,
    query_gain,
    key_gain,
):
    segment_idx = lax.axis_index("segment")
    frames = queue_frames.shape[0]
    queue_len = frames * lax.axis_size("segment")
    rim_width = KEYWIN - 1
    local_width = w_query.shape[1]
    w_joined = jnp.concatenate([w_query, w_key, w_value], axis=1)
    shift_rows = modulate(slot_level, shift_table)
    scale_rows = modulate(slot_level, scale_table)
    gate_rows = modulate(slot_level, gate_table)
    queue_state = queue_frames
    values_in = queue_state.astype(jnp.float32)
    inverse = lax.rsqrt(jnp.mean(values_in * values_in, axis=2) + epsilon)
    hidden = (
        values_in * inverse[:, :, None] * (1.0 + scale_rows[:, None]) + shift_rows[:, None]
    ).astype(jnp.bfloat16)
    joined = jnp.einsum(
        "ftd,de->fte",
        lax.all_gather(hidden, "seq", axis=1, tiled=True),
        w_joined,
        preferred_element_type=jnp.float32,
    )
    q_raw = joined[:, :, :local_width]
    k_raw = joined[:, :, local_width : 2 * local_width]
    own_values = joined[:, :, 2 * local_width :].astype(jnp.bfloat16)
    q_squares, k_squares = lax.psum(
        (jnp.sum(q_raw * q_raw, axis=2), jnp.sum(k_raw * k_raw, axis=2)), "seq"
    )
    queries = scaled(q_raw, q_squares, query_gain)
    own_keys = scaled(k_raw, k_squares, key_gain)
    paired = extended(jnp.stack([own_keys, own_values]), (("segment", 1),), rim_width)
    keys = paired[0]
    value_rows = paired[1]
    attended = attend(queries, keys, value_rows, window_start, segment_idx, queue_len)
    partial_value = jnp.einsum(
        "tfe,ed->tfd", attended, w_out, preferred_element_type=jnp.float32
    ).astype(jnp.bfloat16)
    partial_value = lax.optimization_barrier(partial_value)
    summed = lax.psum_scatter(
        partial_value.astype(jnp.float32).astype(jnp.bfloat16),
        "seq",
        scatter_dimension=0,
        tiled=True,
    ).astype(jnp.float32)
    projected = jnp.transpose(summed, (1, 0, 2))
    updated = (values_in + gate_rows[:, None] * projected).astype(jnp.bfloat16)
    departed = [updated[0]]
    queue_state = handoff(updated, fresh_frames[0])
    return (queue_state, jnp.stack(departed)[None])


def solution(mesh):
    return jax.shard_map(
        shards,
        mesh=mesh,
        in_specs=(
            P(("groups", "segment"), "seq", None),
            P("groups", "seq", None),
            P(("groups", "segment")),
            P(("groups", "segment")),
            P(),
            P(),
            P(),
            P(None, "seq"),
            P(None, "seq"),
            P(None, "seq"),
            P("seq", None),
            P("seq"),
            P("seq"),
        ),
        out_specs=(
            P(("groups", "segment"), "seq", None),
            P(("groups", "segment"), None, "seq", None),
        ),
        check_vma=False,
    )
```

profile of v0, /device:TPU:0, one launch (start us, length us, event | category | flops | bytes accessed | tf_op | source)
XLA Modules:
  0.0 200.4 jit_solution(8836512309598153663)
XLA Ops:
  7.2 0.0 copy-start
  7.2 0.0 all-gather.2.cloned.1.call-start
  7.2 1.2 copy-done
  8.4 1.1 convolution_add_fusion
  9.6 1.7 fusion.26
  11.3 1.2 fusion.10
  12.6 1.9 fusion.13
  14.5 0.0 all-gather.2.cloned.1.call-update
  14.5 0.0 reduce-scatter.2.cloned.1.call-start
  14.5 0.7 add_add_fusion
  15.2 56.6 %all-gather.2.cloned.1.call-done = bf16[8,32,5120]{2,0,1:T(8,128)(2,1)} async-done(((bf16[8,4,5120]{2,0,1:T(8,128)(2,1)}), bf16[8,32,5120]{2,0,1:T(8,128)(2,1)}) %all-gather.2.cloned.1.call-update) | async-done | bytes 2621456 | tf_op jit(solution)/shard_map/all_gather | solution.py:122
  71.8 8.6 %fusion.1 = f32[8,32,1536]{2,1,0:T(8,128)S(1)} fusion(bf16[5120,512]{1,0:T(8,128)(2,1)} %param.22, bf16[5120,512]{1,0:T(8,128)(2,1)} %param.21, bf16[5120,512]{1,0:T(8,128)(2,1)} %param.20, bf16[8,32,5120]{2,0,1:T(8,128)(2,1)} %all-gather.2.cloned.1.call-done), kind=kOutput, calls=%fused_computation.4 | convolution fusion | flops 4073717760 | bytes 19922944 | tf_op jit(solution)/shard_map/ftd,de->fte/dot_general | solution.py:120
  80.3 0.1 multiply_reduce_fusion
  80.5 19.3 %all-reduce.1 = (f32[8,32]{1,0:T(8,128)S(1)}, f32[8,32]{1,0:T(8,128)S(1)}) all-reduce(f32[8,32]{1,0:T(8,128)S(1)} %get-tuple-element.7, f32[8,32]{1,0:T(8,128)S(1)} %get-tuple-element.6), channel_id=1, replica_groups=mesh['groups'=2,'seq'=8,'segment'=2] {'seq'}, use_global_device_ids=true, to_apply=%region_2.0 | all-reduce | flops 512 | bytes 4096 | tf_op jit(solution)/shard_map/psum | solution.py:129
  99.9 0.0 copy-done.6
  99.9 0.2 fusion.16
  100.1 1.3 collective-permute-start
  101.4 1.3 collective-permute-start.1
  102.7 0.1 fusion.28
  102.8 0.1 broadcast_in_dim.17
  102.9 0.1 broadcast_in_dim.18
  103.0 0.0 collective-permute-done
  103.0 1.8 collective-permute-done.1
  104.8 0.1 pad_maximum_fusion
  104.9 0.1 slice_bitcast_fusion.1
  105.0 1.6 gather_fusion.1
  106.6 1.3 reshape.38
  107.9 0.6 fusion.5
  108.6 0.4 fusion.36
  108.9 0.6 gather_fusion
  109.6 1.1 reshape.36
  110.7 3.0 %fusion.7 = bf16[32,8,4,128]{3,0,2,1:T(8,128)(2,1)S(1)} fusion(bf16[8,128,4,128]{3,2,1,0:T(4,128)(2,1)} %reshape.36, f32[8,4,32]{2,1,0:T(4,128)S(1)} %fusion.36, f32[8,4,32,128]{3,2,1,0:T(8,128)S(1)} %fusion.5), kind=kOutput, calls=%fused_computation.14 | convolution fusion | flops 34079872 | bytes 1839104 | tf_op jit(solution)/shard_map/fhqk,fkhd->qfhd/dot_general | solution.py:79
  113.7 0.0 copy-start.5
  113.8 0.0 copy-start.1
  113.8 0.0 copy-start.3
  113.8 5.7 %convolution_convert_fusion = bf16[32,8,5120]{2,1,0:T(8,128)(2,1)} fusion(bf16[512,5120]{1,0:T(8,128)(2,1)} %param.23, bf16[32,8,4,128]{3,0,2,1:T(8,128)(2,1)S(1)} %fusion.7), kind=kOutput, calls=%fused_computation.5 | convolution fusion | flops 1343488000 | bytes 8126464 | tf_op jit(solution)/shard_map/tfe,ed->tfd/dot_general | solution.py:138
  119.5 0.0 reduce-scatter.2.cloned.1.call-update
  119.5 0.5 fusion.27
  120.0 67.9 %reduce-scatter.2.cloned.1.call-done = bf16[4,8,5120]{2,1,0:T(8,128)(2,1)} async-done(((bf16[32,8,5120]{2,1,0:T(8,128)(2,1)}), bf16[4,8,5120]{2,1,0:T(8,128)(2,1)}) %reduce-scatter.2.cloned.1.call-update) | async-done | bytes 327696 | tf_op jit(solution)/shard_map/reduce_scatter | solution.py:142
  188.0 1.1 fusion.14
  189.2 0.0 copy-start.4
  189.2 1.3 collective-permute-start.2
  190.5 0.1 slice.49
  190.5 1.7 collective-permute-done.2
  192.3 0.1 copy.38
  192.4 0.2 pad_maximum_fusion.1
  192.6 1.0 copy.39
  193.5 0.0 copy-done.4
  (15 shorter events, 0.2 us)
Async XLA Ops:
  7.2 1.3 copy-start
  7.2 64.6 %all-gather.2.cloned.1.call-start = ((), (), s32[]{:S(2)}) async-start(), calls=%async_computation.1 | async-start | bytes 2949120 | tf_op jit(solution)/shard_map/all_gather | solution.py:122
  14.5 173.5 %reduce-scatter.2.cloned.1.call-start = ((), (), s32[]{:S(2)}) async-start(), calls=%async_computation.2 | async-start | bytes 2949120 | tf_op jit(solution)/shard_map/reduce_scatter | solution.py:142
  15.2 84.7 %copy-start.6 = (f32[512]{0:T(512)S(1)}, f32[512]{0:T(512)}, u32[]{:S(2)}) copy-start(f32[512]{0:T(512)} %param.24) | copy-start | bytes 6148
  15.2 84.7 %copy-start.7 = (f32[512]{0:T(512)S(1)}, f32[512]{0:T(512)}, u32[]{:S(2)}) copy-start(f32[512]{0:T(512)} %param.25) | copy-start | bytes 6148
  100.1 2.9 %collective-permute-start = (bf16[2,3,32,512]{3,2,1,0:T(8,128)(2,1)S(1)}, bf16[2,3,32,512]{3,2,1,0:T(8,128)(2,1)S(1)}, u32[]{:S(2)}, u32[]{:S(2)}) collective-permute-start(bf16[2,3,32,512]{3,2,1,0:T(8,128)(2,1)S(1)} %get-tuple-element.14), channel_id=1, source_target_pairs={{0,1},{2,3},{4,5},{6,7},{8,9},{10,11},{12,13},{14,15},{16,17},{18,... | collective-permute-start | bytes 589832 | tf_op jit(solution)/shard_map/ppermute | solution.py:28
  101.4 3.3 %collective-permute-start.1 = (bf16[2,3,32,512]{3,2,1,0:T(8,128)(2,1)S(1)}, bf16[2,3,32,512]{3,2,1,0:T(8,128)(2,1)S(1)}, u32[]{:S(2)}, u32[]{:S(2)}) collective-permute-start(bf16[2,3,32,512]{3,2,1,0:T(8,128)(2,1)S(1)} %get-tuple-element.15), channel_id=1, source_target_pairs={{1,0},{3,2},{5,4},{7,6},{9,8},{11,10},{13,12},{15,14},{17,16},{19,... | collective-permute-start | bytes 589832 | tf_op jit(solution)/shard_map/ppermute | solution.py:29
  113.7 5.8 %copy-start.2 = (f32[50,5120]{1,0:T(8,128)S(1)}, f32[50,5120]{1,0:T(8,128)}, u32[]{:S(2)}) copy-start(f32[50,5120]{1,0:T(8,128)} %param.19) | copy-start | bytes 3072004
  113.7 5.8 %copy-start.5 = (s32[8]{0:T(128)S(1)}, s32[8]{0:T(128)}, u32[]{:S(2)}) copy-start(s32[8]{0:T(128)} %param.15) | copy-start | bytes 100
  113.8 74.2 %copy-start.1 = (bf16[8,4,5120]{2,1,0:T(4,128)(2,1)S(1)}, bf16[8,4,5120]{2,1,0:T(4,128)(2,1)}, u32[]{:S(2)}) copy-start(bf16[8,4,5120]{2,1,0:T(4,128)(2,1)} %param.13) | copy-start | bytes 983044
  113.8 78.5 %copy-start.3 = (bf16[1,4,5120]{2,1,0:T(4,128)(2,1)S(1)}, bf16[1,4,5120]{2,1,0:T(4,128)(2,1)}, u32[]{:S(2)}) copy-start(bf16[1,4,5120]{2,1,0:T(4,128)(2,1)} %param.14) | copy-start | bytes 122884
  189.2 4.4 %copy-start.4 = (bf16[1,4,5120]{2,1,0:T(4,128)(2,1)}, bf16[1,4,5120]{2,1,0:T(4,128)(2,1)S(1)}, u32[]{:S(2)}) copy-start(bf16[1,4,5120]{2,1,0:T(4,128)(2,1)S(1)} %copy.62) | copy-start | bytes 122884
  189.2 3.1 %collective-permute-start.2 = (bf16[4,5120]{1,0:T(4,128)(2,1)S(1)}, bf16[4,5120]{1,0:T(4,128)(2,1)S(1)}, u32[]{:S(2)}, u32[]{:S(2)}) collective-permute-start(bf16[4,5120]{1,0:T(4,128)(2,1)S(1)} %bitcast.46), channel_id=1, source_target_pairs={{1,0},{3,2},{5,4},{7,6},{9,8},{11,10},{13,12},{15,14},{17,16},{19,... | collective-permute-start | bytes 122888 | tf_op jit(solution)/shard_map/ppermute | solution.py:18
Sparse Core Ops, SparseCore 0:
  14.6 57.1 all-gather.1
  119.6 68.2 reduce-scatter.1
where the time goes:
time: 201 us; the launch traced here: 200 us
  waiting for transfers between devices  128 us (64%)
  matrix products  21.3 us (11%)
  blocking collectives  19.3 us (10%)
  between operations  14.3 us (7%)
  local copies, waits for them, and re-layouts  7.4 us (4%)
  other arithmetic  6.01 us (3%)
  starting transfers between devices  3.97 us (2%)
    reduce_scatter x1, waiting for transfers between devices, shards(): lax.psum_scatter(partial_value.astype(jnp.float32).astype(jnp.bfloat16),...  67.9 us
    all_gather x1, waiting for transfers between devices, shards(): lax.all_gather(hidden, 'seq', axis=1, tiled=True)  56.6 us
    psum x1, blocking collectives, shards(): lax.psum((jnp.sum(q_raw * q_raw, axis=2), jnp.sum(k_raw * k_raw, axis=2))...  19.3 us
    dot_general x1, matrix products, shards(): jnp.einsum('ftd,de->fte', lax.all_gather(hidden, 'seq', axis=1, tiled=Tru...  8.56 us
    dot_general x1, matrix products, shards(): jnp.einsum('tfe,ed->tfd', attended, w_out, preferred_element_type=jnp.flo...  5.7 us
  transfers between devices with their start and end apart: 5, of which 4 were waited for; matrix products, arithmetic and copies ran while one was open for 1% of the time, Pallas kernels for 0%

commit v1 on v0

v1 whole, which is shorter than its diff:
```python
import functools

import jax
import jax.numpy as jnp
from jax import lax
from jax.experimental import pallas as pl
from jax.experimental.pallas import tpu as pltpu
from jax.sharding import PartitionSpec as P

HD = 128
KEYWIN = 4


epsilon = 1e-06
masked_score = -1e30
VMEM_LIMIT = 16 << 20
WHOLE = pl.BlockSpec(memory_space=pltpu.VMEM)
SCALARS = pl.BlockSpec(memory_space=pltpu.SMEM)


def call(kernel, ins, outs, flops, scalars=0, scratch=(), limit=VMEM_LIMIT):
    moved = sum(x.size * x.dtype.itemsize for x in list(ins) + list(outs))
    return pl.pallas_call(
        kernel,
        in_specs=[SCALARS] * scalars + [WHOLE] * (len(ins) - scalars),
        out_specs=[WHOLE] * len(outs),
        out_shape=list(outs),
        scratch_shapes=list(scratch),
        compiler_params=pltpu.CompilerParams(vmem_limit_bytes=limit),
        cost_estimate=pl.CostEstimate(flops=flops, bytes_accessed=moved, transcendentals=0),
    )(*ins)


def like(shape, dtype=jnp.bfloat16):
    return jax.ShapeDtypeStruct(shape, dtype)


def rows_kernel(level_ref, *refs):
    tables, outs = refs[: len(refs) // 2], refs[len(refs) // 2 :]
    for f in range(outs[0].shape[0]):
        level = level_ref[f]
        for table, out in zip(tables, outs):
            out[f : f + 1, :] = table[pl.ds(level, 1), :]


def slot_rows(levels, tables):
    outs = [like((levels.shape[0], table.shape[1]), table.dtype) for table in tables]
    return call(rows_kernel, [levels, *tables], outs, 1000, scalars=1)


def place(column, first, total):
    rows = column.shape[0]
    lanes = lax.broadcasted_iota(jnp.int32, (rows, total), 1)
    picked = lanes == lax.broadcasted_iota(jnp.int32, (rows, total), 0) + first
    return jnp.sum(jnp.where(picked, column, 0.0), axis=0, keepdims=True)


def unplace(row, first, rows):
    total = row.shape[1]
    lanes = lax.broadcasted_iota(jnp.int32, (rows, total), 1)
    picked = lanes == lax.broadcasted_iota(jnp.int32, (rows, total), 0) + first
    return jnp.sum(jnp.where(picked, row, 0.0), axis=1, keepdims=True)


def row_of(position, offset, peers, rows):
    return pl.multiple_of(lax.rem(position + offset, peers) * rows, rows)


def project_kernel(first_frames, offsets, peers, position_ref, *refs):
    count = len(first_frames)
    x_refs, refs = refs[:count], refs[count:]
    scale_ref, shift_ref, wq_ref, wk_ref, wv_ref, gq_ref, gk_ref, q_ref, kv_ref, sq_ref, h_ref = refs
    row = 0
    for x_ref, first in zip(x_refs, first_frames):
        frames, tokens, width = x_ref.shape
        x = x_ref[...].astype(jnp.float32)
        inverse = lax.rsqrt(jnp.mean(x * x, axis=2, keepdims=True) + epsilon)
        scale = 1.0 + scale_ref[first : first + frames, :][:, None, :]
        shift = shift_ref[first : first + frames, :][:, None, :]
        hidden = (x * inverse * scale + shift).astype(jnp.bfloat16)
        h_ref[row : row + frames * tokens, :] = hidden.reshape(frames * tokens, width)
        row += frames * tokens
    rows = row // len(offsets)
    total = sq_ref.shape[1]
    hidden = h_ref[...]

    def squares_of(raw):
        column = jnp.sum(raw * raw, axis=1, keepdims=True)
        parts = [
            place(column[i * rows : (i + 1) * rows], row_of(position_ref[0], offset, peers, rows), total)
            for i, offset in enumerate(offsets)
        ]
        return sum(parts[1:], parts[0])

    q_raw = jnp.dot(hidden, wq_ref[...], preferred_element_type=jnp.float32)
    sq_ref[0:1, :] = squares_of(q_raw)
    q_ref[...] = (q_raw * gq_ref[...]).astype(jnp.bfloat16)
    k_raw = jnp.dot(hidden, wk_ref[...], preferred_element_type=jnp.float32)
    sq_ref[1:2, :] = squares_of(k_raw)
    kv_ref[0] = (k_raw * gk_ref[...]).astype(jnp.bfloat16)
    value = jnp.dot(hidden, wv_ref[...], preferred_element_type=jnp.float32)
    kv_ref[1] = value.astype(jnp.bfloat16)


def project(blocks, first_frames, offsets, peers, position, scale_rows, shift_rows, weights, gains):
    width, local = weights[0].shape
    rows = sum(x.shape[0] * x.shape[1] for x in blocks)
    total = rows // len(offsets) * peers
    return call(
        functools.partial(project_kernel, tuple(first_frames), tuple(offsets), peers),
        [position, *blocks, scale_rows, shift_rows, *weights, *gains],
        [like((rows, local)), like((2, rows, local)), like((2, total), jnp.float32)],
        6 * rows * width * local,
        scalars=1,
        scratch=[pltpu.VMEM((rows, width), jnp.bfloat16)],
    )


def gather_kernel(offsets, peers, rows, position_ref, *refs):
    kv_refs, out_ref = refs[:-1], refs[-1]
    for i, kv_ref in enumerate(kv_refs):
        base = i // len(offsets) * peers * rows
        for j, offset in enumerate(offsets[i % len(offsets)]):
            at = row_of(position_ref[0], offset, peers, rows)
            out_ref[:, pl.ds(base + at, rows), :] = kv_ref[:, j * rows : (j + 1) * rows, :]


def gather(sets, offsets, peers, rows, position):
    local = sets[0][0].shape[2]
    return call(
        functools.partial(gather_kernel, tuple(map(tuple, offsets)), peers, rows),
        [position, *(kv for kvs in sets for kv in kvs)],
        [like((2, len(sets) * peers * rows, local))],
        1000,
        scalars=1,
    )[0]


def attend_kernel(sizes, peers, inner, offsets, position_ref, start_ref, base_ref, q_ref, kv_ref, sq_ref, out_ref):
    frames, tokens, queue_len = sizes
    rows, local = q_ref.shape
    block = rows // len(offsets)
    columns = kv_ref.shape[1]
    total = sq_ref.shape[1]
    inverse_q_row = lax.rsqrt(sq_ref[0:1, :] / inner + epsilon)
    parts = [unplace(inverse_q_row, row_of(position_ref[0], offset, peers, block), block) for offset in offsets]
    inverse_q = parts[0] if len(parts) == 1 else jnp.concatenate(parts, axis=0)
    parts = [lax.rsqrt(sq_ref[1 + i : 2 + i, :] / inner + epsilon) for i in range(columns // total)]
    inverse_k = parts[0] if len(parts) == 1 else jnp.concatenate(parts, axis=1)
    row_frame = lax.broadcasted_iota(jnp.int32, (rows, columns), 0) // tokens % frames
    column = lax.broadcasted_iota(jnp.int32, (rows, columns), 1)
    column_frame = column // tokens % frames
    key_frame = column_frame + base_ref[0]
    for i in range(1, columns // total):
        key_frame = jnp.where(column >= i * total, column_frame + base_ref[i], key_frame)
    begin = row_frame + base_ref[0]
    for f in range(frames):
        begin = jnp.where(row_frame == f, begin - start_ref[f], begin)
    offset = key_frame - begin
    usable = (offset >= 0) & (offset < KEYWIN) & (key_frame >= 0) & (key_frame < queue_len)
    factor = inverse_q * inverse_k * HD ** (-0.5)
    for head in range(local // HD):
        lanes = slice(head * HD, (head + 1) * HD)
        scores = lax.dot_general(
            q_ref[:, lanes], kv_ref[0, :, lanes], (((1,), (1,)), ((), ())), preferred_element_type=jnp.float32
        )
        scores = jnp.where(usable, scores * factor, masked_score)
        lifted = jnp.exp(scores - jnp.max(scores, axis=1, keepdims=True))
        weights = (lifted / jnp.sum(lifted, axis=1, keepdims=True)).astype(jnp.bfloat16)
        out = jnp.dot(weights, kv_ref[1, :, lanes], preferred_element_type=jnp.float32)
        out_ref[:, lanes] = out.astype(jnp.bfloat16)


def attend(q, offsets, peers, position, kv, squares, window_start, bases, sizes, inner):
    rows, local = q.shape
    return call(
        functools.partial(attend_kernel, sizes, peers, inner, tuple(offsets)),
        [position, window_start, bases, q, kv, squares],
        [like((rows, local))],
        4 * rows * kv.shape[1] * local,
        scalars=3,
    )[0]


def partial_rows(att_ref, rows, w_ref):
    pieces = [att_ref[lo:hi, :] for lo, hi in rows]
    att = pieces[0] if len(pieces) == 1 else jnp.concatenate(pieces, axis=0)
    out = jnp.dot(att, w_ref[...], preferred_element_type=jnp.float32)
    return out.astype(jnp.bfloat16)


def first_sends_kernel(att_ref, w_ref, *outs):
    out = partial_rows(att_ref, [(0, att_ref.shape[0])], w_ref)
    size = outs[0].shape[0]
    for i, ref in enumerate(outs):
        ref[...] = out[i * size : (i + 1) * size]


def first_sends(att, w_out):
    quarter = like((att.shape[0] // 4, w_out.shape[1]))
    return call(first_sends_kernel, [att, w_out], [quarter] * 4, 2 * att.shape[0] * w_out.size)


def next_sends_kernel(half, rows, places, att_ref, w_ref, right_in, left_in, right_out, left_out):
    low = half * (rows // 2)
    spans = [(rows + low, rows + low + rows // 2), (low, low + rows // 2)]
    out = partial_rows(att_ref, spans, w_ref).astype(jnp.float32)
    for i, (arrived, ref) in enumerate(((right_in, right_out), (left_in, left_out))):
        own = out[i * (rows // 2) : (i + 1) * (rows // 2)]
        lo, hi = places[i]
        total = (own[lo:hi] + arrived[...].astype(jnp.float32)).astype(jnp.bfloat16)
        own = own.astype(jnp.bfloat16)
        parts = [x for x in (own[:lo], total, own[hi:]) if x.shape[0]]
        ref[...] = parts[0] if len(parts) == 1 else jnp.concatenate(parts, axis=0)


def next_sends(half, rows, places, att, w_out, right_in, left_in):
    out = like((rows // 2, w_out.shape[1]))
    return call(
        functools.partial(next_sends_kernel, half, rows, places),
        [att, w_out, right_in, left_in],
        [out, out],
        2 * rows * w_out.size,
    )


def finish_kernel(half, places, x_ref, gate_ref, att_ref, w_ref, right_in, left_in, out_ref):
    frames, tokens, width = out_ref.shape
    rows = frames * tokens
    own = partial_rows(att_ref, [(half * rows, half * rows + rows)], w_ref).astype(jnp.float32)
    for arrived, (lo, hi) in ((right_in, places[0]), (left_in, places[1])):
        added = own[lo:hi] + arrived[...].astype(jnp.float32)
        parts = [x for x in (own[:lo], added, own[hi:]) if x.shape[0]]
        own = parts[0] if len(parts) == 1 else jnp.concatenate(parts, axis=0)
    first = half * frames
    x = x_ref[first : first + frames].astype(jnp.float32)
    gate = gate_ref[first : first + frames, :][:, None, :]
    out_ref[...] = (x + gate * own.reshape(frames, tokens, width)).astype(jnp.bfloat16)


def finish(half, places, x, gate_rows, att, w_out, right_in, left_in):
    frames, tokens, width = x.shape
    return call(
        functools.partial(finish_kernel, half, places),
        [x, gate_rows, att, w_out, right_in, left_in],
        [like((frames // 2, tokens, width))],
        frames * tokens * w_out.size,
    )[0]


def shards(
    ring,
    queue_frames,
    fresh_frames,
    slot_level,
    window_start,
    shift_table,
    scale_table,
    gate_table,
    w_query,
    w_key,
    w_value,
    w_out,
    query_gain,
    key_gain,
):
    peers = lax.axis_size("seq")
    sections = lax.axis_size("segment")
    section = lax.axis_index("segment")
    frames, tokens, width = queue_frames.shape
    rows = frames * tokens
    half_frames = frames // 2
    queue_len = frames * sections
    local = w_query.shape[1]
    inner = local * peers
    far = peers // 2

    def right(x):
        return lax.ppermute(x, "seq", [(ring[i], ring[(i + 1) % peers]) for i in range(peers)])

    def left(x):
        return lax.ppermute(x, "seq", [(ring[(i + 1) % peers], ring[i]) for i in range(peers)])

    def from_sections(x):
        if sections == 2:
            return [lax.ppermute(x, "segment", [(0, 1), (1, 0)])]
        up = [(i, i + 1) for i in range(sections - 1)]
        return [lax.ppermute(x, "segment", route) for route in (up, [(j, i) for i, j in up])]

    if sections == 2:
        bases = jnp.stack([section, 1 - section])
    else:
        bases = jnp.stack([section, section - 1, section + 1])
    bases = bases.astype(jnp.int32) * frames

    place_in_ring = [ring.index(i) for i in range(peers)]
    position = jnp.asarray(place_in_ring, jnp.int32)[lax.axis_index("seq")][None]
    shift_rows, scale_rows, gate_rows = slot_rows(slot_level, [shift_table, scale_table, gate_table])
    weights = (w_query, w_key, w_value)
    gains = (query_gain[None], key_gain[None])

    def projected(blocks, first_frames, offsets):
        return project(blocks, first_frames, offsets, peers, position, scale_rows, shift_rows, weights, gains)

    from_left = from_right = queue_frames
    groups, offsets = [], [[0]]
    done = ([queue_frames], [0])
    for step in range(1, far + 1):
        if step < far:
            from_left, from_right = right(from_left), left(from_right)
            groups.append(projected(*done, offsets[-1]))
            done = ([from_left, from_right], [0, 0])
            offsets.append([peers - step, step])
        else:
            last = [right(from_left[:half_frames]), left(from_right[half_frames:])]
            groups.append(projected(*done, offsets[-1]))
            done = (last, [0, half_frames])
            offsets.append([far])
    groups.append(projected(*done, offsets[-1]))

    others = [from_sections(kv) for _, kv, _ in groups]
    squares = functools.reduce(jnp.add, [sq for _, _, sq in groups])
    squares = jnp.concatenate([squares] + from_sections(squares[1:2]), axis=0)
    distance = 1
    while distance < peers:
        pairs = [(i, i ^ distance) for i in range(peers)]
        squares = squares + lax.ppermute(squares, "seq", pairs)
        distance *= 2
    sets = [[kv for _, kv, _ in groups]] + [[other[i] for other in others] for i in range(len(others[0]))]
    kv = gather(sets, offsets, peers, rows, position)
    sizes = (frames, tokens, queue_len)

    def attended(i):
        return attend(groups[i][0], offsets[i], peers, position, kv, squares, window_start, bases, sizes, inner)

    quarter = rows // 4
    sends = first_sends(attended(far), w_out)
    carried = [(right(sends[0]), left(sends[1])), (right(sends[2]), left(sends[3]))]
    places = ((0, quarter), (quarter, 2 * quarter))
    for step in range(far - 1, 0, -1):
        att = attended(step)
        for half in range(2):
            out = next_sends(half, rows, places, att, w_out, *carried[half])
            carried[half] = (right(out[0]), left(out[1]))
        places = ((0, 2 * quarter), (0, 2 * quarter))
    att = attended(0)
    near = finish(0, places, queue_frames, gate_rows, att, w_out, *carried[0])
    handed = lax.ppermute(near[0], "segment", [(i, i - 1) for i in range(1, sections)])
    later = finish(1, places, queue_frames, gate_rows, att, w_out, *carried[1])
    arriving = jnp.where(section == sections - 1, fresh_frames[0], handed)
    queue_state = jnp.concatenate([near[1:], later, arriving[None]], axis=0)
    return (queue_state, near[0][None, None])


def ring_order(mesh):
    axes = list(mesh.axis_names)
    index = [0] * len(axes)
    index[axes.index("seq")] = slice(None)
    places = [tuple(d.coords) for d in mesh.devices[tuple(index)]]
    spread = [d for d in range(3) if len({p[d] for p in places}) > 1]
    at = {tuple(p[d] for d in spread): i for i, p in enumerate(places)}
    if len(spread) == 1:
        return [at[key] for key in sorted(at)]
    if len(spread) == 2:
        spans = [sorted({key[i] for key in at}) for i in range(2)]
        long = 0 if len(spans[0]) % 2 == 0 else 1
        if len(spans[long]) % 2 == 0 and len(at) == len(spans[0]) * len(spans[1]):
            outward, across = spans[long], spans[1 - long]
            path = []
            for i, a in enumerate(outward):
                turn = across[1:] if i % 2 == 0 else across[:0:-1]
                path += [(a, b) for b in turn]
            path += [(a, across[0]) for a in reversed(outward)]
            return [at[key if long == 0 else key[::-1]] for key in path]
    return list(range(len(places)))


def solution(mesh):
    return jax.shard_map(
        functools.partial(shards, ring_order(mesh)),
        mesh=mesh,
        in_specs=(
            P(("groups", "segment"), "seq", None),
            P("groups", "seq", None),
            P(("groups", "segment")),
            P(("groups", "segment")),
            P(),
            P(),
            P(),
            P(None, "seq"),
            P(None, "seq"),
            P(None, "seq"),
            P("seq", None),
            P("seq"),
            P("seq"),
        ),
        out_specs=(
            P(("groups", "segment"), "seq", None),
            P(("groups", "segment"), None, "seq", None),
        ),
        check_vma=False,
    )
```

time: 201 us -> 142 us (0.71)
  waiting for transfers between devices: 128 us -> 25.2 us
  Pallas kernels: 0 us -> 44.9 us
  starting transfers between devices: 3.97 us -> 33.4 us
  local copies, waits for them, and re-layouts: 7.4 us -> 34.5 us
  matrix products: 21.3 us -> 0 us
  blocking collectives: 19.3 us -> 0 us
  between operations: 14.3 us -> 1.02 us
  other arithmetic: 6.01 us -> 1.11 us
    reduce_scatter x1 -> x0, waiting for transfers between devices: 67.9 us -> none  [shards(): lax.psum_scatter(partial_value.astype(jnp.float32).astype(jnp.bfloat16),...]
    all_gather x1 -> x0, waiting for transfers between devices: 56.6 us -> none  [shards(): lax.all_gather(hidden, 'seq', axis=1, tiled=True)]
    pallas_call x0 -> x21, Pallas kernels: none -> 44.9 us  [call(): pl.pallas_call(kernel, in_specs=[SCALARS] * scalars + [WHOLE] * (len(ins)...]
    unnamed x18 -> x52, local copies, waits for them, and re-layouts: 2.25 us -> 32.4 us
    ppermute x3 -> x34, starting transfers between devices: 3.89 us -> 33.4 us  [the longest x12 20.9 us: right(): lax.ppermute(x, 'seq', [(ring[i], ring[(i + 1) % peers]) for i in range(p...]
    ppermute x3 -> x34, waiting for transfers between devices: 3.52 us -> 25.2 us  [the longest x12 14.7 us: right(): lax.ppermute(x, 'seq', [(ring[i], ring[(i + 1) % peers]) for i in range(p...]
    dot_general x7 -> x0, matrix products: 21.3 us -> none  [the longest x1 8.56 us: shards(): jnp.einsum('ftd,de->fte', lax.all_gather(hidden, 'seq', axis=1, tiled=Tru...]
    psum x1 -> x0, blocking collectives: 19.3 us -> none  [shards(): lax.psum((jnp.sum(q_raw * q_raw, axis=2), jnp.sum(k_raw * k_raw, axis=2))...]
  transfers between devices with their start and end apart: 5 -> 34, of which waited for: 4 -> 9; matrix products, arithmetic and copies ran while one was open for 1% -> 2% of each run, Pallas kernels for 0% -> 25%
where the time goes in v1:
time: 142 us; the launch traced here: 140 us
  Pallas kernels  44.9 us (32%)
  local copies, waits for them, and re-layouts  34.5 us (24%)
  starting transfers between devices  33.4 us (24%)
  waiting for transfers between devices  25.2 us (18%)
    pallas_call x21, Pallas kernels, call(): pl.pallas_call(kernel, in_specs=[SCALARS] * scalars + [WHOLE] * (len(ins)...  44.9 us
    unnamed x52, local copies, waits for them, and re-layouts  32.4 us
    ppermute x12, starting transfers between devices, right(): lax.ppermute(x, 'seq', [(ring[i], ring[(i + 1) % peers]) for i in range(p...  20.9 us
    ppermute x12, waiting for transfers between devices, right(): lax.ppermute(x, 'seq', [(ring[i], ring[(i + 1) % peers]) for i in range(p...  14.7 us
    ppermute x3, waiting for transfers between devices, shards(): squares = squares + lax.ppermute(squares, 'seq', pairs)  5.72 us
    ppermute x3, starting transfers between devices, shards(): squares = squares + lax.ppermute(squares, 'seq', pairs)  5.55 us
    ppermute x12, starting transfers between devices, left(): lax.ppermute(x, 'seq', [(ring[(i + 1) % peers], ring[i]) for i in range(p...  5.14 us
  transfers between devices with their start and end apart: 34, of which 9 were waited for; matrix products, arithmetic and copies ran while one was open for 2% of the time, Pallas kernels for 25%

profile of v1, /device:TPU:0, one launch (start us, length us, event | category | flops | bytes accessed | tf_op | source)
XLA Modules:
  0.0 140.2 jit_solution(11756858627366943193)
XLA Ops:
  0.6 3.1 %collective-permute-start = (bf16[8,4,5120]{2,1,0:T(4,128)(2,1)}, bf16[8,4,5120]{2,1,0:T(4,128)(2,1)S(1)}, u32[]{:S(2)}, u32[]{:S(2)}) collective-permute-start(bf16[8,4,5120]{2,1,0:T(4,128)(2,1)} %x_ref.3), channel_id=1, source_target_pairs={{4,8},{8,12},{12,14},{14,10},{10,6},{6,2},{2,0},{0,4},{5,9},{9,13}... | collective-permute-start | bytes 983048 | tf_op jit(solution)/shard_map/ppermute | solution.py:279
  3.7 7.9 %collective-permute-done.refs_0_ = bf16[8,4,5120]{2,1,0:T(4,128)(2,1)S(1)} collective-permute-done((bf16[8,4,5120]{2,1,0:T(4,128)(2,1)}, bf16[8,4,5120]{2,1,0:T(4,128)(2,1)S(1)}, u32[]{:S(2)}, u32[]{:S(2)}) %collective-permute-start) | collective-permute-done | bytes 327712 | tf_op jit(solution)/shard_map/ppermute | solution.py:279
  11.6 1.8 %collective-permute-start.2 = (bf16[8,4,5120]{2,1,0:T(4,128)(2,1)S(1)}, bf16[8,4,5120]{2,1,0:T(4,128)(2,1)S(1)}, u32[]{:S(2)}, u32[]{:S(2)}) collective-permute-start(bf16[8,4,5120]{2,1,0:T(4,128)(2,1)S(1)} %collective-permute-done.refs_0_), channel_id=1, source_target_pairs={{4,8},{8,12},{12,14},{14,10},{10,6},{6,2},{2,0},{0,4},{5,9},{9,13}... | collective-permute-start | bytes 983048 | tf_op jit(solution)/shard_map/ppermute | solution.py:279
  13.6 6.8 %collective-permute-done.2.refs_0_ = bf16[8,4,5120]{2,1,0:T(4,128)(2,1)S(1)} collective-permute-done((bf16[8,4,5120]{2,1,0:T(4,128)(2,1)S(1)}, bf16[8,4,5120]{2,1,0:T(4,128)(2,1)S(1)}, u32[]{:S(2)}, u32[]{:S(2)}) %collective-permute-start.2) | collective-permute-done | bytes 327712 | tf_op jit(solution)/shard_map/ppermute | solution.py:279
  20.5 1.5 %collective-permute-start.4 = (bf16[8,4,5120]{2,1,0:T(4,128)(2,1)S(1)}, bf16[8,4,5120]{2,1,0:T(4,128)(2,1)S(1)}, u32[]{:S(2)}, u32[]{:S(2)}) collective-permute-start(bf16[8,4,5120]{2,1,0:T(4,128)(2,1)S(1)} %collective-permute-done.2.refs_0_), channel_id=1, source_target_pairs={{4,8},{8,12},{12,14},{14,10},{10,6},{6,2},{2,0},{0,4},{5,9},{9,13}... | collective-permute-start | bytes 983048 | tf_op jit(solution)/shard_map/ppermute | solution.py:279
  22.5 1.3 copy-done.14
  23.8 1.3 copy-done.15
  25.0 1.3 copy-done.16
  27.6 1.2 dynamic_slice.3.position_ref
  28.9 2.5 %copy-done.7 = bf16[5120,512]{1,0:T(8,128)(2,1)S(1)} copy-done((bf16[5120,512]{1,0:T(8,128)(2,1)S(1)}, bf16[5120,512]{1,0:T(8,128)(2,1)}, u32[]{:S(2)}) %copy-start.7) | copy-done | bytes 5242904
  31.4 2.5 %copy-done.8 = bf16[5120,512]{1,0:T(8,128)(2,1)S(1)} copy-done((bf16[5120,512]{1,0:T(8,128)(2,1)S(1)}, bf16[5120,512]{1,0:T(8,128)(2,1)}, u32[]{:S(2)}) %copy-start.8) | copy-done | bytes 5242904
  33.9 2.5 %copy-done.10 = bf16[5120,512]{1,0:T(8,128)(2,1)S(1)} copy-done((bf16[5120,512]{1,0:T(8,128)(2,1)S(1)}, bf16[5120,512]{1,0:T(8,128)(2,1)}, u32[]{:S(2)}) %copy-start.10) | copy-done | bytes 5242904
  38.7 4.5 %shard_map.150 = (bf16[32,512]{1,0:T(8,128)(2,1)S(1)}, bf16[2,32,512]{2,1,0:T(8,128)(2,1)}, f32[2,256]{1,0:T(2,128)S(1)}) custom-call(s32[1]{0:T(128)} %dynamic_slice.3.position_ref, bf16[8,4,5120]{2,1,0:T(4,128)(2,1)S(1)} %copy-done.12, f32[8,5120]{1,0:T(8,128)S(1)} %get-tuple-element.37.refs_1_.refs_2_, f32[8,5120]{1,0:T(8,128)S(1)} %get-tuple-element.38.refs_2_.refs_3_, ...), custom_call_target="tpu_custom_call" | custom-call | flops 503316480 | bytes 16488452 | tf_op jit(solution)/shard_map/pallas_call | solution.py:23
  44.0 4.5 %shard_map.151 = (bf16[64,512]{1,0:T(8,128)(2,1)S(1)}, bf16[2,64,512]{2,1,0:T(8,128)(2,1)}, f32[2,256]{1,0:T(2,128)S(1)}) custom-call(s32[1]{0:T(128)} %dynamic_slice.3.position_ref, bf16[8,4,5120]{2,1,0:T(4,128)(2,1)S(1)} %collective-permute-done.refs_0_, bf16[8,4,5120]{2,1,0:T(4,128)(2,1)S(1)} %collective-permute-done.1.refs_1_, ...), custom_call_target="tpu_custom_call" | custom-call | flops 1006632960 | bytes 16914436 | tf_op jit(solution)/shard_map/pallas_call | solution.py:23
  48.6 1.6 %collective-permute-start.6 = (bf16[4,4,5120]{2,1,0:T(4,128)(2,1)S(1)}, bf16[4,4,5120]{2,1,0:T(4,128)(2,1)S(1)}, u32[]{:S(2)}, u32[]{:S(2)}) collective-permute-start(bf16[4,4,5120]{2,1,0:T(4,128)(2,1)S(1)} %slice.21), channel_id=1, source_target_pairs={{4,8},{8,12},{12,14},{14,10},{10,6},{6,2},{2,0},{0,4},{5,9},{9,13}... | collective-permute-start | bytes 491528 | tf_op jit(solution)/shard_map/ppermute | solution.py:279
  51.0 3.9 %shard_map.152 = (bf16[64,512]{1,0:T(8,128)(2,1)S(1)}, bf16[2,64,512]{2,1,0:T(8,128)(2,1)S(1)}, f32[2,256]{1,0:T(2,128)S(1)}) custom-call(s32[1]{0:T(128)} %dynamic_slice.3.position_ref, bf16[8,4,5120]{2,1,0:T(4,128)(2,1)S(1)} %collective-permute-done.2.refs_0_, bf16[8,4,5120]{2,1,0:T(4,128)(2,1)S(1)} %collective-permute-done.3.refs_1_, ...), custom_call_target="tpu_custom_call" | custom-call | flops 1006632960 | bytes 16914436 | tf_op jit(solution)/shard_map/pallas_call | solution.py:23
  54.8 3.9 %shard_map.153 = (bf16[64,512]{1,0:T(8,128)(2,1)S(1)}, bf16[2,64,512]{2,1,0:T(8,128)(2,1)S(1)}, f32[2,256]{1,0:T(2,128)S(1)}) custom-call(s32[1]{0:T(128)} %dynamic_slice.3.position_ref, bf16[8,4,5120]{2,1,0:T(4,128)(2,1)S(1)} %collective-permute-done.4.refs_0_, bf16[8,4,5120]{2,1,0:T(4,128)(2,1)S(1)} %collective-permute-done.5.refs_1_, ...), custom_call_target="tpu_custom_call" | custom-call | flops 1006632960 | bytes 16914436 | tf_op jit(solution)/shard_map/pallas_call | solution.py:23
  58.8 3.7 %shard_map.154 = (bf16[32,512]{1,0:T(8,128)(2,1)S(1)}, bf16[2,32,512]{2,1,0:T(8,128)(2,1)S(1)}, f32[2,256]{1,0:T(2,128)S(1)}) custom-call(s32[1]{0:T(128)} %dynamic_slice.3.position_ref, bf16[4,4,5120]{2,1,0:T(4,128)(2,1)S(1)} %collective-permute-done.6.refs_0_, bf16[4,4,5120]{2,1,0:T(4,128)(2,1)S(1)} %collective-permute-done.7.refs_1_, ...), custom_call_target="tpu_custom_call" | custom-call | flops 503316480 | bytes 16488452 | tf_op jit(solution)/shard_map/pallas_call | solution.py:23
  63.7 1.5 %collective-permute-start.14 = (f32[3,256]{1,0:T(4,128)S(1)}, f32[3,256]{1,0:T(4,128)S(1)}, u32[]{:S(2)}, u32[]{:S(2)}) collective-permute-start(f32[3,256]{1,0:T(4,128)S(1)} %pad_maximum_fusion.1), channel_id=1, source_target_pairs={{0,2},{2,0},{4,6},{6,4},{8,10},{10,8},{12,14},{14,12},{1,3},{3,1},... | collective-permute-start | bytes 9224 | tf_op jit(solution)/shard_map/ppermute | solution.py:327
  65.7 1.6 %collective-permute-done.14 = f32[3,256]{1,0:T(4,128)S(1)} collective-permute-done((f32[3,256]{1,0:T(4,128)S(1)}, f32[3,256]{1,0:T(4,128)S(1)}, u32[]{:S(2)}, u32[]{:S(2)}) %collective-permute-start.14) | collective-permute-done | bytes 3104 | tf_op jit(solution)/shard_map/ppermute | solution.py:327
  67.3 1.6 %collective-permute-start.15 = (f32[3,256]{1,0:T(4,128)S(1)}, f32[3,256]{1,0:T(4,128)S(1)}, u32[]{:S(2)}, u32[]{:S(2)}) collective-permute-start(f32[3,256]{1,0:T(4,128)S(1)} %fusion.1), channel_id=1, source_target_pairs={{0,4},{2,6},{4,0},{6,2},{8,12},{10,14},{12,8},{14,10},{1,5},{3,7},... | collective-permute-start | bytes 9224 | tf_op jit(solution)/shard_map/ppermute | solution.py:327
  68.9 2.1 %collective-permute-done.15 = f32[3,256]{1,0:T(4,128)S(1)} collective-permute-done((f32[3,256]{1,0:T(4,128)S(1)}, f32[3,256]{1,0:T(4,128)S(1)}, u32[]{:S(2)}, u32[]{:S(2)}) %collective-permute-start.15) | collective-permute-done | bytes 3104 | tf_op jit(solution)/shard_map/ppermute | solution.py:327
  71.0 2.5 %collective-permute-start.16 = (f32[3,256]{1,0:T(4,128)S(1)}, f32[3,256]{1,0:T(4,128)S(1)}, u32[]{:S(2)}, u32[]{:S(2)}) collective-permute-start(f32[3,256]{1,0:T(4,128)S(1)} %add.30), channel_id=1, source_target_pairs={{0,8},{2,10},{4,12},{6,14},{8,0},{10,2},{12,4},{14,6},{1,9},{3,11}... | collective-permute-start | bytes 9224 | tf_op jit(solution)/shard_map/ppermute | solution.py:327
  73.5 2.0 %collective-permute-done.16 = f32[3,256]{1,0:T(4,128)S(1)} collective-permute-done((f32[3,256]{1,0:T(4,128)S(1)}, f32[3,256]{1,0:T(4,128)S(1)}, u32[]{:S(2)}, u32[]{:S(2)}) %collective-permute-start.16) | collective-permute-done | bytes 3104 | tf_op jit(solution)/shard_map/ppermute | solution.py:327
  76.7 1.7 %shard_map.155.kv_ref = bf16[2,512,512]{2,1,0:T(8,128)(2,1)S(1)} custom-call(s32[1]{0:T(128)} %dynamic_slice.3.position_ref, bf16[2,32,512]{2,1,0:T(8,128)(2,1)} %get-tuple-element.40.refs_0_, bf16[2,64,512]{2,1,0:T(8,128)(2,1)} %get-tuple-element.41.refs_1_, bf16[2,64,512]{2,1,0:T(8,128)(2,1)S(1)} %get-tuple-element.42.refs_2_, ...), custom_call_target="tpu_custom_call" | custom-call | flops 1000 | bytes 2097156 | tf_op jit(solution)/shard_map/pallas_call | solution.py:23
  78.4 2.6 %shard_map.160.att_ref = bf16[32,512]{1,0:T(8,128)(2,1)S(1)} custom-call(s32[1]{0:T(128)} %dynamic_slice.3.position_ref, s32[8]{0:T(128)S(1)} %copy-done.21, s32[2]{0:T(128)S(1)} %add_multiply_fusion.base_ref, bf16[32,512]{1,0:T(8,128)(2,1)S(1)} %get-tuple-element.53.q_ref, bf16[2,512,512]{2,1,0:T(8,128)(2,1)S(1)} %shard_map.155.kv_ref, f32[3,256]{1,0:T(4,128)S(1)} %add.31.sq_ref), custom_call_target="tpu_custom_call" | custom-call | flops 33554432 | bytes 1117228 | tf_op jit(solution)/shard_map/pallas_call | solution.py:23
  81.1 2.5 %copy-done = bf16[512,5120]{1,0:T(8,128)(2,1)S(1)} copy-done((bf16[512,5120]{1,0:T(8,128)(2,1)S(1)}, bf16[512,5120]{1,0:T(8,128)(2,1)}, u32[]{:S(2)}) %copy-start) | copy-done | bytes 5242904
  84.5 1.5 %collective-permute-start.17 = (bf16[8,5120]{1,0:T(8,128)(2,1)S(1)}, bf16[8,5120]{1,0:T(8,128)(2,1)S(1)}, u32[]{:S(2)}, u32[]{:S(2)}) collective-permute-start(bf16[8,5120]{1,0:T(8,128)(2,1)S(1)} %get-tuple-element.54), channel_id=1, source_target_pairs={{4,8},{8,12},{12,14},{14,10},{10,6},{6,2},{2,0},{0,4},{5,9},{9,13}... | collective-permute-start | bytes 245768 | tf_op jit(solution)/shard_map/ppermute | solution.py:279
  86.6 2.7 %shard_map.159.att_ref = bf16[64,512]{1,0:T(8,128)(2,1)S(1)} custom-call(s32[1]{0:T(128)} %dynamic_slice.3.position_ref, s32[8]{0:T(128)S(1)} %copy-done.21, s32[2]{0:T(128)S(1)} %add_multiply_fusion.base_ref, bf16[64,512]{1,0:T(8,128)(2,1)S(1)} %get-tuple-element.52.q_ref, bf16[2,512,512]{2,1,0:T(8,128)(2,1)S(1)} %shard_map.155.kv_ref, f32[3,256]{1,0:T(4,128)S(1)} %add.31.sq_ref), custom_call_target="tpu_custom_call" | custom-call | flops 67108864 | bytes 1182764 | tf_op jit(solution)/shard_map/pallas_call | solution.py:23
  89.3 1.2 collective-permute-done.18.left_in
  90.5 2.5 %copy-done.1 = bf16[512,5120]{1,0:T(8,128)(2,1)S(1)} copy-done((bf16[512,5120]{1,0:T(8,128)(2,1)S(1)}, bf16[512,5120]{1,0:T(8,128)(2,1)}, u32[]{:S(2)}) %copy-start.1) | copy-done | bytes 5242904
  94.0 1.6 %collective-permute-start.19 = (bf16[16,5120]{1,0:T(8,128)(2,1)S(1)}, bf16[16,5120]{1,0:T(8,128)(2,1)S(1)}, u32[]{:S(2)}, u32[]{:S(2)}) collective-permute-start(bf16[16,5120]{1,0:T(8,128)(2,1)S(1)} %get-tuple-element.56), channel_id=1, source_target_pairs={{4,8},{8,12},{12,14},{14,10},{10,6},{6,2},{2,0},{0,4},{5,9},{9,13}... | collective-permute-start | bytes 491528 | tf_op jit(solution)/shard_map/ppermute | solution.py:279
  96.1 1.6 %collective-permute-start.25 = (bf16[8,5120]{1,0:T(8,128)(2,1)S(1)}, bf16[8,5120]{1,0:T(8,128)(2,1)S(1)}, u32[]{:S(2)}, u32[]{:S(2)}) collective-permute-start(bf16[8,5120]{1,0:T(8,128)(2,1)S(1)} %get-tuple-element.62), channel_id=1, source_target_pairs={{4,8},{8,12},{12,14},{14,10},{10,6},{6,2},{2,0},{0,4},{5,9},{9,13}... | collective-permute-start | bytes 245768 | tf_op jit(solution)/shard_map/ppermute | solution.py:279
  98.1 2.7 %shard_map.158.att_ref = bf16[64,512]{1,0:T(8,128)(2,1)S(1)} custom-call(s32[1]{0:T(128)} %dynamic_slice.3.position_ref, s32[8]{0:T(128)S(1)} %copy-done.21, s32[2]{0:T(128)S(1)} %add_multiply_fusion.base_ref, bf16[64,512]{1,0:T(8,128)(2,1)S(1)} %get-tuple-element.51.q_ref, bf16[2,512,512]{2,1,0:T(8,128)(2,1)S(1)} %shard_map.155.kv_ref, f32[3,256]{1,0:T(4,128)S(1)} %add.31.sq_ref), custom_call_target="tpu_custom_call" | custom-call | flops 67108864 | bytes 1182764 | tf_op jit(solution)/shard_map/pallas_call | solution.py:23
  100.9 1.3 collective-permute-done.26.left_in
  102.1 2.5 %copy-done.2 = bf16[512,5120]{1,0:T(8,128)(2,1)S(1)} copy-done((bf16[512,5120]{1,0:T(8,128)(2,1)S(1)}, bf16[512,5120]{1,0:T(8,128)(2,1)}, u32[]{:S(2)}) %copy-start.2) | copy-done | bytes 5242904
  105.6 1.6 %collective-permute-start.27 = (bf16[16,5120]{1,0:T(8,128)(2,1)S(1)}, bf16[16,5120]{1,0:T(8,128)(2,1)S(1)}, u32[]{:S(2)}, u32[]{:S(2)}) collective-permute-start(bf16[16,5120]{1,0:T(8,128)(2,1)S(1)} %get-tuple-element.64), channel_id=1, source_target_pairs={{4,8},{8,12},{12,14},{14,10},{10,6},{6,2},{2,0},{0,4},{5,9},{9,13}... | collective-permute-start | bytes 491528 | tf_op jit(solution)/shard_map/ppermute | solution.py:279
  108.7 1.6 %collective-permute-start.21 = (bf16[16,5120]{1,0:T(8,128)(2,1)S(1)}, bf16[16,5120]{1,0:T(8,128)(2,1)S(1)}, u32[]{:S(2)}, u32[]{:S(2)}) collective-permute-start(bf16[16,5120]{1,0:T(8,128)(2,1)S(1)} %get-tuple-element.58), channel_id=1, source_target_pairs={{4,8},{8,12},{12,14},{14,10},{10,6},{6,2},{2,0},{0,4},{5,9},{9,13}... | collective-permute-start | bytes 491528 | tf_op jit(solution)/shard_map/ppermute | solution.py:279
  110.8 2.7 %shard_map.157.att_ref = bf16[64,512]{1,0:T(8,128)(2,1)S(1)} custom-call(s32[1]{0:T(128)} %dynamic_slice.3.position_ref, s32[8]{0:T(128)S(1)} %copy-done.21, s32[2]{0:T(128)S(1)} %add_multiply_fusion.base_ref, bf16[64,512]{1,0:T(8,128)(2,1)S(1)} %copy-done.18, bf16[2,512,512]{2,1,0:T(8,128)(2,1)S(1)} %shard_map.155.kv_ref, f32[3,256]{1,0:T(4,128)S(1)} %add.31.sq_ref), custom_call_target="tpu_custom_call" | custom-call | flops 67108864 | bytes 1182764 | tf_op jit(solution)/shard_map/pallas_call | solution.py:23
  113.5 2.5 %copy-done.3 = bf16[512,5120]{1,0:T(8,128)(2,1)S(1)} copy-done((bf16[512,5120]{1,0:T(8,128)(2,1)S(1)}, bf16[512,5120]{1,0:T(8,128)(2,1)}, u32[]{:S(2)}) %copy-start.3) | copy-done | bytes 5242904
  117.0 1.6 %collective-permute-start.29 = (bf16[16,5120]{1,0:T(8,128)(2,1)S(1)}, bf16[16,5120]{1,0:T(8,128)(2,1)S(1)}, u32[]{:S(2)}, u32[]{:S(2)}) collective-permute-start(bf16[16,5120]{1,0:T(8,128)(2,1)S(1)} %get-tuple-element.66), channel_id=1, source_target_pairs={{4,8},{8,12},{12,14},{14,10},{10,6},{6,2},{2,0},{0,4},{5,9},{9,13}... | collective-permute-start | bytes 491528 | tf_op jit(solution)/shard_map/ppermute | solution.py:279
  120.1 1.6 %collective-permute-start.23 = (bf16[16,5120]{1,0:T(8,128)(2,1)S(1)}, bf16[16,5120]{1,0:T(8,128)(2,1)S(1)}, u32[]{:S(2)}, u32[]{:S(2)}) collective-permute-start(bf16[16,5120]{1,0:T(8,128)(2,1)S(1)} %get-tuple-element.60), channel_id=1, source_target_pairs={{4,8},{8,12},{12,14},{14,10},{10,6},{6,2},{2,0},{0,4},{5,9},{9,13}... | collective-permute-start | bytes 491528 | tf_op jit(solution)/shard_map/ppermute | solution.py:279
  122.2 2.6 %shard_map.156.att_ref = bf16[32,512]{1,0:T(8,128)(2,1)S(1)} custom-call(s32[1]{0:T(128)} %dynamic_slice.3.position_ref, s32[8]{0:T(128)S(1)} %copy-done.21, s32[2]{0:T(128)S(1)} %add_multiply_fusion.base_ref, bf16[32,512]{1,0:T(8,128)(2,1)S(1)} %get-tuple-element.39.q_ref, bf16[2,512,512]{2,1,0:T(8,128)(2,1)S(1)} %shard_map.155.kv_ref, f32[3,256]{1,0:T(4,128)S(1)} %add.31.sq_ref), custom_call_target="tpu_custom_call" | custom-call | flops 33554432 | bytes 1117228 | tf_op jit(solution)/shard_map/pallas_call | solution.py:23
  124.9 2.5 %copy-done.4 = bf16[512,5120]{1,0:T(8,128)(2,1)S(1)} copy-done((bf16[512,5120]{1,0:T(8,128)(2,1)S(1)}, bf16[512,5120]{1,0:T(8,128)(2,1)}, u32[]{:S(2)}) %copy-start.4) | copy-done | bytes 5242904
  128.4 1.6 %collective-permute-start.31 = (bf16[16,5120]{1,0:T(8,128)(2,1)S(1)}, bf16[16,5120]{1,0:T(8,128)(2,1)S(1)}, u32[]{:S(2)}, u32[]{:S(2)}) collective-permute-start(bf16[16,5120]{1,0:T(8,128)(2,1)S(1)} %get-tuple-element.68), channel_id=1, source_target_pairs={{4,8},{8,12},{12,14},{14,10},{10,6},{6,2},{2,0},{0,4},{5,9},{9,13}... | collective-permute-start | bytes 491528 | tf_op jit(solution)/shard_map/ppermute | solution.py:279
  130.5 2.5 %copy-done.5 = bf16[512,5120]{1,0:T(8,128)(2,1)S(1)} copy-done((bf16[512,5120]{1,0:T(8,128)(2,1)S(1)}, bf16[512,5120]{1,0:T(8,128)(2,1)}, u32[]{:S(2)}) %copy-start.5) | copy-done | bytes 5242904
  134.5 1.3 collective-permute-start.33
  135.8 2.5 %copy-done.6 = bf16[512,5120]{1,0:T(8,128)(2,1)S(1)} copy-done((bf16[512,5120]{1,0:T(8,128)(2,1)S(1)}, bf16[512,5120]{1,0:T(8,128)(2,1)}, u32[]{:S(2)}) %copy-start.6) | copy-done | bytes 5242904
  (108 shorter events, 23.3 us)
Async XLA Ops:
  0.6 11.0 %collective-permute-start = (bf16[8,4,5120]{2,1,0:T(4,128)(2,1)}, bf16[8,4,5120]{2,1,0:T(4,128)(2,1)S(1)}, u32[]{:S(2)}, u32[]{:S(2)}) collective-permute-start(bf16[8,4,5120]{2,1,0:T(4,128)(2,1)} %x_ref.3), channel_id=1, source_target_pairs={{4,8},{8,12},{12,14},{14,10},{10,6},{6,2},{2,0},{0,4},{5,9},{9,13}... | collective-permute-start | bytes 983048 | tf_op jit(solution)/shard_map/ppermute | solution.py:279
  3.7 9.7 %collective-permute-start.1 = (bf16[8,4,5120]{2,1,0:T(4,128)(2,1)}, bf16[8,4,5120]{2,1,0:T(4,128)(2,1)S(1)}, u32[]{:S(2)}, u32[]{:S(2)}) collective-permute-start(bf16[8,4,5120]{2,1,0:T(4,128)(2,1)} %x_ref.3), channel_id=1, source_target_pairs={{8,4},{12,8},{14,12},{10,14},{6,10},{2,6},{0,2},{4,0},{9,5},{13,9}... | collective-permute-start | bytes 983048 | tf_op jit(solution)/shard_map/ppermute | solution.py:282
  11.6 8.9 %collective-permute-start.2 = (bf16[8,4,5120]{2,1,0:T(4,128)(2,1)S(1)}, bf16[8,4,5120]{2,1,0:T(4,128)(2,1)S(1)}, u32[]{:S(2)}, u32[]{:S(2)}) collective-permute-start(bf16[8,4,5120]{2,1,0:T(4,128)(2,1)S(1)} %collective-permute-done.refs_0_), channel_id=1, source_target_pairs={{4,8},{8,12},{12,14},{14,10},{10,6},{6,2},{2,0},{0,4},{5,9},{9,13}... | collective-permute-start | bytes 983048 | tf_op jit(solution)/shard_map/ppermute | solution.py:279
  13.4 8.6 %collective-permute-start.3 = (bf16[8,4,5120]{2,1,0:T(4,128)(2,1)S(1)}, bf16[8,4,5120]{2,1,0:T(4,128)(2,1)S(1)}, u32[]{:S(2)}, u32[]{:S(2)}) collective-permute-start(bf16[8,4,5120]{2,1,0:T(4,128)(2,1)S(1)} %collective-permute-done.1.refs_1_), channel_id=1, source_target_pairs={{8,4},{12,8},{14,12},{10,14},{6,10},{2,6},{0,2},{4,0},{9,5},{13,9}... | collective-permute-start | bytes 983048 | tf_op jit(solution)/shard_map/ppermute | solution.py:282
  20.5 28.0 %collective-permute-start.4 = (bf16[8,4,5120]{2,1,0:T(4,128)(2,1)S(1)}, bf16[8,4,5120]{2,1,0:T(4,128)(2,1)S(1)}, u32[]{:S(2)}, u32[]{:S(2)}) collective-permute-start(bf16[8,4,5120]{2,1,0:T(4,128)(2,1)S(1)} %collective-permute-done.2.refs_0_), channel_id=1, source_target_pairs={{4,8},{8,12},{12,14},{14,10},{10,6},{6,2},{2,0},{0,4},{5,9},{9,13}... | collective-permute-start | bytes 983048 | tf_op jit(solution)/shard_map/ppermute | solution.py:279
  22.0 28.2 %collective-permute-start.5 = (bf16[8,4,5120]{2,1,0:T(4,128)(2,1)S(1)}, bf16[8,4,5120]{2,1,0:T(4,128)(2,1)S(1)}, u32[]{:S(2)}, u32[]{:S(2)}) collective-permute-start(bf16[8,4,5120]{2,1,0:T(4,128)(2,1)S(1)} %collective-permute-done.3.refs_1_), channel_id=1, source_target_pairs={{8,4},{12,8},{14,12},{10,14},{6,10},{2,6},{0,2},{4,0},{9,5},{13,9}... | collective-permute-start | bytes 983048 | tf_op jit(solution)/shard_map/ppermute | solution.py:282
  26.9 16.2 %slice-start = ((s8[5242880]{0:T(1024)(128)(4,1)}), s8[1048576]{0:T(1024)(128)(4,1)S(1)}, s32[]{:S(2)}) async-start(s8[5242880]{0:T(1024)(128)(4,1)} %bitcast.14), calls=%async_computation | async-start | bytes 2097152
  38.7 4.5 %slice-start.1 = ((s8[5242880]{0:T(1024)(128)(4,1)}), s8[4194304]{0:T(1024)(128)(4,1)S(1)}, s32[]{:S(2)}) async-start(s8[5242880]{0:T(1024)(128)(4,1)} %bitcast.14), calls=%async_computation.1 | async-start | bytes 8388608
  38.7 4.5 %copy-start.9 = (bf16[5120,512]{1,0:T(8,128)(2,1)S(1)}, bf16[5120,512]{1,0:T(8,128)(2,1)}, u32[]{:S(2)}) copy-start(bf16[5120,512]{1,0:T(8,128)(2,1)} %refs_5_.9) | copy-start | bytes 15728644
  38.7 5.3 %copy-start.11 = (bf16[5120,512]{1,0:T(8,128)(2,1)S(1)}, bf16[5120,512]{1,0:T(8,128)(2,1)}, u32[]{:S(2)}) copy-start(bf16[5120,512]{1,0:T(8,128)(2,1)} %refs_6_.7) | copy-start | bytes 15728644
  48.5 6.3 %copy-start.17 = (bf16[64,512]{1,0:T(8,128)(2,1)}, bf16[64,512]{1,0:T(8,128)(2,1)S(1)}, u32[]{:S(2)}) copy-start(bf16[64,512]{1,0:T(8,128)(2,1)S(1)} %get-tuple-element.50.q_ref) | copy-start | bytes 196612
  48.6 10.2 %collective-permute-start.6 = (bf16[4,4,5120]{2,1,0:T(4,128)(2,1)S(1)}, bf16[4,4,5120]{2,1,0:T(4,128)(2,1)S(1)}, u32[]{:S(2)}, u32[]{:S(2)}) collective-permute-start(bf16[4,4,5120]{2,1,0:T(4,128)(2,1)S(1)} %slice.21), channel_id=1, source_target_pairs={{4,8},{8,12},{12,14},{14,10},{10,6},{6,2},{2,0},{0,4},{5,9},{9,13}... | collective-permute-start | bytes 491528 | tf_op jit(solution)/shard_map/ppermute | solution.py:279
  50.2 8.5 %collective-permute-start.7 = (bf16[4,4,5120]{2,1,0:T(4,128)(2,1)S(1)}, bf16[4,4,5120]{2,1,0:T(4,128)(2,1)S(1)}, u32[]{:S(2)}, u32[]{:S(2)}) collective-permute-start(bf16[4,4,5120]{2,1,0:T(4,128)(2,1)S(1)} %slice.22), channel_id=1, source_target_pairs={{8,4},{12,8},{14,12},{10,14},{6,10},{2,6},{0,2},{4,0},{9,5},{13,9}... | collective-permute-start | bytes 491528 | tf_op jit(solution)/shard_map/ppermute | solution.py:282
  58.7 19.7 %copy-start.21 = (s32[8]{0:T(128)S(1)}, s32[8]{0:T(128)}, u32[]{:S(2)}) copy-start(s32[8]{0:T(128)} %start_ref.9) | copy-start | bytes 100
  62.5 1.2 collective-permute-start.13
  63.7 3.6 %collective-permute-start.14 = (f32[3,256]{1,0:T(4,128)S(1)}, f32[3,256]{1,0:T(4,128)S(1)}, u32[]{:S(2)}, u32[]{:S(2)}) collective-permute-start(f32[3,256]{1,0:T(4,128)S(1)} %pad_maximum_fusion.1), channel_id=1, source_target_pairs={{0,2},{2,0},{4,6},{6,4},{8,10},{10,8},{12,14},{14,12},{1,3},{3,1},... | collective-permute-start | bytes 9224 | tf_op jit(solution)/shard_map/ppermute | solution.py:327
  65.1 10.4 %collective-permute-start.9 = (bf16[2,64,512]{2,1,0:T(8,128)(2,1)}, bf16[2,64,512]{2,1,0:T(8,128)(2,1)S(1)}, u32[]{:S(2)}, u32[]{:S(2)}) collective-permute-start(bf16[2,64,512]{2,1,0:T(8,128)(2,1)} %get-tuple-element.41.refs_1_), channel_id=1, source_target_pairs={{0,1},{1,0},{2,3},{3,2},{4,5},{5,4},{6,7},{7,6},{8,9},{9,8},{10,11... | collective-permute-start | bytes 393224 | tf_op jit(solution)/shard_map/ppermute | solution.py:286
  65.1 10.4 %collective-permute-start.10 = (bf16[2,64,512]{2,1,0:T(8,128)(2,1)S(1)}, bf16[2,64,512]{2,1,0:T(8,128)(2,1)S(1)}, u32[]{:S(2)}, u32[]{:S(2)}) collective-permute-start(bf16[2,64,512]{2,1,0:T(8,128)(2,1)S(1)} %get-tuple-element.42.refs_2_), channel_id=1, source_target_pairs={{0,1},{1,0},{2,3},{3,2},{4,5},{5,4},{6,7},{7,6},{8,9},{9,8},{10,11... | collective-permute-start | bytes 393224 | tf_op jit(solution)/shard_map/ppermute | solution.py:286
  65.6 9.9 %collective-permute-start.11 = (bf16[2,64,512]{2,1,0:T(8,128)(2,1)S(1)}, bf16[2,64,512]{2,1,0:T(8,128)(2,1)S(1)}, u32[]{:S(2)}, u32[]{:S(2)}) collective-permute-start(bf16[2,64,512]{2,1,0:T(8,128)(2,1)S(1)} %get-tuple-element.43.refs_3_), channel_id=1, source_target_pairs={{0,1},{1,0},{2,3},{3,2},{4,5},{5,4},{6,7},{7,6},{8,9},{9,8},{10,11... | collective-permute-start | bytes 393224 | tf_op jit(solution)/shard_map/ppermute | solution.py:286
  67.3 3.7 %collective-permute-start.15 = (f32[3,256]{1,0:T(4,128)S(1)}, f32[3,256]{1,0:T(4,128)S(1)}, u32[]{:S(2)}, u32[]{:S(2)}) collective-permute-start(f32[3,256]{1,0:T(4,128)S(1)} %fusion.1), channel_id=1, source_target_pairs={{0,4},{2,6},{4,0},{6,2},{8,12},{10,14},{12,8},{14,10},{1,5},{3,7},... | collective-permute-start | bytes 9224 | tf_op jit(solution)/shard_map/ppermute | solution.py:327
  71.0 4.5 %collective-permute-start.16 = (f32[3,256]{1,0:T(4,128)S(1)}, f32[3,256]{1,0:T(4,128)S(1)}, u32[]{:S(2)}, u32[]{:S(2)}) collective-permute-start(f32[3,256]{1,0:T(4,128)S(1)} %add.30), channel_id=1, source_target_pairs={{0,8},{2,10},{4,12},{6,14},{8,0},{10,2},{12,4},{14,6},{1,9},{3,11}... | collective-permute-start | bytes 9224 | tf_op jit(solution)/shard_map/ppermute | solution.py:327
  73.5 2.1 %collective-permute-start.8 = (bf16[2,32,512]{2,1,0:T(8,128)(2,1)}, bf16[2,32,512]{2,1,0:T(8,128)(2,1)S(1)}, u32[]{:S(2)}, u32[]{:S(2)}) collective-permute-start(bf16[2,32,512]{2,1,0:T(8,128)(2,1)} %get-tuple-element.40.refs_0_), channel_id=1, source_target_pairs={{0,1},{1,0},{2,3},{3,2},{4,5},{5,4},{6,7},{7,6},{8,9},{9,8},{10,11... | collective-permute-start | bytes 196616 | tf_op jit(solution)/shard_map/ppermute | solution.py:286
  75.5 1.3 collective-permute-start.12
  81.1 2.5 %copy-start = (bf16[512,5120]{1,0:T(8,128)(2,1)S(1)}, bf16[512,5120]{1,0:T(8,128)(2,1)}, u32[]{:S(2)}) copy-start(bf16[512,5120]{1,0:T(8,128)(2,1)} %w_ref.17) | copy-start | bytes 15728644
  84.5 4.7 %collective-permute-start.17 = (bf16[8,5120]{1,0:T(8,128)(2,1)S(1)}, bf16[8,5120]{1,0:T(8,128)(2,1)S(1)}, u32[]{:S(2)}, u32[]{:S(2)}) collective-permute-start(bf16[8,5120]{1,0:T(8,128)(2,1)S(1)} %get-tuple-element.54), channel_id=1, source_target_pairs={{4,8},{8,12},{12,14},{14,10},{10,6},{6,2},{2,0},{0,4},{5,9},{9,13}... | collective-permute-start | bytes 245768 | tf_op jit(solution)/shard_map/ppermute | solution.py:279
  86.1 4.4 %collective-permute-start.18 = (bf16[8,5120]{1,0:T(8,128)(2,1)S(1)}, bf16[8,5120]{1,0:T(8,128)(2,1)S(1)}, u32[]{:S(2)}, u32[]{:S(2)}) collective-permute-start(bf16[8,5120]{1,0:T(8,128)(2,1)S(1)} %get-tuple-element.55), channel_id=1, source_target_pairs={{8,4},{12,8},{14,12},{10,14},{6,10},{2,6},{0,2},{4,0},{9,5},{13,9}... | collective-permute-start | bytes 245768 | tf_op jit(solution)/shard_map/ppermute | solution.py:282
  94.0 13.7 %collective-permute-start.19 = (bf16[16,5120]{1,0:T(8,128)(2,1)S(1)}, bf16[16,5120]{1,0:T(8,128)(2,1)S(1)}, u32[]{:S(2)}, u32[]{:S(2)}) collective-permute-start(bf16[16,5120]{1,0:T(8,128)(2,1)S(1)} %get-tuple-element.56), channel_id=1, source_target_pairs={{4,8},{8,12},{12,14},{14,10},{10,6},{6,2},{2,0},{0,4},{5,9},{9,13}... | collective-permute-start | bytes 491528 | tf_op jit(solution)/shard_map/ppermute | solution.py:279
  95.7 12.1 %collective-permute-start.20 = (bf16[16,5120]{1,0:T(8,128)(2,1)S(1)}, bf16[16,5120]{1,0:T(8,128)(2,1)S(1)}, u32[]{:S(2)}, u32[]{:S(2)}) collective-permute-start(bf16[16,5120]{1,0:T(8,128)(2,1)S(1)} %get-tuple-element.57), channel_id=1, source_target_pairs={{8,4},{12,8},{14,12},{10,14},{6,10},{2,6},{0,2},{4,0},{9,5},{13,9}... | collective-permute-start | bytes 491528 | tf_op jit(solution)/shard_map/ppermute | solution.py:282
  96.1 4.8 %collective-permute-start.25 = (bf16[8,5120]{1,0:T(8,128)(2,1)S(1)}, bf16[8,5120]{1,0:T(8,128)(2,1)S(1)}, u32[]{:S(2)}, u32[]{:S(2)}) collective-permute-start(bf16[8,5120]{1,0:T(8,128)(2,1)S(1)} %get-tuple-element.62), channel_id=1, source_target_pairs={{4,8},{8,12},{12,14},{14,10},{10,6},{6,2},{2,0},{0,4},{5,9},{9,13}... | collective-permute-start | bytes 245768 | tf_op jit(solution)/shard_map/ppermute | solution.py:279
  97.7 4.4 %collective-permute-start.26 = (bf16[8,5120]{1,0:T(8,128)(2,1)S(1)}, bf16[8,5120]{1,0:T(8,128)(2,1)S(1)}, u32[]{:S(2)}, u32[]{:S(2)}) collective-permute-start(bf16[8,5120]{1,0:T(8,128)(2,1)S(1)} %get-tuple-element.63), channel_id=1, source_target_pairs={{8,4},{12,8},{14,12},{10,14},{6,10},{2,6},{0,2},{4,0},{9,5},{13,9}... | collective-permute-start | bytes 245768 | tf_op jit(solution)/shard_map/ppermute | solution.py:282
  98.1 12.7 %copy-start.18 = (bf16[64,512]{1,0:T(8,128)(2,1)S(1)}, bf16[64,512]{1,0:T(8,128)(2,1)}, u32[]{:S(2)}) copy-start(bf16[64,512]{1,0:T(8,128)(2,1)} %copy-done.17) | copy-start | bytes 196612
  105.6 7.9 %collective-permute-start.27 = (bf16[16,5120]{1,0:T(8,128)(2,1)S(1)}, bf16[16,5120]{1,0:T(8,128)(2,1)S(1)}, u32[]{:S(2)}, u32[]{:S(2)}) collective-permute-start(bf16[16,5120]{1,0:T(8,128)(2,1)S(1)} %get-tuple-element.64), channel_id=1, source_target_pairs={{4,8},{8,12},{12,14},{14,10},{10,6},{6,2},{2,0},{0,4},{5,9},{9,13}... | collective-permute-start | bytes 491528 | tf_op jit(solution)/shard_map/ppermute | solution.py:279
  107.3 6.3 %collective-permute-start.28 = (bf16[16,5120]{1,0:T(8,128)(2,1)S(1)}, bf16[16,5120]{1,0:T(8,128)(2,1)S(1)}, u32[]{:S(2)}, u32[]{:S(2)}) collective-permute-start(bf16[16,5120]{1,0:T(8,128)(2,1)S(1)} %get-tuple-element.65), channel_id=1, source_target_pairs={{8,4},{12,8},{14,12},{10,14},{6,10},{2,6},{0,2},{4,0},{9,5},{13,9}... | collective-permute-start | bytes 491528 | tf_op jit(solution)/shard_map/ppermute | solution.py:282
  108.7 10.4 %collective-permute-start.21 = (bf16[16,5120]{1,0:T(8,128)(2,1)S(1)}, bf16[16,5120]{1,0:T(8,128)(2,1)S(1)}, u32[]{:S(2)}, u32[]{:S(2)}) collective-permute-start(bf16[16,5120]{1,0:T(8,128)(2,1)S(1)} %get-tuple-element.58), channel_id=1, source_target_pairs={{4,8},{8,12},{12,14},{14,10},{10,6},{6,2},{2,0},{0,4},{5,9},{9,13}... | collective-permute-start | bytes 491528 | tf_op jit(solution)/shard_map/ppermute | solution.py:279
  110.4 8.8 %collective-permute-start.22 = (bf16[16,5120]{1,0:T(8,128)(2,1)S(1)}, bf16[16,5120]{1,0:T(8,128)(2,1)S(1)}, u32[]{:S(2)}, u32[]{:S(2)}) collective-permute-start(bf16[16,5120]{1,0:T(8,128)(2,1)S(1)} %get-tuple-element.59), channel_id=1, source_target_pairs={{8,4},{12,8},{14,12},{10,14},{6,10},{2,6},{0,2},{4,0},{9,5},{13,9}... | collective-permute-start | bytes 491528 | tf_op jit(solution)/shard_map/ppermute | solution.py:282
  113.5 2.5 %copy-start.3 = (bf16[512,5120]{1,0:T(8,128)(2,1)S(1)}, bf16[512,5120]{1,0:T(8,128)(2,1)}, u32[]{:S(2)}) copy-start(bf16[512,5120]{1,0:T(8,128)(2,1)} %w_ref.17) | copy-start | bytes 15728644
  117.0 7.8 %collective-permute-start.29 = (bf16[16,5120]{1,0:T(8,128)(2,1)S(1)}, bf16[16,5120]{1,0:T(8,128)(2,1)S(1)}, u32[]{:S(2)}, u32[]{:S(2)}) collective-permute-start(bf16[16,5120]{1,0:T(8,128)(2,1)S(1)} %get-tuple-element.66), channel_id=1, source_target_pairs={{4,8},{8,12},{12,14},{14,10},{10,6},{6,2},{2,0},{0,4},{5,9},{9,13}... | collective-permute-start | bytes 491528 | tf_op jit(solution)/shard_map/ppermute | solution.py:279
  118.7 11.8 %copy-start.13 = (bf16[8,4,5120]{2,1,0:T(4,128)(2,1)S(1)}, bf16[8,4,5120]{2,1,0:T(4,128)(2,1)}, u32[]{:S(2)}) copy-start(bf16[8,4,5120]{2,1,0:T(4,128)(2,1)} %x_ref.3) | copy-start | bytes 983044
  118.7 6.2 %collective-permute-start.30 = (bf16[16,5120]{1,0:T(8,128)(2,1)S(1)}, bf16[16,5120]{1,0:T(8,128)(2,1)S(1)}, u32[]{:S(2)}, u32[]{:S(2)}) collective-permute-start(bf16[16,5120]{1,0:T(8,128)(2,1)S(1)} %get-tuple-element.67), channel_id=1, source_target_pairs={{8,4},{12,8},{14,12},{10,14},{6,10},{2,6},{0,2},{4,0},{9,5},{13,9}... | collective-permute-start | bytes 491528 | tf_op jit(solution)/shard_map/ppermute | solution.py:282
  120.1 10.3 %collective-permute-start.23 = (bf16[16,5120]{1,0:T(8,128)(2,1)S(1)}, bf16[16,5120]{1,0:T(8,128)(2,1)S(1)}, u32[]{:S(2)}, u32[]{:S(2)}) collective-permute-start(bf16[16,5120]{1,0:T(8,128)(2,1)S(1)} %get-tuple-element.60), channel_id=1, source_target_pairs={{4,8},{8,12},{12,14},{14,10},{10,6},{6,2},{2,0},{0,4},{5,9},{9,13}... | collective-permute-start | bytes 491528 | tf_op jit(solution)/shard_map/ppermute | solution.py:279
  121.8 8.7 %collective-permute-start.24 = (bf16[16,5120]{1,0:T(8,128)(2,1)S(1)}, bf16[16,5120]{1,0:T(8,128)(2,1)S(1)}, u32[]{:S(2)}, u32[]{:S(2)}) collective-permute-start(bf16[16,5120]{1,0:T(8,128)(2,1)S(1)} %get-tuple-element.61), channel_id=1, source_target_pairs={{8,4},{12,8},{14,12},{10,14},{6,10},{2,6},{0,2},{4,0},{9,5},{13,9}... | collective-permute-start | bytes 491528 | tf_op jit(solution)/shard_map/ppermute | solution.py:282
  124.9 2.5 %copy-start.4 = (bf16[512,5120]{1,0:T(8,128)(2,1)S(1)}, bf16[512,5120]{1,0:T(8,128)(2,1)}, u32[]{:S(2)}) copy-start(bf16[512,5120]{1,0:T(8,128)(2,1)} %w_ref.17) | copy-start | bytes 15728644
  128.4 7.4 %collective-permute-start.31 = (bf16[16,5120]{1,0:T(8,128)(2,1)S(1)}, bf16[16,5120]{1,0:T(8,128)(2,1)S(1)}, u32[]{:S(2)}, u32[]{:S(2)}) collective-permute-start(bf16[16,5120]{1,0:T(8,128)(2,1)S(1)} %get-tuple-element.68), channel_id=1, source_target_pairs={{4,8},{8,12},{12,14},{14,10},{10,6},{6,2},{2,0},{0,4},{5,9},{9,13}... | collective-permute-start | bytes 491528 | tf_op jit(solution)/shard_map/ppermute | solution.py:279
  130.0 5.8 %collective-permute-start.32 = (bf16[16,5120]{1,0:T(8,128)(2,1)S(1)}, bf16[16,5120]{1,0:T(8,128)(2,1)S(1)}, u32[]{:S(2)}, u32[]{:S(2)}) collective-permute-start(bf16[16,5120]{1,0:T(8,128)(2,1)S(1)} %get-tuple-element.69), channel_id=1, source_target_pairs={{8,4},{12,8},{14,12},{10,14},{6,10},{2,6},{0,2},{4,0},{9,5},{13,9}... | collective-permute-start | bytes 491528 | tf_op jit(solution)/shard_map/ppermute | solution.py:282
  130.5 2.5 %copy-start.5 = (bf16[512,5120]{1,0:T(8,128)(2,1)S(1)}, bf16[512,5120]{1,0:T(8,128)(2,1)}, u32[]{:S(2)}) copy-start(bf16[512,5120]{1,0:T(8,128)(2,1)} %w_ref.17) | copy-start | bytes 15728644
  133.0 6.2 %copy-start.23 = (bf16[1,4,5120]{2,1,0:T(4,128)(2,1)S(1)}, bf16[1,4,5120]{2,1,0:T(4,128)(2,1)}, u32[]{:S(2)}) copy-start(bf16[1,4,5120]{2,1,0:T(4,128)(2,1)} %param.15) | copy-start | bytes 122884
  134.5 4.7 %collective-permute-start.33 = (bf16[4,5120]{1,0:T(4,128)(2,1)S(1)}, bf16[4,5120]{1,0:T(4,128)(2,1)S(1)}, u32[]{:S(2)}, u32[]{:S(2)}) collective-permute-start(bf16[4,5120]{1,0:T(4,128)(2,1)S(1)} %get-tuple-element.71), channel_id=1, source_target_pairs={{1,0},{3,2},{5,4},{7,6},{9,8},{11,10},{13,12},{15,14},{17,16},{19,... | collective-permute-start | bytes 122888 | tf_op jit(solution)/shard_map/ppermute | solution.py:348
  135.8 2.5 %copy-start.6 = (bf16[512,5120]{1,0:T(8,128)(2,1)S(1)}, bf16[512,5120]{1,0:T(8,128)(2,1)}, u32[]{:S(2)}) copy-start(bf16[512,5120]{1,0:T(8,128)(2,1)} %w_ref.17) | copy-start | bytes 15728644
  (12 other events, 19.2 us)

commit v2 on v1

v2 whole, which is shorter than its diff:
```python
import functools

import jax
import jax.numpy as jnp
from jax import lax
from jax.experimental import pallas as pl
from jax.experimental.pallas import tpu as pltpu
from jax.sharding import PartitionSpec as P

HD = 128
KEYWIN = 4


epsilon = 1e-06
masked_score = -1e30
VMEM_LIMIT = 16 << 20
WHOLE = pl.BlockSpec(memory_space=pltpu.VMEM)
SCALARS = pl.BlockSpec(memory_space=pltpu.SMEM)


def call(kernel, ins, outs, flops, scalars=0, scratch=(), limit=VMEM_LIMIT):
    moved = sum(x.size * x.dtype.itemsize for x in list(ins) + list(outs))
    return pl.pallas_call(
        kernel,
        in_specs=[SCALARS] * scalars + [WHOLE] * (len(ins) - scalars),
        out_specs=[WHOLE] * len(outs),
        out_shape=list(outs),
        scratch_shapes=list(scratch),
        compiler_params=pltpu.CompilerParams(vmem_limit_bytes=limit),
        cost_estimate=pl.CostEstimate(flops=flops, bytes_accessed=moved, transcendentals=0),
    )(*ins)


def like(shape, dtype=jnp.bfloat16):
    return jax.ShapeDtypeStruct(shape, dtype)


def after(arrived, done):
    return lax.optimization_barrier((arrived, done))


def prepare_kernel(tables, count, level_ref, *refs):
    ins, refs = refs[: tables + count], refs[tables + count :]
    rows, kept, scratch, sems = refs[:tables], refs[tables : tables + count], refs[tables + count : -1], refs[-1]
    copies = [
        pltpu.make_async_copy(src, dst, sems.at[i]) for i, (src, dst) in enumerate(zip(ins, (*scratch, *kept)))
    ]
    for copy in copies:
        copy.start()
    for copy in copies[:tables]:
        copy.wait()
    for f in range(rows[0].shape[0]):
        level = level_ref[f]
        for table, out in zip(scratch, rows):
            out[f : f + 1, :] = table[pl.ds(level, 1), :]
    for copy in copies[tables:]:
        copy.wait()


def prepare(levels, tables, arrays):
    anywhere = pl.BlockSpec(memory_space=pl.ANY)
    outs = [like((levels.shape[0], table.shape[1]), table.dtype) for table in tables]
    outs += [like(x.shape, x.dtype) for x in arrays]
    moved = sum(x.size * x.dtype.itemsize for x in (*tables, *arrays))
    return pl.pallas_call(
        functools.partial(prepare_kernel, len(tables), len(arrays)),
        in_specs=[SCALARS] + [anywhere] * (len(tables) + len(arrays)),
        out_specs=[WHOLE] * len(outs),
        out_shape=outs,
        scratch_shapes=[pltpu.VMEM(x.shape, x.dtype) for x in tables]
        + [pltpu.SemaphoreType.DMA((len(tables) + len(arrays),))],
        compiler_params=pltpu.CompilerParams(vmem_limit_bytes=32 << 20),
        cost_estimate=pl.CostEstimate(flops=1000, bytes_accessed=moved, transcendentals=0),
    )(levels, *tables, *arrays)


def place(column, first, total):
    rows = column.shape[0]
    lanes = lax.broadcasted_iota(jnp.int32, (rows, total), 1)
    picked = lanes == lax.broadcasted_iota(jnp.int32, (rows, total), 0) + first
    return jnp.sum(jnp.where(picked, column, 0.0), axis=0, keepdims=True)


def unplace(row, first, rows):
    total = row.shape[1]
    lanes = lax.broadcasted_iota(jnp.int32, (rows, total), 1)
    picked = lanes == lax.broadcasted_iota(jnp.int32, (rows, total), 0) + first
    return jnp.sum(jnp.where(picked, row, 0.0), axis=1, keepdims=True)


def row_of(ring, offset, rows):
    index = lax.axis_index("seq")
    first = jnp.int32(0)
    for i, device in enumerate(ring):
        first = jnp.where(index == device, (i + offset) % len(ring) * rows, first)
    return pl.multiple_of(first, rows)


def project_kernel(first_frames, offsets, ring, *refs):
    count = len(first_frames)
    x_refs, refs = refs[:count], refs[count:]
    scale_ref, shift_ref, wq_ref, wk_ref, wv_ref, gq_ref, gk_ref, q_ref, kv_ref, sq_ref, h_ref = refs
    row = 0
    for x_ref, first in zip(x_refs, first_frames):
        frames, tokens, width = x_ref.shape
        x = x_ref[...].astype(jnp.float32)
        inverse = lax.rsqrt(jnp.mean(x * x, axis=2, keepdims=True) + epsilon)
        scale = 1.0 + scale_ref[first : first + frames, :][:, None, :]
        shift = shift_ref[first : first + frames, :][:, None, :]
        hidden = (x * inverse * scale + shift).astype(jnp.bfloat16)
        h_ref[row : row + frames * tokens, :] = hidden.reshape(frames * tokens, width)
        row += frames * tokens
    rows = row // len(offsets)
    total = sq_ref.shape[1]
    hidden = h_ref[...]

    def squares_of(raw):
        column = jnp.sum(raw * raw, axis=1, keepdims=True)
        parts = [
            place(column[i * rows : (i + 1) * rows], row_of(ring, offset, rows), total)
            for i, offset in enumerate(offsets)
        ]
        return sum(parts[1:], parts[0])

    q_raw = jnp.dot(hidden, wq_ref[...], preferred_element_type=jnp.float32)
    sq_ref[0:1, :] = squares_of(q_raw)
    q_ref[...] = (q_raw * gq_ref[...]).astype(jnp.bfloat16)
    k_raw = jnp.dot(hidden, wk_ref[...], preferred_element_type=jnp.float32)
    sq_ref[1:2, :] = squares_of(k_raw)
    kv_ref[0] = (k_raw * gk_ref[...]).astype(jnp.bfloat16)
    value = jnp.dot(hidden, wv_ref[...], preferred_element_type=jnp.float32)
    kv_ref[1] = value.astype(jnp.bfloat16)


def project(blocks, offsets, first_frames, ring, scale_rows, shift_rows, weights):
    width, local = weights[0].shape
    offsets = dict.fromkeys(offsets)
    rows = sum(x.shape[0] * x.shape[1] for x in blocks)
    total = rows // len(offsets) * len(ring)
    return call(
        functools.partial(project_kernel, tuple(first_frames), tuple(offsets), ring),
        [*blocks, scale_rows, shift_rows, *weights],
        [like((rows, local)), like((2, rows, local)), like((2, total), jnp.float32)],
        6 * rows * width * local,
        scratch=[pltpu.VMEM((rows, width), jnp.bfloat16)],
    )


def gather_kernel(offsets, ring, rows, *refs):
    kv_refs, out_ref = refs[:-1], refs[-1]
    for i, kv_ref in enumerate(kv_refs):
        base = i // len(offsets) * len(ring) * rows
        for j, offset in enumerate(offsets[i % len(offsets)]):
            at = row_of(ring, offset, rows)
            out_ref[:, pl.ds(base + at, rows), :] = kv_ref[:, j * rows : (j + 1) * rows, :]


def gather(sets, offsets, ring, rows):
    local = sets[0][0].shape[2]
    return call(
        functools.partial(gather_kernel, tuple(map(tuple, offsets)), ring, rows),
        [kv for kvs in sets for kv in kvs],
        [like((2, len(sets) * len(ring) * rows, local))],
        1000,
    )[0]


def attend_kernel(sizes, ring, inner, offsets, start_ref, *refs):
    frames, tokens, sections = sizes
    q_refs, (kv_ref, sq_ref, out_ref) = refs[:-3], refs[-3:]
    rows, local = out_ref.shape
    block = rows // len(offsets)
    columns = kv_ref.shape[1]
    total = sq_ref.shape[1]
    inverse_q_row = lax.rsqrt(sq_ref[0:1, :] / inner + epsilon)
    parts = [unplace(inverse_q_row, row_of(ring, offset, block), block) for offset in offsets]
    inverse_q = parts[0] if len(parts) == 1 else jnp.concatenate(parts, axis=0)
    parts = [lax.rsqrt(sq_ref[1 + i : 2 + i, :] / inner + epsilon) for i in range(columns // total)]
    inverse_k = parts[0] if len(parts) == 1 else jnp.concatenate(parts, axis=1)
    section = lax.axis_index("segment")
    if sections == 2:
        bases = [section, 1 - section]
    else:
        bases = [section, section - 1, section + 1]
    row_frame = lax.broadcasted_iota(jnp.int32, (rows, 1), 0) // tokens % frames
    column = lax.broadcasted_iota(jnp.int32, (1, columns), 1)
    column_frame = column // tokens % frames
    key_frame = column_frame + bases[0] * frames
    for i in range(1, columns // total):
        key_frame = jnp.where(column >= i * total, column_frame + bases[i] * frames, key_frame)
    begin = row_frame + section * frames
    for f in range(frames):
        begin = jnp.where(row_frame == f, begin - start_ref[f], begin)
    key_frame = jnp.where((key_frame >= 0) & (key_frame < frames * sections), key_frame, -frames)
    usable = (key_frame >= begin) & (key_frame < begin + KEYWIN)
    usable &= jnp.broadcast_to(key_frame >= 0, usable.shape)
    inverse_q = inverse_q * HD ** (-0.5)
    for head in range(local // HD):
        lanes = slice(head * HD, (head + 1) * HD)
        parts = [q_ref[:, lanes] for q_ref in q_refs]
        q = parts[0] if len(parts) == 1 else jnp.concatenate(parts, axis=0)
        scores = lax.dot_general(
            q, kv_ref[0, :, lanes], (((1,), (1,)), ((), ())), preferred_element_type=jnp.float32
        )
        scores = jnp.where(usable, scores * inverse_q * inverse_k, masked_score)
        lifted = jnp.exp(scores - jnp.max(scores, axis=1, keepdims=True))
        weights = (lifted * (1.0 / jnp.sum(lifted, axis=1, keepdims=True))).astype(jnp.bfloat16)
        out = jnp.dot(weights, kv_ref[1, :, lanes], preferred_element_type=jnp.float32)
        out_ref[:, lanes] = out.astype(jnp.bfloat16)


def attend(queries, offsets, ring, kv, squares, window_start, sizes, inner):
    rows, local = sum(q.shape[0] for q in queries), queries[0].shape[1]
    return call(
        functools.partial(attend_kernel, sizes, ring, inner, tuple(offsets)),
        [window_start, *queries, kv, squares],
        [like((rows, local))],
        4 * rows * kv.shape[1] * local,
        scalars=1,
    )[0]


def partial_kernel(row, att_ref, w_ref, *outs):
    rows = sum(ref.shape[0] for ref in outs)
    out = jnp.dot(att_ref[row : row + rows, :], w_ref[...], preferred_element_type=jnp.float32)
    row = 0
    for ref in outs:
        ref[...] = out[row : row + ref.shape[0]].astype(jnp.bfloat16)
        row += ref.shape[0]


def partials(att, row, w_out, sizes):
    return call(
        functools.partial(partial_kernel, row),
        [att, w_out],
        [like((size, w_out.shape[1])) for size in sizes],
        2 * sum(sizes) * w_out.size,
    )


def added(own, arrived, lo):
    hi = lo + arrived.shape[0]
    total = own[lo:hi] + arrived.astype(jnp.float32)
    parts = [x for x in (own[:lo], total, own[hi:]) if x.shape[0]]
    return parts[0] if len(parts) == 1 else jnp.concatenate(parts, axis=0)


def next_sends_kernel(rows, places, right_own, left_own, right_in, left_in, right_out, left_out):
    low, high = rows
    pairs = ((right_own, right_in, right_out), (left_own, left_in, left_out))
    for at, (own, arrived, out) in zip(places, pairs):
        total = added(own[low:high, :].astype(jnp.float32), arrived[...], at)
        out[...] = total.astype(jnp.bfloat16)


def next_sends(half, places, right_own, left_own, right_in, left_in):
    rows = right_own.shape[0] // 2
    out = like((rows, right_own.shape[1]))
    return call(
        functools.partial(next_sends_kernel, (half * rows, half * rows + rows), places),
        [right_own, left_own, right_in, left_in],
        [out, out],
        4 * rows * right_own.shape[1],
    )


def updated_half(half, places, x_ref, gate_ref, own_ref, right_in, left_in):
    frames, tokens, width = x_ref.shape
    frames = frames // 2
    rows = frames * tokens
    own = own_ref[half * rows : half * rows + rows, :].astype(jnp.float32)
    own = added(added(own, right_in[...], places[0]), left_in[...], places[1])
    first = half * frames
    x = x_ref[first : first + frames].astype(jnp.float32)
    gate = gate_ref[first : first + frames, :][:, None, :]
    return (x + gate * own.reshape(frames, tokens, width)).astype(jnp.bfloat16)


def near_kernel(places, x_ref, gate_ref, own_ref, right_in, left_in, first_ref, rest_ref):
    out = updated_half(0, places, x_ref, gate_ref, own_ref, right_in, left_in)
    first_ref[...] = out[0]
    rest_ref[...] = out[1:]


def near_half(places, x, gate_rows, own, right_in, left_in):
    frames, tokens, width = x.shape
    return call(
        functools.partial(near_kernel, places),
        [x, gate_rows, own, right_in, left_in],
        [like((tokens, width)), like((frames // 2 - 1, tokens, width))],
        4 * x.size,
    )


def last_kernel(places, sections, x_ref, gate_ref, own_ref, right_in, left_in, rest_ref, handed_ref, fresh_ref, out_ref):
    frames = out_ref.shape[0]
    out = updated_half(1, places, x_ref, gate_ref, own_ref, right_in, left_in)
    out_ref[: frames // 2 - 1] = rest_ref[...]
    out_ref[frames // 2 - 1 : frames - 1] = out
    newest = lax.axis_index("segment") == sections - 1

    @pl.when(newest)
    def _():
        out_ref[frames - 1 :] = fresh_ref[...]

    @pl.when(jnp.logical_not(newest))
    def _():
        out_ref[frames - 1] = handed_ref[...]


def last_half(places, sections, x, gate_rows, own, right_in, left_in, rest, handed, fresh):
    return call(
        functools.partial(last_kernel, places, sections),
        [x, gate_rows, own, right_in, left_in, rest, handed, fresh],
        [like(x.shape)],
        4 * x.size,
    )[0]


def shards(
    ring,
    queue_frames,
    fresh_frames,
    slot_level,
    window_start,
    shift_table,
    scale_table,
    gate_table,
    w_query,
    w_key,
    w_value,
    w_out,
    query_gain,
    key_gain,
):
    peers = lax.axis_size("seq")
    sections = lax.axis_size("segment")
    frames, tokens, width = queue_frames.shape
    rows = frames * tokens
    half_frames = frames // 2
    local = w_query.shape[1]
    inner = local * peers
    far = peers // 2

    def right(x):
        return lax.ppermute(x, "seq", [(ring[i], ring[(i + 1) % peers]) for i in range(peers)])

    def left(x):
        return lax.ppermute(x, "seq", [(ring[(i + 1) % peers], ring[i]) for i in range(peers)])

    def from_sections(x):
        if sections == 2:
            return [lax.ppermute(x, "segment", [(0, 1), (1, 0)])]
        up = [(i, i + 1) for i in range(sections - 1)]
        return [lax.ppermute(x, "segment", route) for route in (up, [(j, i) for i, j in up])]

    from_left = from_right = queue_frames
    groups, offsets, waiting = [], [], [(queue_frames, 0, 0)]
    for step in range(1, far + 1):
        if step < far:
            arrived = right(from_left), left(from_right)
            news = [(peers - step, 0), (step, 0)]
        else:
            arrived = right(from_left[:half_frames]), left(from_right[half_frames:])
            news = [(far, 0), (far, half_frames)]
        if step == 1:
            prepared = prepare(
                slot_level,
                [shift_table, scale_table, gate_table],
                [w_query, w_key, w_value, query_gain[None], key_gain[None]],
            )
            arrived, prepared = after(arrived, prepared)
            shift_rows, scale_rows, gate_rows, *weights = prepared
        else:
            groups.append(project(*zip(*waiting), ring, scale_rows, shift_rows, weights))
            offsets.append(list(dict.fromkeys(offset for _, offset, _ in waiting)))
            waiting = []
            arrived, groups[-1] = after(arrived, groups[-1])
        from_left, from_right = arrived
        waiting += [(x, *new) for x, new in zip(arrived, news)]
    groups.append(project(*zip(*waiting), ring, scale_rows, shift_rows, weights))
    offsets.append(list(dict.fromkeys(offset for _, offset, _ in waiting)))

    others = [from_sections(kv) for _, kv, _ in groups]
    squares = functools.reduce(jnp.add, [sq for _, _, sq in groups])
    squares = jnp.concatenate([squares] + from_sections(squares[1:2]), axis=0)
    distance = 1
    while distance < peers:
        pairs = [(i, i ^ distance) for i in range(peers)]
        squares = squares + lax.ppermute(squares, "seq", pairs)
        distance *= 2
    sets = [[kv for _, kv, _ in groups]] + [[other[i] for other in others] for i in range(len(others[0]))]
    kv = gather(sets, offsets, ring, rows)
    sizes = (frames, tokens, sections)

    att = attend([q for q, _, _ in groups], sum(offsets, []), ring, kv, squares, window_start, sizes, inner)

    quarter = rows // 4
    order = [offset for offset in sum(offsets, [])]
    sends = partials(att, order.index(far) * rows, w_out, [quarter] * 4)
    carried = [(right(sends[0]), left(sends[1])), (right(sends[2]), left(sends[3]))]
    own = dict(zip(order, partials(att, 0, w_out, [rows] * (peers - 1))))
    places = (0, quarter)
    for step in range(far - 1, 0, -1):
        for half in range(2):
            out = next_sends(half, places, own[step], own[peers - step], *carried[half])
            carried[half] = (right(out[0]), left(out[1]))
        places = (0, 0)
    first, rest = near_half(places, queue_frames, gate_rows, own[0], *carried[0])
    handed = lax.ppermute(first, "segment", [(i, i - 1) for i in range(1, sections)])
    queue_state = last_half(
        places, sections, queue_frames, gate_rows, own[0], *carried[1], rest, handed, fresh_frames
    )
    return (queue_state, first[None, None])


def ring_order(mesh):
    axes = list(mesh.axis_names)
    index = [0] * len(axes)
    index[axes.index("seq")] = slice(None)
    places = [tuple(d.coords) for d in mesh.devices[tuple(index)]]
    spread = [d for d in range(3) if len({p[d] for p in places}) > 1]
    at = {tuple(p[d] for d in spread): i for i, p in enumerate(places)}
    if len(spread) == 1:
        return [at[key] for key in sorted(at)]
    if len(spread) == 2:
        spans = [sorted({key[i] for key in at}) for i in range(2)]
        long = 0 if len(spans[0]) % 2 == 0 else 1
        if len(spans[long]) % 2 == 0 and len(at) == len(spans[0]) * len(spans[1]):
            outward, across = spans[long], spans[1 - long]
            path = []
            for i, a in enumerate(outward):
                turn = across[1:] if i % 2 == 0 else across[:0:-1]
                path += [(a, b) for b in turn]
            path += [(a, across[0]) for a in reversed(outward)]
            return [at[key if long == 0 else key[::-1]] for key in path]
    return list(range(len(places)))


def solution(mesh):
    return jax.shard_map(
        functools.partial(shards, tuple(ring_order(mesh))),
        mesh=mesh,
        in_specs=(
            P(("groups", "segment"), "seq", None),
            P("groups", "seq", None),
            P(("groups", "segment")),
            P(("groups", "segment")),
            P(),
            P(),
            P(),
            P(None, "seq"),
            P(None, "seq"),
            P(None, "seq"),
            P("seq", None),
            P("seq"),
            P("seq"),
        ),
        out_specs=(
            P(("groups", "segment"), "seq", None),
            P(("groups", "segment"), None, "seq", None),
        ),
        check_vma=False,
    )
```

time: 142 us -> 96.1 us (0.68); the launches traced: 140 us -> 95.8 us
  local copies, waits for them, and re-layouts: 34.5 us -> 5.93 us
  Pallas kernels: 44.9 us -> 27.1 us
  waiting for transfers between devices: 25.2 us -> 29.9 us
    unnamed x52 -> x22, local copies, waits for them, and re-layouts: 32.4 us -> 5.81 us
    pallas_call x21 -> x16, Pallas kernels: 44.9 us -> 20.4 us  [call(): pl.pallas_call(kernel, in_specs=[SCALARS] * scalars + [WHOLE] * (len(ins)...]
    pallas_call x0 -> x1, Pallas kernels: none -> 6.75 us  [prepare(): pl.pallas_call(functools.partial(prepare_kernel, len(tables), len(arrays)...]
    ppermute x12, starting transfers between devices: 5.14 us -> 11.8 us  [left(): lax.ppermute(x, 'seq', [(ring[(i + 1) % peers], ring[i]) for i in range(p...]
    ppermute x12, starting transfers between devices: 20.9 us -> 14.3 us  [right(): lax.ppermute(x, 'seq', [(ring[i], ring[(i + 1) % peers]) for i in range(p...]
    ppermute x12, waiting for transfers between devices: 2.5 us -> 9.02 us  [left(): lax.ppermute(x, 'seq', [(ring[(i + 1) % peers], ring[i]) for i in range(p...]
    ppermute x12, waiting for transfers between devices: 14.7 us -> 12 us  [right(): lax.ppermute(x, 'seq', [(ring[i], ring[(i + 1) % peers]) for i in range(p...]
    ppermute x3, starting transfers between devices: 5.55 us -> 3.55 us  [shards(): squares = squares + lax.ppermute(squares, 'seq', pairs)]
  transfers between devices with their start and end apart: 34 -> 33, of which waited for: 9 -> 23; matrix products, arithmetic and copies ran while one was open for 2% -> 0% of each run, Pallas kernels for 25% -> 20%
where the time goes in v2:
time: 96.1 us; the launch traced here: 95.8 us
  starting transfers between devices  32 us (33%)
  waiting for transfers between devices  29.9 us (31%)
  Pallas kernels  27.1 us (28%)
  local copies, waits for them, and re-layouts  5.93 us (6%)
    pallas_call x16, Pallas kernels, call(): pl.pallas_call(kernel, in_specs=[SCALARS] * scalars + [WHOLE] * (len(ins)...  20.4 us
    ppermute x12, starting transfers between devices, right(): lax.ppermute(x, 'seq', [(ring[i], ring[(i + 1) % peers]) for i in range(p...  14.3 us
    ppermute x12, waiting for transfers between devices, right(): lax.ppermute(x, 'seq', [(ring[i], ring[(i + 1) % peers]) for i in range(p...  12 us
    ppermute x12, starting transfers between devices, left(): lax.ppermute(x, 'seq', [(ring[(i + 1) % peers], ring[i]) for i in range(p...  11.8 us
    ppermute x12, waiting for transfers between devices, left(): lax.ppermute(x, 'seq', [(ring[(i + 1) % peers], ring[i]) for i in range(p...  9.02 us
    ppermute x3, waiting for transfers between devices, shards(): squares = squares + lax.ppermute(squares, 'seq', pairs)  7.21 us
    pallas_call x1, Pallas kernels, prepare(): pl.pallas_call(functools.partial(prepare_kernel, len(tables), len(arrays)...  6.75 us
    unnamed x22, local copies, waits for them, and re-layouts  5.81 us
  transfers between devices with their start and end apart: 33, of which 23 were waited for; matrix products, arithmetic and copies ran while one was open for 0% of the time, Pallas kernels for 20%

profile of v2, /device:TPU:0, one launch (start us, length us, event | category | flops | bytes accessed | tf_op | source)
XLA Modules:
  0.0 95.8 jit_solution(3295840890982758810)
XLA Ops:
  0.6 3.1 %collective-permute-start = (bf16[8,4,5120]{2,1,0:T(4,128)(2,1)}, bf16[8,4,5120]{2,1,0:T(4,128)(2,1)S(1)}, u32[]{:S(2)}, u32[]{:S(2)}) collective-permute-start(bf16[8,4,5120]{2,1,0:T(4,128)(2,1)} %x_ref.3), channel_id=1, source_target_pairs={{4,8},{8,12},{12,14},{14,10},{10,6},{6,2},{2,0},{0,4},{5,9},{9,13}... | collective-permute-start | bytes 983048 | tf_op jit(solution)/shard_map/ppermute | solution.py:346
  3.7 1.3 %copy-done.1 = f32[50,5120]{1,0:T(8,128)S(1)} copy-done((f32[50,5120]{1,0:T(8,128)S(1)}, f32[50,5120]{1,0:T(8,128)}, u32[]{:S(2)}) %copy-start.1) | copy-done | bytes 1024024
  5.0 1.3 %copy-done.2 = f32[50,5120]{1,0:T(8,128)S(1)} copy-done((f32[50,5120]{1,0:T(8,128)S(1)}, f32[50,5120]{1,0:T(8,128)}, u32[]{:S(2)}) %copy-start.2) | copy-done | bytes 1024024
  6.3 1.3 %copy-done.3 = f32[50,5120]{1,0:T(8,128)S(1)} copy-done((f32[50,5120]{1,0:T(8,128)S(1)}, f32[50,5120]{1,0:T(8,128)}, u32[]{:S(2)}) %copy-start.3) | copy-done | bytes 1024024
  7.5 0.7 copy-done.5
  8.2 0.7 copy-done.6
  8.9 0.7 copy-done.7
  9.5 6.8 %shard_map.140 = (f32[8,5120]{1,0:T(8,128)S(1)}, f32[8,5120]{1,0:T(8,128)S(1)}, f32[8,5120]{1,0:T(8,128)S(1)}, bf16[5120,512]{1,0:T(8,128)(2,1)S(1)}, bf16[5120,...) custom-call(s32[8]{0:T(128)S(1)} %copy-done.7, ...), custom_call_target="tpu_custom_call" | custom-call | flops 1000 | bytes 18804736 | tf_op jit(solution)/shard_map/pallas_call | solution.py:65
  16.3 2.1 %collective-permute-start.2 = (bf16[8,4,5120]{2,1,0:T(4,128)(2,1)S(1)}, bf16[8,4,5120]{2,1,0:T(4,128)(2,1)S(1)}, u32[]{:S(2)}, u32[]{:S(2)}) collective-permute-start(bf16[8,4,5120]{2,1,0:T(4,128)(2,1)S(1)} %collective-permute-done.refs_1_), channel_id=1, source_target_pairs={{4,8},{8,12},{12,14},{14,10},{10,6},{6,2},{2,0},{0,4},{5,9},{9,13}... | collective-permute-start | bytes 983048 | tf_op jit(solution)/shard_map/ppermute | solution.py:346
  18.4 3.5 %shard_map.141 = (bf16[96,512]{1,0:T(8,128)(2,1)S(1)}, bf16[2,96,512]{2,1,0:T(8,128)(2,1)S(1)}, f32[2,256]{1,0:T(2,128)S(1)}) custom-call(bf16[8,4,5120]{2,1,0:T(4,128)(2,1)S(1)} %copy-done, bf16[8,4,5120]{2,1,0:T(4,128)(2,1)S(1)} %collective-permute-done.refs_1_, bf16[8,4,5120]{2,1,0:T(4,128)(2,1)S(1)} %collective-permute-done.1.refs_2_, ...), custom_call_target="tpu_custom_call" | custom-call | flops 1509949440 | bytes 17340416 | tf_op jit(solution)/shard_map/pallas_call | solution.py:23
  22.0 3.6 %collective-permute-done.2.refs_0_ = bf16[8,4,5120]{2,1,0:T(4,128)(2,1)S(1)} collective-permute-done((bf16[8,4,5120]{2,1,0:T(4,128)(2,1)S(1)}, bf16[8,4,5120]{2,1,0:T(4,128)(2,1)S(1)}, u32[]{:S(2)}, u32[]{:S(2)}) %collective-permute-start.2) | collective-permute-done | bytes 327712 | tf_op jit(solution)/shard_map/ppermute | solution.py:346
  25.6 1.5 %collective-permute-done.3.refs_1_ = bf16[8,4,5120]{2,1,0:T(4,128)(2,1)S(1)} collective-permute-done((bf16[8,4,5120]{2,1,0:T(4,128)(2,1)S(1)}, bf16[8,4,5120]{2,1,0:T(4,128)(2,1)S(1)}, u32[]{:S(2)}, u32[]{:S(2)}) %collective-permute-start.3) | collective-permute-done | bytes 327712 | tf_op jit(solution)/shard_map/ppermute | solution.py:349
  27.0 1.6 %collective-permute-start.4 = (bf16[8,4,5120]{2,1,0:T(4,128)(2,1)S(1)}, bf16[8,4,5120]{2,1,0:T(4,128)(2,1)S(1)}, u32[]{:S(2)}, u32[]{:S(2)}) collective-permute-start(bf16[8,4,5120]{2,1,0:T(4,128)(2,1)S(1)} %collective-permute-done.2.refs_0_), channel_id=1, source_target_pairs={{4,8},{8,12},{12,14},{14,10},{10,6},{6,2},{2,0},{0,4},{5,9},{9,13}... | collective-permute-start | bytes 983048 | tf_op jit(solution)/shard_map/ppermute | solution.py:346
  29.0 3.3 %shard_map.142 = (bf16[64,512]{1,0:T(8,128)(2,1)S(1)}, bf16[2,64,512]{2,1,0:T(8,128)(2,1)S(1)}, f32[2,256]{1,0:T(2,128)S(1)}) custom-call(bf16[8,4,5120]{2,1,0:T(4,128)(2,1)S(1)} %collective-permute-done.2.refs_0_, bf16[8,4,5120]{2,1,0:T(4,128)(2,1)S(1)} %collective-permute-done.3.refs_1_, f32[8,5120]{1,0:T(8,128)S(1)} %get-tuple-element.83.refs_3_.refs_2_, ...), custom_call_target="tpu_custom_call" | custom-call | flops 1006632960 | bytes 16914432 | tf_op jit(solution)/shard_map/pallas_call | solution.py:23
  32.4 2.4 %collective-permute-done.4.refs_0_ = bf16[8,4,5120]{2,1,0:T(4,128)(2,1)S(1)} collective-permute-done((bf16[8,4,5120]{2,1,0:T(4,128)(2,1)S(1)}, bf16[8,4,5120]{2,1,0:T(4,128)(2,1)S(1)}, u32[]{:S(2)}, u32[]{:S(2)}) %collective-permute-start.4) | collective-permute-done | bytes 327712 | tf_op jit(solution)/shard_map/ppermute | solution.py:346
  34.8 1.3 %collective-permute-done.5.refs_1_ = bf16[8,4,5120]{2,1,0:T(4,128)(2,1)S(1)} collective-permute-done((bf16[8,4,5120]{2,1,0:T(4,128)(2,1)S(1)}, bf16[8,4,5120]{2,1,0:T(4,128)(2,1)S(1)}, u32[]{:S(2)}, u32[]{:S(2)}) %collective-permute-start.5) | collective-permute-done | bytes 327712 | tf_op jit(solution)/shard_map/ppermute | solution.py:349
  36.1 1.6 %collective-permute-start.6 = (bf16[4,4,5120]{2,1,0:T(4,128)(2,1)S(1)}, bf16[4,4,5120]{2,1,0:T(4,128)(2,1)S(1)}, u32[]{:S(2)}, u32[]{:S(2)}) collective-permute-start(bf16[4,4,5120]{2,1,0:T(4,128)(2,1)S(1)} %slice.9), channel_id=1, source_target_pairs={{4,8},{8,12},{12,14},{14,10},{10,6},{6,2},{2,0},{0,4},{5,9},{9,13}... | collective-permute-start | bytes 491528 | tf_op jit(solution)/shard_map/ppermute | solution.py:346
  37.8 0.7 collective-permute-start.7
  38.5 3.3 %shard_map.143 = (bf16[64,512]{1,0:T(8,128)(2,1)S(1)}, bf16[2,64,512]{2,1,0:T(8,128)(2,1)S(1)}, f32[2,256]{1,0:T(2,128)S(1)}) custom-call(bf16[8,4,5120]{2,1,0:T(4,128)(2,1)S(1)} %collective-permute-done.4.refs_0_, bf16[8,4,5120]{2,1,0:T(4,128)(2,1)S(1)} %collective-permute-done.5.refs_1_, f32[8,5120]{1,0:T(8,128)S(1)} %get-tuple-element.83.refs_3_.refs_2_, ...), custom_call_target="tpu_custom_call" | custom-call | flops 1006632960 | bytes 16914432 | tf_op jit(solution)/shard_map/pallas_call | solution.py:23
  41.8 1.5 %collective-permute-done.7.refs_1_ = bf16[4,4,5120]{2,1,0:T(4,128)(2,1)S(1)} collective-permute-done((bf16[4,4,5120]{2,1,0:T(4,128)(2,1)S(1)}, bf16[4,4,5120]{2,1,0:T(4,128)(2,1)S(1)}, u32[]{:S(2)}, u32[]{:S(2)}) %collective-permute-start.7) | collective-permute-done | bytes 163872 | tf_op jit(solution)/shard_map/ppermute | solution.py:349
  43.4 3.1 %shard_map.144 = (bf16[32,512]{1,0:T(8,128)(2,1)S(1)}, bf16[2,32,512]{2,1,0:T(8,128)(2,1)S(1)}, f32[2,256]{1,0:T(2,128)S(1)}) custom-call(bf16[4,4,5120]{2,1,0:T(4,128)(2,1)S(1)} %collective-permute-done.6.refs_0_, bf16[4,4,5120]{2,1,0:T(4,128)(2,1)S(1)} %collective-permute-done.7.refs_1_, f32[8,5120]{1,0:T(8,128)S(1)} %get-tuple-element.83.refs_3_.refs_2_, ...), custom_call_target="tpu_custom_call" | custom-call | flops 503316480 | bytes 16488448 | tf_op jit(solution)/shard_map/pallas_call | solution.py:23
  46.5 1.1 %collective-permute-done.12 = f32[1,256]{1,0:T(1,128)S(1)} collective-permute-done((f32[1,256]{1,0:T(1,128)S(1)}, f32[1,256]{1,0:T(1,128)S(1)}, u32[]{:S(2)}, u32[]{:S(2)}) %collective-permute-start.12) | collective-permute-done | bytes 1056 | tf_op jit(solution)/shard_map/ppermute | solution.py:353
  49.2 2.1 %collective-permute-done.13 = f32[3,256]{1,0:T(4,128)S(1)} collective-permute-done((f32[3,256]{1,0:T(4,128)S(1)}, f32[3,256]{1,0:T(4,128)S(1)}, u32[]{:S(2)}, u32[]{:S(2)}) %collective-permute-start.13) | collective-permute-done | bytes 3104 | tf_op jit(solution)/shard_map/ppermute | solution.py:390
  51.3 1.6 %collective-permute-start.14 = (f32[3,256]{1,0:T(4,128)S(1)}, f32[3,256]{1,0:T(4,128)S(1)}, u32[]{:S(2)}, u32[]{:S(2)}) collective-permute-start(f32[3,256]{1,0:T(4,128)S(1)} %fusion), channel_id=1, source_target_pairs={{0,4},{2,6},{4,0},{6,2},{8,12},{10,14},{12,8},{14,10},{1,5},{3,7},... | collective-permute-start | bytes 9224 | tf_op jit(solution)/shard_map/ppermute | solution.py:390
  52.9 2.1 %collective-permute-done.14 = f32[3,256]{1,0:T(4,128)S(1)} collective-permute-done((f32[3,256]{1,0:T(4,128)S(1)}, f32[3,256]{1,0:T(4,128)S(1)}, u32[]{:S(2)}, u32[]{:S(2)}) %collective-permute-start.14) | collective-permute-done | bytes 3104 | tf_op jit(solution)/shard_map/ppermute | solution.py:390
  55.0 1.5 %collective-permute-start.15 = (f32[3,256]{1,0:T(4,128)S(1)}, f32[3,256]{1,0:T(4,128)S(1)}, u32[]{:S(2)}, u32[]{:S(2)}) collective-permute-start(f32[3,256]{1,0:T(4,128)S(1)} %add.22), channel_id=1, source_target_pairs={{0,8},{2,10},{4,12},{6,14},{8,0},{10,2},{12,4},{14,6},{1,9},{3,11}... | collective-permute-start | bytes 9224 | tf_op jit(solution)/shard_map/ppermute | solution.py:390
  56.5 3.0 %collective-permute-done.15 = f32[3,256]{1,0:T(4,128)S(1)} collective-permute-done((f32[3,256]{1,0:T(4,128)S(1)}, f32[3,256]{1,0:T(4,128)S(1)}, u32[]{:S(2)}, u32[]{:S(2)}) %collective-permute-start.15) | collective-permute-done | bytes 3104 | tf_op jit(solution)/shard_map/ppermute | solution.py:390
  59.6 2.6 %shard_map.146.att_ref = bf16[256,512]{1,0:T(8,128)(2,1)S(1)} custom-call(s32[8]{0:T(128)S(1)} %copy-done.8, bf16[96,512]{1,0:T(8,128)(2,1)S(1)} %get-tuple-element.93.refs_0_, bf16[64,512]{1,0:T(8,128)(2,1)S(1)} %get-tuple-element.99.refs_1_, bf16[64,512]{1,0:T(8,128)(2,1)S(1)} %get-tuple-element.105.refs_2_, ...), custom_call_target="tpu_custom_call" | custom-call | flops 268435456 | bytes 1575968 | tf_op jit(solution)/shard_map/pallas_call | solution.py:23
  62.3 1.0 %shard_map.148 = (bf16[8,5120]{1,0:T(8,128)(2,1)S(1)}, bf16[8,5120]{1,0:T(8,128)(2,1)S(1)}, bf16[8,5120]{1,0:T(8,128)(2,1)S(1)}, bf16[8,5120]{1,0:T(8,128)(2,1)S(1)}) custom-call(bf16[256,512]{1,0:T(8,128)(2,1)S(1)} %shard_map.146.att_ref, bf16[512,5120]{1,0:T(8,128)(2,1)S(1)} %bitcast.4), custom_call_target="tpu_custom_call" | custom-call | flops 167772160 | bytes 5832704 | tf_op jit(solution)/shard_map/pallas_call | solution.py:23
  63.3 1.6 %collective-permute-start.24 = (bf16[8,5120]{1,0:T(8,128)(2,1)S(1)}, bf16[8,5120]{1,0:T(8,128)(2,1)S(1)}, u32[]{:S(2)}, u32[]{:S(2)}) collective-permute-start(bf16[8,5120]{1,0:T(8,128)(2,1)S(1)} %get-tuple-element.132), channel_id=1, source_target_pairs={{4,8},{8,12},{12,14},{14,10},{10,6},{6,2},{2,0},{0,4},{5,9},{9,13}... | collective-permute-start | bytes 245768 | tf_op jit(solution)/shard_map/ppermute | solution.py:346
  65.3 1.5 %collective-permute-start.16 = (bf16[8,5120]{1,0:T(8,128)(2,1)S(1)}, bf16[8,5120]{1,0:T(8,128)(2,1)S(1)}, u32[]{:S(2)}, u32[]{:S(2)}) collective-permute-start(bf16[8,5120]{1,0:T(8,128)(2,1)S(1)} %get-tuple-element.124), channel_id=1, source_target_pairs={{4,8},{8,12},{12,14},{14,10},{10,6},{6,2},{2,0},{0,4},{5,9},{9,13}... | collective-permute-start | bytes 245768 | tf_op jit(solution)/shard_map/ppermute | solution.py:346
  67.4 1.4 %shard_map.147 = (bf16[32,5120]{1,0:T(8,128)(2,1)S(1)}, bf16[32,5120]{1,0:T(8,128)(2,1)S(1)}, bf16[32,5120]{1,0:T(8,128)(2,1)S(1)}, bf16[32,5120]{1,0:T(8,128)(2...) custom-call(bf16[256,512]{1,0:T(8,128)(2,1)S(1)} %shard_map.146.att_ref, ...), custom_call_target="tpu_custom_call" | custom-call | flops 1174405120 | bytes 7798784 | tf_op jit(solution)/shard_map/pallas_call | solution.py:23
  68.8 1.4 %collective-permute-done.25.left_in = bf16[8,5120]{1,0:T(8,128)(2,1)S(1)} collective-permute-done((bf16[8,5120]{1,0:T(8,128)(2,1)S(1)}, bf16[8,5120]{1,0:T(8,128)(2,1)S(1)}, u32[]{:S(2)}, u32[]{:S(2)}) %collective-permute-start.25) | collective-permute-done | bytes 81952 | tf_op jit(solution)/shard_map/ppermute | solution.py:349
  70.8 1.5 %collective-permute-start.27 = (bf16[16,5120]{1,0:T(8,128)(2,1)S(1)}, bf16[16,5120]{1,0:T(8,128)(2,1)S(1)}, u32[]{:S(2)}, u32[]{:S(2)}) collective-permute-start(bf16[16,5120]{1,0:T(8,128)(2,1)S(1)} %get-tuple-element.135), channel_id=1, source_target_pairs={{8,4},{12,8},{14,12},{10,14},{6,10},{2,6},{0,2},{4,0},{9,5},{13,9}... | collective-permute-start | bytes 491528 | tf_op jit(solution)/shard_map/ppermute | solution.py:349
  73.0 1.5 %collective-permute-start.19 = (bf16[16,5120]{1,0:T(8,128)(2,1)S(1)}, bf16[16,5120]{1,0:T(8,128)(2,1)S(1)}, u32[]{:S(2)}, u32[]{:S(2)}) collective-permute-start(bf16[16,5120]{1,0:T(8,128)(2,1)S(1)} %get-tuple-element.127), channel_id=1, source_target_pairs={{8,4},{12,8},{14,12},{10,14},{6,10},{2,6},{0,2},{4,0},{9,5},{13,9}... | collective-permute-start | bytes 491528 | tf_op jit(solution)/shard_map/ppermute | solution.py:349
  74.4 2.5 %collective-permute-done.26.right_in = bf16[16,5120]{1,0:T(8,128)(2,1)S(1)} collective-permute-done((bf16[16,5120]{1,0:T(8,128)(2,1)S(1)}, bf16[16,5120]{1,0:T(8,128)(2,1)S(1)}, u32[]{:S(2)}, u32[]{:S(2)}) %collective-permute-start.26) | collective-permute-done | bytes 163872 | tf_op jit(solution)/shard_map/ppermute | solution.py:346
  76.9 0.8 collective-permute-done.27.left_in
  78.3 1.6 %collective-permute-start.29 = (bf16[16,5120]{1,0:T(8,128)(2,1)S(1)}, bf16[16,5120]{1,0:T(8,128)(2,1)S(1)}, u32[]{:S(2)}, u32[]{:S(2)}) collective-permute-start(bf16[16,5120]{1,0:T(8,128)(2,1)S(1)} %get-tuple-element.137), channel_id=1, source_target_pairs={{8,4},{12,8},{14,12},{10,14},{6,10},{2,6},{0,2},{4,0},{9,5},{13,9}... | collective-permute-start | bytes 491528 | tf_op jit(solution)/shard_map/ppermute | solution.py:349
  80.4 0.8 collective-permute-done.19.left_in
  81.8 1.6 %collective-permute-start.21 = (bf16[16,5120]{1,0:T(8,128)(2,1)S(1)}, bf16[16,5120]{1,0:T(8,128)(2,1)S(1)}, u32[]{:S(2)}, u32[]{:S(2)}) collective-permute-start(bf16[16,5120]{1,0:T(8,128)(2,1)S(1)} %get-tuple-element.129), channel_id=1, source_target_pairs={{8,4},{12,8},{14,12},{10,14},{6,10},{2,6},{0,2},{4,0},{9,5},{13,9}... | collective-permute-start | bytes 491528 | tf_op jit(solution)/shard_map/ppermute | solution.py:349
  83.4 1.3 %collective-permute-done.28.right_in = bf16[16,5120]{1,0:T(8,128)(2,1)S(1)} collective-permute-done((bf16[16,5120]{1,0:T(8,128)(2,1)S(1)}, bf16[16,5120]{1,0:T(8,128)(2,1)S(1)}, u32[]{:S(2)}, u32[]{:S(2)}) %collective-permute-start.28) | collective-permute-done | bytes 163872 | tf_op jit(solution)/shard_map/ppermute | solution.py:346
  84.6 0.7 collective-permute-done.29.left_in
  85.5 2.0 %collective-permute-start.31 = (bf16[16,5120]{1,0:T(8,128)(2,1)S(1)}, bf16[16,5120]{1,0:T(8,128)(2,1)S(1)}, u32[]{:S(2)}, u32[]{:S(2)}) collective-permute-start(bf16[16,5120]{1,0:T(8,128)(2,1)S(1)} %get-tuple-element.139), channel_id=1, source_target_pairs={{8,4},{12,8},{14,12},{10,14},{6,10},{2,6},{0,2},{4,0},{9,5},{13,9}... | collective-permute-start | bytes 491528 | tf_op jit(solution)/shard_map/ppermute | solution.py:349
  89.0 1.6 %collective-permute-start.23 = (bf16[16,5120]{1,0:T(8,128)(2,1)S(1)}, bf16[16,5120]{1,0:T(8,128)(2,1)S(1)}, u32[]{:S(2)}, u32[]{:S(2)}) collective-permute-start(bf16[16,5120]{1,0:T(8,128)(2,1)S(1)} %get-tuple-element.131), channel_id=1, source_target_pairs={{8,4},{12,8},{14,12},{10,14},{6,10},{2,6},{0,2},{4,0},{9,5},{13,9}... | collective-permute-start | bytes 491528 | tf_op jit(solution)/shard_map/ppermute | solution.py:349
  90.9 0.7 shard_map.155
  91.6 1.3 %collective-permute-start.32 = (bf16[4,5120]{1,0:T(4,128)(2,1)}, bf16[4,5120]{1,0:T(4,128)(2,1)S(1)}, u32[]{:S(2)}, u32[]{:S(2)}) collective-permute-start(bf16[4,5120]{1,0:T(4,128)(2,1)} %get-tuple-element.141), channel_id=1, source_target_pairs={{1,0},{3,2},{5,4},{7,6},{9,8},{11,10},{13,12},{15,14},{17,16},{19,... | collective-permute-start | bytes 122888 | tf_op jit(solution)/shard_map/ppermute | solution.py:410
  92.8 1.0 %collective-permute-done.22.right_in = bf16[16,5120]{1,0:T(8,128)(2,1)S(1)} collective-permute-done((bf16[16,5120]{1,0:T(8,128)(2,1)S(1)}, bf16[16,5120]{1,0:T(8,128)(2,1)S(1)}, u32[]{:S(2)}, u32[]{:S(2)}) %collective-permute-start.22) | collective-permute-done | bytes 163872 | tf_op jit(solution)/shard_map/ppermute | solution.py:346
  94.9 0.9 shard_map.156
  (66 shorter events, 9.2 us)
Async XLA Ops:
  0.6 15.7 %collective-permute-start = (bf16[8,4,5120]{2,1,0:T(4,128)(2,1)}, bf16[8,4,5120]{2,1,0:T(4,128)(2,1)S(1)}, u32[]{:S(2)}, u32[]{:S(2)}) collective-permute-start(bf16[8,4,5120]{2,1,0:T(4,128)(2,1)} %x_ref.3), channel_id=1, source_target_pairs={{4,8},{8,12},{12,14},{14,10},{10,6},{6,2},{2,0},{0,4},{5,9},{9,13}... | collective-permute-start | bytes 983048 | tf_op jit(solution)/shard_map/ppermute | solution.py:346
  3.7 12.6 %collective-permute-start.1 = (bf16[8,4,5120]{2,1,0:T(4,128)(2,1)}, bf16[8,4,5120]{2,1,0:T(4,128)(2,1)S(1)}, u32[]{:S(2)}, u32[]{:S(2)}) collective-permute-start(bf16[8,4,5120]{2,1,0:T(4,128)(2,1)} %x_ref.3), channel_id=1, source_target_pairs={{8,4},{12,8},{14,12},{10,14},{6,10},{2,6},{0,2},{4,0},{9,5},{13,9}... | collective-permute-start | bytes 983048 | tf_op jit(solution)/shard_map/ppermute | solution.py:349
  3.7 1.3 %copy-start.1 = (f32[50,5120]{1,0:T(8,128)S(1)}, f32[50,5120]{1,0:T(8,128)}, u32[]{:S(2)}) copy-start(f32[50,5120]{1,0:T(8,128)} %refs_0_.2) | copy-start | bytes 3072004
  5.0 1.3 %copy-start.2 = (f32[50,5120]{1,0:T(8,128)S(1)}, f32[50,5120]{1,0:T(8,128)}, u32[]{:S(2)}) copy-start(f32[50,5120]{1,0:T(8,128)} %refs_1_.1) | copy-start | bytes 3072004
  6.3 1.3 %copy-start.3 = (f32[50,5120]{1,0:T(8,128)S(1)}, f32[50,5120]{1,0:T(8,128)}, u32[]{:S(2)}) copy-start(f32[50,5120]{1,0:T(8,128)} %refs_2_.1) | copy-start | bytes 3072004
  7.5 0.7 copy-start.5
  8.2 0.7 copy-start.6
  8.9 0.7 copy-start.7
  9.5 8.9 %copy-start = (bf16[8,4,5120]{2,1,0:T(4,128)(2,1)S(1)}, bf16[8,4,5120]{2,1,0:T(4,128)(2,1)}, u32[]{:S(2)}) copy-start(bf16[8,4,5120]{2,1,0:T(4,128)(2,1)} %x_ref.3) | copy-start | bytes 983044
  16.3 9.2 %collective-permute-start.2 = (bf16[8,4,5120]{2,1,0:T(4,128)(2,1)S(1)}, bf16[8,4,5120]{2,1,0:T(4,128)(2,1)S(1)}, u32[]{:S(2)}, u32[]{:S(2)}) collective-permute-start(bf16[8,4,5120]{2,1,0:T(4,128)(2,1)S(1)} %collective-permute-done.refs_1_), channel_id=1, source_target_pairs={{4,8},{8,12},{12,14},{14,10},{10,6},{6,2},{2,0},{0,4},{5,9},{9,13}... | collective-permute-start | bytes 983048 | tf_op jit(solution)/shard_map/ppermute | solution.py:346
  18.4 8.6 %collective-permute-start.3 = (bf16[8,4,5120]{2,1,0:T(4,128)(2,1)S(1)}, bf16[8,4,5120]{2,1,0:T(4,128)(2,1)S(1)}, u32[]{:S(2)}, u32[]{:S(2)}) collective-permute-start(bf16[8,4,5120]{2,1,0:T(4,128)(2,1)S(1)} %collective-permute-done.1.refs_2_), channel_id=1, source_target_pairs={{8,4},{12,8},{14,12},{10,14},{6,10},{2,6},{0,2},{4,0},{9,5},{13,9}... | collective-permute-start | bytes 983048 | tf_op jit(solution)/shard_map/ppermute | solution.py:349
  27.0 7.8 %collective-permute-start.4 = (bf16[8,4,5120]{2,1,0:T(4,128)(2,1)S(1)}, bf16[8,4,5120]{2,1,0:T(4,128)(2,1)S(1)}, u32[]{:S(2)}, u32[]{:S(2)}) collective-permute-start(bf16[8,4,5120]{2,1,0:T(4,128)(2,1)S(1)} %collective-permute-done.2.refs_0_), channel_id=1, source_target_pairs={{4,8},{8,12},{12,14},{14,10},{10,6},{6,2},{2,0},{0,4},{5,9},{9,13}... | collective-permute-start | bytes 983048 | tf_op jit(solution)/shard_map/ppermute | solution.py:346
  28.6 7.5 %collective-permute-start.5 = (bf16[8,4,5120]{2,1,0:T(4,128)(2,1)S(1)}, bf16[8,4,5120]{2,1,0:T(4,128)(2,1)S(1)}, u32[]{:S(2)}, u32[]{:S(2)}) collective-permute-start(bf16[8,4,5120]{2,1,0:T(4,128)(2,1)S(1)} %collective-permute-done.3.refs_1_), channel_id=1, source_target_pairs={{8,4},{12,8},{14,12},{10,14},{6,10},{2,6},{0,2},{4,0},{9,5},{13,9}... | collective-permute-start | bytes 983048 | tf_op jit(solution)/shard_map/ppermute | solution.py:349
  36.1 5.7 %collective-permute-start.6 = (bf16[4,4,5120]{2,1,0:T(4,128)(2,1)S(1)}, bf16[4,4,5120]{2,1,0:T(4,128)(2,1)S(1)}, u32[]{:S(2)}, u32[]{:S(2)}) collective-permute-start(bf16[4,4,5120]{2,1,0:T(4,128)(2,1)S(1)} %slice.9), channel_id=1, source_target_pairs={{4,8},{8,12},{12,14},{14,10},{10,6},{6,2},{2,0},{0,4},{5,9},{9,13}... | collective-permute-start | bytes 491528 | tf_op jit(solution)/shard_map/ppermute | solution.py:346
  37.8 5.6 %collective-permute-start.7 = (bf16[4,4,5120]{2,1,0:T(4,128)(2,1)S(1)}, bf16[4,4,5120]{2,1,0:T(4,128)(2,1)S(1)}, u32[]{:S(2)}, u32[]{:S(2)}) collective-permute-start(bf16[4,4,5120]{2,1,0:T(4,128)(2,1)S(1)} %slice.10), channel_id=1, source_target_pairs={{8,4},{12,8},{14,12},{10,14},{6,10},{2,6},{0,2},{4,0},{9,5},{13,9}... | collective-permute-start | bytes 491528 | tf_op jit(solution)/shard_map/ppermute | solution.py:349
  43.4 18.9 %slice-start = ((s8[5242880]{0:T(1024)(128)(4,1)}), s8[4194304]{0:T(1024)(128)(4,1)S(1)}, s32[]{:S(2)}) async-start(s8[5242880]{0:T(1024)(128)(4,1)} %bitcast.3), calls=%async_computation | async-start | bytes 8388608
  43.4 16.3 %copy-start.8 = (s32[8]{0:T(128)S(1)}, s32[8]{0:T(128)}, u32[]{:S(2)}) copy-start(s32[8]{0:T(128)} %start_ref.1) | copy-start | bytes 100
  43.4 18.9 %slice-start.1 = ((s8[5242880]{0:T(1024)(128)(4,1)}), s8[1048576]{0:T(1024)(128)(4,1)S(1)}, s32[]{:S(2)}) async-start(s8[5242880]{0:T(1024)(128)(4,1)} %bitcast.3), calls=%async_computation.1 | async-start | bytes 2097152
  46.5 1.2 %collective-permute-start.12 = (f32[1,256]{1,0:T(1,128)S(1)}, f32[1,256]{1,0:T(1,128)S(1)}, u32[]{:S(2)}, u32[]{:S(2)}) collective-permute-start(f32[1,256]{1,0:T(1,128)S(1)} %slice.12), channel_id=1, source_target_pairs={{0,1},{1,0},{2,3},{3,2},{4,5},{5,4},{6,7},{7,6},{8,9},{9,8},{10,11... | collective-permute-start | bytes 3080 | tf_op jit(solution)/shard_map/ppermute | solution.py:353
  47.7 3.6 %collective-permute-start.13 = (f32[3,256]{1,0:T(4,128)S(1)}, f32[3,256]{1,0:T(4,128)S(1)}, u32[]{:S(2)}, u32[]{:S(2)}) collective-permute-start(f32[3,256]{1,0:T(4,128)S(1)} %pad_maximum_fusion), channel_id=1, source_target_pairs={{0,2},{2,0},{4,6},{6,4},{8,10},{10,8},{12,14},{14,12},{1,3},{3,1},... | collective-permute-start | bytes 9224 | tf_op jit(solution)/shard_map/ppermute | solution.py:390
  48.1 11.4 %collective-permute-start.8 = (bf16[2,96,512]{2,1,0:T(8,128)(2,1)S(1)}, bf16[2,96,512]{2,1,0:T(8,128)(2,1)S(1)}, u32[]{:S(2)}, u32[]{:S(2)}) collective-permute-start(bf16[2,96,512]{2,1,0:T(8,128)(2,1)S(1)} %get-tuple-element.109.refs_0_), channel_id=1, source_target_pairs={{0,1},{1,0},{2,3},{3,2},{4,5},{5,4},{6,7},{7,6},{8,9},{9,8},{10,11... | collective-permute-start | bytes 589832 | tf_op jit(solution)/shard_map/ppermute | solution.py:353
  48.1 11.4 %collective-permute-start.9 = (bf16[2,64,512]{2,1,0:T(8,128)(2,1)S(1)}, bf16[2,64,512]{2,1,0:T(8,128)(2,1)S(1)}, u32[]{:S(2)}, u32[]{:S(2)}) collective-permute-start(bf16[2,64,512]{2,1,0:T(8,128)(2,1)S(1)} %get-tuple-element.110.refs_1_), channel_id=1, source_target_pairs={{0,1},{1,0},{2,3},{3,2},{4,5},{5,4},{6,7},{7,6},{8,9},{9,8},{10,11... | collective-permute-start | bytes 393224 | tf_op jit(solution)/shard_map/ppermute | solution.py:353
  48.7 10.9 %collective-permute-start.11 = (bf16[2,32,512]{2,1,0:T(8,128)(2,1)S(1)}, bf16[2,32,512]{2,1,0:T(8,128)(2,1)S(1)}, u32[]{:S(2)}, u32[]{:S(2)}) collective-permute-start(bf16[2,32,512]{2,1,0:T(8,128)(2,1)S(1)} %get-tuple-element.112.refs_3_), channel_id=1, source_target_pairs={{0,1},{1,0},{2,3},{3,2},{4,5},{5,4},{6,7},{7,6},{8,9},{9,8},{10,11... | collective-permute-start | bytes 196616 | tf_op jit(solution)/shard_map/ppermute | solution.py:353
  48.7 10.9 %collective-permute-start.10 = (bf16[2,64,512]{2,1,0:T(8,128)(2,1)S(1)}, bf16[2,64,512]{2,1,0:T(8,128)(2,1)S(1)}, u32[]{:S(2)}, u32[]{:S(2)}) collective-permute-start(bf16[2,64,512]{2,1,0:T(8,128)(2,1)S(1)} %get-tuple-element.111.refs_2_), channel_id=1, source_target_pairs={{0,1},{1,0},{2,3},{3,2},{4,5},{5,4},{6,7},{7,6},{8,9},{9,8},{10,11... | collective-permute-start | bytes 393224 | tf_op jit(solution)/shard_map/ppermute | solution.py:353
  51.3 3.7 %collective-permute-start.14 = (f32[3,256]{1,0:T(4,128)S(1)}, f32[3,256]{1,0:T(4,128)S(1)}, u32[]{:S(2)}, u32[]{:S(2)}) collective-permute-start(f32[3,256]{1,0:T(4,128)S(1)} %fusion), channel_id=1, source_target_pairs={{0,4},{2,6},{4,0},{6,2},{8,12},{10,14},{12,8},{14,10},{1,5},{3,7},... | collective-permute-start | bytes 9224 | tf_op jit(solution)/shard_map/ppermute | solution.py:390
  55.0 4.5 %collective-permute-start.15 = (f32[3,256]{1,0:T(4,128)S(1)}, f32[3,256]{1,0:T(4,128)S(1)}, u32[]{:S(2)}, u32[]{:S(2)}) collective-permute-start(f32[3,256]{1,0:T(4,128)S(1)} %add.22), channel_id=1, source_target_pairs={{0,8},{2,10},{4,12},{6,14},{8,0},{10,2},{12,4},{14,6},{1,9},{3,11}... | collective-permute-start | bytes 9224 | tf_op jit(solution)/shard_map/ppermute | solution.py:390
  63.3 5.4 %collective-permute-start.24 = (bf16[8,5120]{1,0:T(8,128)(2,1)S(1)}, bf16[8,5120]{1,0:T(8,128)(2,1)S(1)}, u32[]{:S(2)}, u32[]{:S(2)}) collective-permute-start(bf16[8,5120]{1,0:T(8,128)(2,1)S(1)} %get-tuple-element.132), channel_id=1, source_target_pairs={{4,8},{8,12},{12,14},{14,10},{10,6},{6,2},{2,0},{0,4},{5,9},{9,13}... | collective-permute-start | bytes 245768 | tf_op jit(solution)/shard_map/ppermute | solution.py:346
  64.9 5.3 %collective-permute-start.25 = (bf16[8,5120]{1,0:T(8,128)(2,1)S(1)}, bf16[8,5120]{1,0:T(8,128)(2,1)S(1)}, u32[]{:S(2)}, u32[]{:S(2)}) collective-permute-start(bf16[8,5120]{1,0:T(8,128)(2,1)S(1)} %get-tuple-element.133), channel_id=1, source_target_pairs={{8,4},{12,8},{14,12},{10,14},{6,10},{2,6},{0,2},{4,0},{9,5},{13,9}... | collective-permute-start | bytes 245768 | tf_op jit(solution)/shard_map/ppermute | solution.py:349
  65.3 7.0 %collective-permute-start.16 = (bf16[8,5120]{1,0:T(8,128)(2,1)S(1)}, bf16[8,5120]{1,0:T(8,128)(2,1)S(1)}, u32[]{:S(2)}, u32[]{:S(2)}) collective-permute-start(bf16[8,5120]{1,0:T(8,128)(2,1)S(1)} %get-tuple-element.124), channel_id=1, source_target_pairs={{4,8},{8,12},{12,14},{14,10},{10,6},{6,2},{2,0},{0,4},{5,9},{9,13}... | collective-permute-start | bytes 245768 | tf_op jit(solution)/shard_map/ppermute | solution.py:346
  66.9 28.0 %copy-start.4 = (bf16[1,4,5120]{2,1,0:T(4,128)(2,1)S(1)}, bf16[1,4,5120]{2,1,0:T(4,128)(2,1)}, u32[]{:S(2)}) copy-start(bf16[1,4,5120]{2,1,0:T(4,128)(2,1)} %fresh_ref.1) | copy-start | bytes 122884
  66.9 5.4 %collective-permute-start.17 = (bf16[8,5120]{1,0:T(8,128)(2,1)S(1)}, bf16[8,5120]{1,0:T(8,128)(2,1)S(1)}, u32[]{:S(2)}, u32[]{:S(2)}) collective-permute-start(bf16[8,5120]{1,0:T(8,128)(2,1)S(1)} %get-tuple-element.125), channel_id=1, source_target_pairs={{8,4},{12,8},{14,12},{10,14},{6,10},{2,6},{0,2},{4,0},{9,5},{13,9}... | collective-permute-start | bytes 245768 | tf_op jit(solution)/shard_map/ppermute | solution.py:349
  70.2 6.7 %collective-permute-start.26 = (bf16[16,5120]{1,0:T(8,128)(2,1)S(1)}, bf16[16,5120]{1,0:T(8,128)(2,1)S(1)}, u32[]{:S(2)}, u32[]{:S(2)}) collective-permute-start(bf16[16,5120]{1,0:T(8,128)(2,1)S(1)} %get-tuple-element.134), channel_id=1, source_target_pairs={{4,8},{8,12},{12,14},{14,10},{10,6},{6,2},{2,0},{0,4},{5,9},{9,13}... | collective-permute-start | bytes 491528 | tf_op jit(solution)/shard_map/ppermute | solution.py:346
  70.8 6.9 %collective-permute-start.27 = (bf16[16,5120]{1,0:T(8,128)(2,1)S(1)}, bf16[16,5120]{1,0:T(8,128)(2,1)S(1)}, u32[]{:S(2)}, u32[]{:S(2)}) collective-permute-start(bf16[16,5120]{1,0:T(8,128)(2,1)S(1)} %get-tuple-element.135), channel_id=1, source_target_pairs={{8,4},{12,8},{14,12},{10,14},{6,10},{2,6},{0,2},{4,0},{9,5},{13,9}... | collective-permute-start | bytes 491528 | tf_op jit(solution)/shard_map/ppermute | solution.py:349
  72.4 8.0 %collective-permute-start.18 = (bf16[16,5120]{1,0:T(8,128)(2,1)S(1)}, bf16[16,5120]{1,0:T(8,128)(2,1)S(1)}, u32[]{:S(2)}, u32[]{:S(2)}) collective-permute-start(bf16[16,5120]{1,0:T(8,128)(2,1)S(1)} %get-tuple-element.126), channel_id=1, source_target_pairs={{4,8},{8,12},{12,14},{14,10},{10,6},{6,2},{2,0},{0,4},{5,9},{9,13}... | collective-permute-start | bytes 491528 | tf_op jit(solution)/shard_map/ppermute | solution.py:346
  73.0 8.3 %collective-permute-start.19 = (bf16[16,5120]{1,0:T(8,128)(2,1)S(1)}, bf16[16,5120]{1,0:T(8,128)(2,1)S(1)}, u32[]{:S(2)}, u32[]{:S(2)}) collective-permute-start(bf16[16,5120]{1,0:T(8,128)(2,1)S(1)} %get-tuple-element.127), channel_id=1, source_target_pairs={{8,4},{12,8},{14,12},{10,14},{6,10},{2,6},{0,2},{4,0},{9,5},{13,9}... | collective-permute-start | bytes 491528 | tf_op jit(solution)/shard_map/ppermute | solution.py:349
  77.8 6.9 %collective-permute-start.28 = (bf16[16,5120]{1,0:T(8,128)(2,1)S(1)}, bf16[16,5120]{1,0:T(8,128)(2,1)S(1)}, u32[]{:S(2)}, u32[]{:S(2)}) collective-permute-start(bf16[16,5120]{1,0:T(8,128)(2,1)S(1)} %get-tuple-element.136), channel_id=1, source_target_pairs={{4,8},{8,12},{12,14},{14,10},{10,6},{6,2},{2,0},{0,4},{5,9},{9,13}... | collective-permute-start | bytes 491528 | tf_op jit(solution)/shard_map/ppermute | solution.py:346
  78.3 7.1 %collective-permute-start.29 = (bf16[16,5120]{1,0:T(8,128)(2,1)S(1)}, bf16[16,5120]{1,0:T(8,128)(2,1)S(1)}, u32[]{:S(2)}, u32[]{:S(2)}) collective-permute-start(bf16[16,5120]{1,0:T(8,128)(2,1)S(1)} %get-tuple-element.137), channel_id=1, source_target_pairs={{8,4},{12,8},{14,12},{10,14},{6,10},{2,6},{0,2},{4,0},{9,5},{13,9}... | collective-permute-start | bytes 491528 | tf_op jit(solution)/shard_map/ppermute | solution.py:349
  81.3 6.7 %collective-permute-start.20 = (bf16[16,5120]{1,0:T(8,128)(2,1)S(1)}, bf16[16,5120]{1,0:T(8,128)(2,1)S(1)}, u32[]{:S(2)}, u32[]{:S(2)}) collective-permute-start(bf16[16,5120]{1,0:T(8,128)(2,1)S(1)} %get-tuple-element.128), channel_id=1, source_target_pairs={{4,8},{8,12},{12,14},{14,10},{10,6},{6,2},{2,0},{0,4},{5,9},{9,13}... | collective-permute-start | bytes 491528 | tf_op jit(solution)/shard_map/ppermute | solution.py:346
  81.8 6.6 %collective-permute-start.21 = (bf16[16,5120]{1,0:T(8,128)(2,1)S(1)}, bf16[16,5120]{1,0:T(8,128)(2,1)S(1)}, u32[]{:S(2)}, u32[]{:S(2)}) collective-permute-start(bf16[16,5120]{1,0:T(8,128)(2,1)S(1)} %get-tuple-element.129), channel_id=1, source_target_pairs={{8,4},{12,8},{14,12},{10,14},{6,10},{2,6},{0,2},{4,0},{9,5},{13,9}... | collective-permute-start | bytes 491528 | tf_op jit(solution)/shard_map/ppermute | solution.py:349
  85.4 5.4 %collective-permute-start.30 = (bf16[16,5120]{1,0:T(8,128)(2,1)S(1)}, bf16[16,5120]{1,0:T(8,128)(2,1)S(1)}, u32[]{:S(2)}, u32[]{:S(2)}) collective-permute-start(bf16[16,5120]{1,0:T(8,128)(2,1)S(1)} %get-tuple-element.138), channel_id=1, source_target_pairs={{4,8},{8,12},{12,14},{14,10},{10,6},{6,2},{2,0},{0,4},{5,9},{9,13}... | collective-permute-start | bytes 491528 | tf_op jit(solution)/shard_map/ppermute | solution.py:346
  85.5 5.3 %collective-permute-start.31 = (bf16[16,5120]{1,0:T(8,128)(2,1)S(1)}, bf16[16,5120]{1,0:T(8,128)(2,1)S(1)}, u32[]{:S(2)}, u32[]{:S(2)}) collective-permute-start(bf16[16,5120]{1,0:T(8,128)(2,1)S(1)} %get-tuple-element.139), channel_id=1, source_target_pairs={{8,4},{12,8},{14,12},{10,14},{6,10},{2,6},{0,2},{4,0},{9,5},{13,9}... | collective-permute-start | bytes 491528 | tf_op jit(solution)/shard_map/ppermute | solution.py:349
  88.5 5.4 %collective-permute-start.22 = (bf16[16,5120]{1,0:T(8,128)(2,1)S(1)}, bf16[16,5120]{1,0:T(8,128)(2,1)S(1)}, u32[]{:S(2)}, u32[]{:S(2)}) collective-permute-start(bf16[16,5120]{1,0:T(8,128)(2,1)S(1)} %get-tuple-element.130), channel_id=1, source_target_pairs={{4,8},{8,12},{12,14},{14,10},{10,6},{6,2},{2,0},{0,4},{5,9},{9,13}... | collective-permute-start | bytes 491528 | tf_op jit(solution)/shard_map/ppermute | solution.py:346
  89.0 5.3 %collective-permute-start.23 = (bf16[16,5120]{1,0:T(8,128)(2,1)S(1)}, bf16[16,5120]{1,0:T(8,128)(2,1)S(1)}, u32[]{:S(2)}, u32[]{:S(2)}) collective-permute-start(bf16[16,5120]{1,0:T(8,128)(2,1)S(1)} %get-tuple-element.131), channel_id=1, source_target_pairs={{8,4},{12,8},{14,12},{10,14},{6,10},{2,6},{0,2},{4,0},{9,5},{13,9}... | collective-permute-start | bytes 491528 | tf_op jit(solution)/shard_map/ppermute | solution.py:349
  91.6 3.3 %collective-permute-start.32 = (bf16[4,5120]{1,0:T(4,128)(2,1)}, bf16[4,5120]{1,0:T(4,128)(2,1)S(1)}, u32[]{:S(2)}, u32[]{:S(2)}) collective-permute-start(bf16[4,5120]{1,0:T(4,128)(2,1)} %get-tuple-element.141), channel_id=1, source_target_pairs={{1,0},{3,2},{5,4},{7,6},{9,8},{11,10},{13,12},{15,14},{17,16},{19,... | collective-permute-start | bytes 122888 | tf_op jit(solution)/shard_map/ppermute | solution.py:410

commit v3 on v2

v3 whole, which is shorter than its diff:
```python
import functools

import jax
import jax.numpy as jnp
from jax import lax
from jax.experimental import pallas as pl
from jax.experimental.pallas import tpu as pltpu
from jax.sharding import PartitionSpec as P

HD = 128
KEYWIN = 4


epsilon = 1e-06
masked_score = -1e30
VMEM_LIMIT = 16 << 20
WHOLE = pl.BlockSpec(memory_space=pltpu.VMEM)
SCALARS = pl.BlockSpec(memory_space=pltpu.SMEM)


def call(kernel, ins, outs, flops, scalars=0, scratch=(), limit=VMEM_LIMIT):
    moved = sum(x.size * x.dtype.itemsize for x in list(ins) + list(outs))
    return pl.pallas_call(
        kernel,
        in_specs=[SCALARS] * scalars + [WHOLE] * (len(ins) - scalars),
        out_specs=[WHOLE] * len(outs),
        out_shape=list(outs),
        scratch_shapes=list(scratch),
        compiler_params=pltpu.CompilerParams(vmem_limit_bytes=limit),
        cost_estimate=pl.CostEstimate(flops=flops, bytes_accessed=moved, transcendentals=0),
    )(*ins)


def like(shape, dtype=jnp.bfloat16):
    return jax.ShapeDtypeStruct(shape, dtype)


def after(arrived, done):
    return lax.optimization_barrier((arrived, done))


def prepare_kernel(tables, count, level_in, *refs):
    ins, refs = refs[: tables + count], refs[tables + count :]
    rows, kept, scratch = refs[:tables], refs[tables : tables + count], refs[tables + count : 2 * tables + count]
    level_ref, sems = refs[2 * tables + count :]
    pairs = [(level_in, level_ref), *zip(ins, (*scratch, *kept))]
    copies = [pltpu.make_async_copy(src, dst, sems.at[i]) for i, (src, dst) in enumerate(pairs)]
    for copy in copies:
        copy.start()
    for copy in copies[: tables + 1]:
        copy.wait()
    for f in range(rows[0].shape[0]):
        level = level_ref[f]
        for table, out in zip(scratch, rows):
            out[f : f + 1, :] = table[pl.ds(level, 1), :]
    for copy in copies[tables + 1 :]:
        copy.wait()


def prepare(levels, tables, arrays, limit=VMEM_LIMIT):
    in_hbm = pl.BlockSpec(memory_space=pltpu.HBM)
    outs = [like((levels.shape[0], table.shape[1]), table.dtype) for table in tables]
    outs += [like(x.shape, x.dtype) for x in arrays]
    moved = sum(x.size * x.dtype.itemsize for x in (*tables, *arrays))
    return pl.pallas_call(
        functools.partial(prepare_kernel, len(tables), len(arrays)),
        in_specs=[in_hbm] * (1 + len(tables) + len(arrays)),
        out_specs=[WHOLE] * len(outs),
        out_shape=outs,
        scratch_shapes=[pltpu.VMEM(x.shape, x.dtype) for x in tables]
        + [pltpu.SMEM(levels.shape, levels.dtype), pltpu.SemaphoreType.DMA((1 + len(tables) + len(arrays),))],
        compiler_params=pltpu.CompilerParams(vmem_limit_bytes=limit),
        cost_estimate=pl.CostEstimate(flops=1000, bytes_accessed=moved, transcendentals=0),
    )(*(pltpu.with_memory_space_constraint(x, pltpu.HBM) for x in (levels, *tables, *arrays)))


def place(column, first, total):
    rows = column.shape[0]
    lanes = lax.broadcasted_iota(jnp.int32, (rows, total), 1)
    picked = lanes == lax.broadcasted_iota(jnp.int32, (rows, total), 0) + first
    return jnp.sum(jnp.where(picked, column, 0.0), axis=0, keepdims=True)


def unplace(row, first, rows):
    total = row.shape[1]
    lanes = lax.broadcasted_iota(jnp.int32, (rows, total), 1)
    picked = lanes == lax.broadcasted_iota(jnp.int32, (rows, total), 0) + first
    return jnp.sum(jnp.where(picked, row, 0.0), axis=1, keepdims=True)


def row_of(ring, offset, rows):
    index = lax.axis_index("seq")
    first = jnp.int32(0)
    for i, device in enumerate(ring):
        first = jnp.where(index == device, (i + offset) % len(ring) * rows, first)
    return pl.multiple_of(first, rows)


def project_kernel(first_frames, offsets, ring, *refs):
    count = len(first_frames)
    x_refs, refs = refs[:count], refs[count:]
    scale_ref, shift_ref, wq_ref, wk_ref, q_ref, k_ref, sq_ref, h_ref = refs
    row = 0
    for x_ref, first in zip(x_refs, first_frames):
        frames, tokens, width = x_ref.shape
        x = x_ref[...].astype(jnp.float32)
        inverse = lax.rsqrt(jnp.mean(x * x, axis=2, keepdims=True) + epsilon)
        scale = 1.0 + scale_ref[first : first + frames, :][:, None, :]
        shift = shift_ref[first : first + frames, :][:, None, :]
        hidden = (x * inverse * scale + shift).astype(jnp.bfloat16)
        h_ref[row : row + frames * tokens, :] = hidden.reshape(frames * tokens, width)
        row += frames * tokens
    rows = row // len(offsets)
    total = sq_ref.shape[1]
    hidden = h_ref[...]

    def squares_of(raw):
        column = jnp.sum(raw * raw, axis=1, keepdims=True)
        parts = [
            place(column[i * rows : (i + 1) * rows], row_of(ring, offset, rows), total)
            for i, offset in enumerate(offsets)
        ]
        return sum(parts[1:], parts[0])

    q_raw = jnp.dot(hidden, wq_ref[...], preferred_element_type=jnp.float32)
    sq_ref[0:1, :] = squares_of(q_raw)
    q_ref[...] = q_raw
    k_raw = jnp.dot(hidden, wk_ref[...], preferred_element_type=jnp.float32)
    sq_ref[1:2, :] = squares_of(k_raw)
    k_ref[...] = k_raw


def project(blocks, offsets, first_frames, ring, scale_rows, shift_rows, weights):
    w_query, w_key = weights
    width, local = w_query.shape
    offsets = dict.fromkeys(offsets)
    rows = sum(x.shape[0] * x.shape[1] for x in blocks)
    total = rows // len(offsets) * len(ring)
    return call(
        functools.partial(project_kernel, tuple(first_frames), tuple(offsets), ring),
        [*blocks, scale_rows, shift_rows, w_query, w_key],
        [like((rows, local), jnp.float32)] * 2 + [like((2, total), jnp.float32), like((rows, width))],
        4 * rows * width * local,
    )


def finish_projection_kernel(count, *refs):
    q_refs, k_refs, h_refs = (refs[i * count : (i + 1) * count] for i in range(3))
    wv_ref, gq_ref, gk_ref, q_out, kv_out = refs[3 * count :]
    row = 0
    for q_ref, k_ref in zip(q_refs, k_refs):
        end = row + q_ref.shape[0]
        q_out[row:end, :] = (q_ref[...] * gq_ref[...]).astype(jnp.bfloat16)
        kv_out[0, row:end, :] = (k_ref[...] * gk_ref[...]).astype(jnp.bfloat16)
        row = end
    hidden = jnp.concatenate([h_ref[...] for h_ref in h_refs], axis=0)
    value = jnp.dot(hidden, wv_ref[...], preferred_element_type=jnp.float32)
    kv_out[1] = value.astype(jnp.bfloat16)


def finish_projection(groups, w_value, query_gain, key_gain):
    queries, keys, _, hidden = zip(*groups)
    rows, local = sum(q.shape[0] for q in queries), w_value.shape[1]
    return call(
        functools.partial(finish_projection_kernel, len(groups)),
        [*queries, *keys, *hidden, w_value, query_gain, key_gain],
        [like((rows, local)), like((2, rows, local))],
        2 * rows * w_value.size,
    )


def scores_kernel(sizes, ring, offsets, start_ref, q_ref, *refs):
    frames, tokens, sections = sizes
    kv_refs, (scores_ref, values_ref, keys_ref) = refs[:-3], refs[-3:]
    count = len(kv_refs)
    heads, total, columns = scores_ref.shape
    rows = total // len(ring)
    for i, kv_ref in enumerate(kv_refs):
        for j, offset in enumerate(offsets):
            at = pl.multiple_of(i * total + row_of(ring, offset, rows), rows)
            keys_ref[pl.ds(at, rows), :] = kv_ref[0, j * rows : (j + 1) * rows, :]
            values_ref[pl.ds(at, rows), :] = kv_ref[1, j * rows : (j + 1) * rows, :]
    section = lax.axis_index("segment")
    if sections == 2:
        bases = [section, 1 - section]
    else:
        bases = [section, section - 1, section + 1]
    row_frame = lax.broadcasted_iota(jnp.int32, (total, 1), 0) // tokens % frames
    column = lax.broadcasted_iota(jnp.int32, (1, columns), 1)
    column_frame = column // tokens % frames
    key_frame = column_frame + bases[0] * frames
    for i in range(1, count):
        key_frame = jnp.where(column >= i * total, column_frame + bases[i] * frames, key_frame)
    begin = row_frame + section * frames
    for f in range(frames):
        begin = jnp.where(row_frame == f, begin - start_ref[f], begin)
    key_frame = jnp.where((key_frame >= 0) & (key_frame < frames * sections), key_frame, -2 * frames)
    usable = (key_frame >= begin) & (key_frame < begin + KEYWIN)
    for head in range(heads):
        lanes = slice(head * HD, (head + 1) * HD)
        scores = lax.dot_general(
            q_ref[:, lanes], keys_ref[:, lanes], (((1,), (1,)), ((), ())), preferred_element_type=jnp.float32
        )
        scores_ref[head] = jnp.where(usable, scores * HD ** (-0.5), masked_score)


def raw_scores(queries, kv_sets, offsets, ring, window_start, sizes):
    rows, local = queries.shape
    columns = rows * len(kv_sets)
    return call(
        functools.partial(scores_kernel, sizes, ring, tuple(offsets)),
        [window_start, queries, *kv_sets],
        [like((local // HD, rows, columns), jnp.float32), like((columns, local))],
        2 * rows * columns * local,
        scalars=1,
        scratch=[pltpu.VMEM((columns, local), jnp.bfloat16)],
    )


def attend_kernel(ring, inner, offsets, scores_ref, values_ref, sq_ref, out_ref):
    heads, rows, columns = scores_ref.shape
    block = rows // len(offsets)
    inverse_q_row = lax.rsqrt(sq_ref[0:1, :] / inner + epsilon)
    parts = [unplace(inverse_q_row, row_of(ring, offset, block), block) for offset in offsets]
    inverse_q = parts[0] if len(parts) == 1 else jnp.concatenate(parts, axis=0)
    parts = [lax.rsqrt(sq_ref[1 + i : 2 + i, :] / inner + epsilon) for i in range(columns // rows)]
    inverse_k = parts[0] if len(parts) == 1 else jnp.concatenate(parts, axis=1)
    for head in range(heads):
        lanes = slice(head * HD, (head + 1) * HD)
        scores = scores_ref[head] * inverse_q * inverse_k
        lifted = jnp.exp(scores - jnp.max(scores, axis=1, keepdims=True))
        weights = (lifted * (1.0 / jnp.sum(lifted, axis=1, keepdims=True))).astype(jnp.bfloat16)
        out = jnp.dot(weights, values_ref[:, lanes], preferred_element_type=jnp.float32)
        out_ref[:, lanes] = out.astype(jnp.bfloat16)


def attend(scores, values, offsets, ring, squares, inner):
    rows, local = scores.shape[1], values.shape[1]
    return call(
        functools.partial(attend_kernel, ring, inner, tuple(offsets)),
        [scores, values, squares],
        [like((rows, local))],
        2 * rows * values.shape[0] * local,
    )[0]


def partial_kernel(row, att_ref, w_ref, *outs):
    rows = sum(ref.shape[0] for ref in outs)
    out = jnp.dot(att_ref[row : row + rows, :], w_ref[...], preferred_element_type=jnp.float32)
    row = 0
    for ref in outs:
        ref[...] = out[row : row + ref.shape[0]].astype(jnp.bfloat16)
        row += ref.shape[0]


def partials(att, row, w_out, sizes):
    return call(
        functools.partial(partial_kernel, row),
        [att, w_out],
        [like((size, w_out.shape[1])) for size in sizes],
        2 * sum(sizes) * w_out.size,
    )


def next_send_kernel(own_ref, arrived_ref, out_ref):
    total = own_ref[...].astype(jnp.float32) + arrived_ref[...].astype(jnp.float32)
    out_ref[...] = total.astype(jnp.bfloat16)


def next_send(own, arrived):
    return own if arrived is None else call(next_send_kernel, [own, arrived], [like(own.shape)], own.size)[0]


def updated(frame, count, row, x_ref, gate_ref, parts):
    tokens, width = x_ref.shape[1:]
    rows = slice(row, row + count * tokens)
    total = parts[0][rows, :].astype(jnp.float32)
    for part in parts[1:]:
        total = total + part[rows, :].astype(jnp.float32)
    x = x_ref[frame : frame + count].astype(jnp.float32)
    gate = gate_ref[frame : frame + count, :][:, None, :]
    return (x + gate * total.reshape(count, tokens, width)).astype(jnp.bfloat16)


def first_kernel(x_ref, gate_ref, *refs):
    refs[-1][...] = updated(0, 1, 0, x_ref, gate_ref, refs[:-1])[0]


def first_frame(x, gate_rows, parts):
    return call(first_kernel, [x, gate_rows, *parts], [like(x.shape[1:])], 4 * x.size)[0]


def others_kernel(counts, x_ref, gate_ref, *refs):
    parts, out_ref = refs[:-1], refs[-1]
    frames, tokens, _ = x_ref.shape
    half = frames // 2
    out_ref[: half - 1] = updated(1, half - 1, tokens, x_ref, gate_ref, parts[: counts[0]])
    out_ref[half - 1 :] = updated(half, half, 0, x_ref, gate_ref, parts[counts[0] :])


def other_frames(x, gate_rows, near, later):
    frames, tokens, width = x.shape
    counts = (len(near), len(later))
    return call(
        functools.partial(others_kernel, counts),
        [x, gate_rows, *near, *later],
        [like((frames - 1, tokens, width))],
        4 * x.size,
    )[0]


def join_kernel(sections, rest_ref, handed_ref, fresh_ref, out_ref):
    frames = out_ref.shape[0]
    out_ref[: frames - 1] = rest_ref[...]
    newest = lax.axis_index("segment") == sections - 1

    @pl.when(newest)
    def _():
        out_ref[frames - 1 :] = fresh_ref[...]

    @pl.when(jnp.logical_not(newest))
    def _():
        out_ref[frames - 1] = handed_ref[...]


def join(sections, rest, handed, fresh):
    shape = (rest.shape[0] + 1, *rest.shape[1:])
    return call(functools.partial(join_kernel, sections), [rest, handed, fresh], [like(shape)], 1000)[0]


def shards(
    ring,
    queue_frames,
    fresh_frames,
    slot_level,
    window_start,
    shift_table,
    scale_table,
    gate_table,
    w_query,
    w_key,
    w_value,
    w_out,
    query_gain,
    key_gain,
):
    peers = lax.axis_size("seq")
    sections = lax.axis_size("segment")
    frames, tokens, width = queue_frames.shape
    rows = frames * tokens
    half_frames = frames // 2
    local = w_query.shape[1]
    inner = local * peers
    far = peers // 2

    def right(x):
        return lax.ppermute(x, "seq", [(ring[i], ring[(i + 1) % peers]) for i in range(peers)])

    def left(x):
        return lax.ppermute(x, "seq", [(ring[(i + 1) % peers], ring[i]) for i in range(peers)])

    def from_sections(x):
        if sections == 2:
            return [lax.ppermute(x, "segment", [(0, 1), (1, 0)])]
        up = [(i, i + 1) for i in range(sections - 1)]
        return [lax.ppermute(x, "segment", route) for route in (up, [(j, i) for i, j in up])]

    groups, offsets = [], []

    def projected(blocks):
        out = project(*zip(*blocks), ring, scale_rows, shift_rows, weights)
        offsets.append(list(dict.fromkeys(offset for _, offset, _ in blocks)))
        return out

    halves = ((0, half_frames), (half_frames, frames))
    waiting = [(queue_frames, 0, 0)]
    if far > 1:
        arrived = right(queue_frames), left(queue_frames)
    else:
        arrived = right(queue_frames[:half_frames]), left(queue_frames[half_frames:])
    prepared = prepare(
        slot_level,
        [shift_table, scale_table],
        [w_query, w_key],
    )
    arrived, prepared = after(arrived, prepared)
    shift_rows, scale_rows, *weights = prepared
    if far > 1:
        waiting += [(arrived[0], peers - 1, 0), (arrived[1], 1, 0)]
        streams = [[x[lo:hi] for lo, hi in halves] for x in arrived]
    else:
        waiting += [(arrived[0], far, 0), (arrived[1], far, half_frames)]
    for step in range(2, far + 1):
        if step < far:
            moved = [[right(streams[0][i]), left(streams[1][i])] for i in range(2)]
        else:
            moved = [[right(streams[0][0])], [left(streams[1][1])]]
        group = projected(waiting)
        moved[0], group = after(moved[0], group)
        groups.append(group)
        if step < far:
            streams = [[moved[0][i], moved[1][i]] for i in range(2)]
            waiting = [(x, offset, first) for i, offset in ((0, peers - step), (1, step)) for x, (first, _) in zip(streams[i], halves)]
        else:
            waiting = [(moved[0][0], far, 0), (moved[1][0], far, half_frames)]
    groups.append(projected(waiting))
    offsets = sum(offsets, [])

    squares = functools.reduce(jnp.add, [group[2] for group in groups])
    other_squares, groups = after(from_sections(squares[1:2]), groups)
    squares = jnp.concatenate([squares, *other_squares], axis=0)
    queries, kv = finish_projection(groups, w_value, query_gain[None], key_gain[None])
    other_kv = from_sections(kv)
    distance = 1
    while distance < peers:
        pairs = [(i, i ^ distance) for i in range(peers)]
        arrived = lax.ppermute(squares, "seq", pairs)
        if distance == 1:
            arrived, (queries, kv) = after(arrived, (queries, kv))
        elif distance == 2:
            arrived, other_kv = after(arrived, other_kv)
        squares = squares + arrived
        distance *= 2
    scores, all_values = raw_scores(
        queries, [kv, *other_kv], offsets, ring, window_start, (frames, tokens, sections)
    )
    slot_level, _ = after(slot_level, kv)
    (gate_rows,) = prepare(slot_level, [gate_table], [])
    squares, scores, all_values, gate_rows = lax.optimization_barrier((squares, scores, all_values, gate_rows))
    att = attend(scores, all_values, offsets, ring, squares, inner)

    half_rows = rows // 2
    sends = partials(att, offsets.index(far) * rows, w_out, [half_rows] * 2)
    from_left, from_right = [right(sends[0]), None], [None, left(sends[1])]
    out = partials(att, 0, w_out, [half_rows] * (2 * peers - 2))
    own = {offset: out[2 * i : 2 * i + 2] for i, offset in enumerate(offsets[:-1])}
    for step in range(far - 1, 0, -1):
        for to_right, to_left in ((1, 0), (0, 1)):
            from_left[to_right] = right(next_send(own[step][to_right], from_left[to_right]))
            from_right[to_left] = left(next_send(own[peers - step][to_left], from_right[to_left]))
    near, later = (
        [own[0][i]] + [x for x in (from_left[i], from_right[i]) if x is not None] for i in range(2)
    )
    first = first_frame(queue_frames, gate_rows, near)
    handed = lax.ppermute(first, "segment", [(i, i - 1) for i in range(1, sections)])
    rest = other_frames(queue_frames, gate_rows, near, later)
    return (join(sections, rest, handed, fresh_frames), first[None, None])


def ring_order(mesh):
    axes = list(mesh.axis_names)
    index = [0] * len(axes)
    index[axes.index("seq")] = slice(None)
    places = [tuple(d.coords) for d in mesh.devices[tuple(index)]]
    spread = [d for d in range(3) if len({p[d] for p in places}) > 1]
    at = {tuple(p[d] for d in spread): i for i, p in enumerate(places)}
    if len(spread) == 1:
        return [at[key] for key in sorted(at)]
    if len(spread) == 2:
        spans = [sorted({key[i] for key in at}) for i in range(2)]
        long = 0 if len(spans[0]) % 2 == 0 else 1
        if len(spans[long]) % 2 == 0 and len(at) == len(spans[0]) * len(spans[1]):
            outward, across = spans[long], spans[1 - long]
            path = []
            for i, a in enumerate(outward):
                turn = across[1:] if i % 2 == 0 else across[:0:-1]
                path += [(a, b) for b in turn]
            path += [(a, across[0]) for a in reversed(outward)]
            return [at[key if long == 0 else key[::-1]] for key in path]
    return list(range(len(places)))


def solution(mesh):
    return jax.shard_map(
        functools.partial(shards, tuple(ring_order(mesh))),
        mesh=mesh,
        in_specs=(
            P(("groups", "segment"), "seq", None),
            P("groups", "seq", None),
            P(("groups", "segment")),
            P(("groups", "segment")),
            P(),
            P(),
            P(),
            P(None, "seq"),
            P(None, "seq"),
            P(None, "seq"),
            P("seq", None),
            P("seq"),
            P("seq"),
        ),
        out_specs=(
            P(("groups", "segment"), "seq", None),
            P(("groups", "segment"), None, "seq", None),
        ),
        check_vma=False,
    )
```

time: 96.1 us -> 87.5 us (0.911)
  local copies, waits for them, and re-layouts: 5.93 us -> 0.27 us
  Pallas kernels: 27.1 us -> 24.2 us
  starting transfers between devices: 32 us -> 33.1 us
  waiting for transfers between devices: 29.9 us -> 28.8 us
    ppermute x12 -> x13, starting transfers between devices: 14.3 us -> 20.7 us  [right(): lax.ppermute(x, 'seq', [(ring[i], ring[(i + 1) % peers]) for i in range(p...]
    unnamed x22 -> x18, local copies, waits for them, and re-layouts: 5.81 us -> 0.04 us
    ppermute x12 -> x13, starting transfers between devices: 11.8 us -> 7.11 us  [left(): lax.ppermute(x, 'seq', [(ring[(i + 1) % peers], ring[i]) for i in range(p...]
    pallas_call x16 -> x22, Pallas kernels: 20.4 us -> 18.1 us  [call(): pl.pallas_call(kernel, in_specs=[SCALARS] * scalars + [WHOLE] * (len(ins)...]
    ppermute x12 -> x13, waiting for transfers between devices: 12 us -> 14.1 us  [right(): lax.ppermute(x, 'seq', [(ring[i], ring[(i + 1) % peers]) for i in range(p...]
    ppermute x3, waiting for transfers between devices: 7.21 us -> 5.56 us  [shards(): arrived = lax.ppermute(squares, 'seq', pairs)]
    ppermute x12 -> x13, waiting for transfers between devices: 9.02 us -> 7.96 us  [left(): lax.ppermute(x, 'seq', [(ring[(i + 1) % peers], ring[i]) for i in range(p...]
    pallas_call x1 -> x2, Pallas kernels: 6.75 us -> 6.06 us  [prepare(): pl.pallas_call(functools.partial(prepare_kernel, len(tables), len(arrays)...]
  transfers between devices with their start and end apart: 33 -> 32, of which waited for: 23 -> 21; matrix products, arithmetic and copies ran while one was open for 0% -> 0% of each run, Pallas kernels for 20% -> 20%
where the time goes in v3:
time: 87.5 us; the launch traced here: 87.3 us
  starting transfers between devices  33.1 us (38%)
  waiting for transfers between devices  28.8 us (33%)
  Pallas kernels  24.2 us (28%)
  between operations  0.91 us (1%)
    ppermute x13, starting transfers between devices, right(): lax.ppermute(x, 'seq', [(ring[i], ring[(i + 1) % peers]) for i in range(p...  20.7 us
    pallas_call x22, Pallas kernels, call(): pl.pallas_call(kernel, in_specs=[SCALARS] * scalars + [WHOLE] * (len(ins)...  18.1 us
    ppermute x13, waiting for transfers between devices, right(): lax.ppermute(x, 'seq', [(ring[i], ring[(i + 1) % peers]) for i in range(p...  14.1 us
    ppermute x13, waiting for transfers between devices, left(): lax.ppermute(x, 'seq', [(ring[(i + 1) % peers], ring[i]) for i in range(p...  7.96 us
    ppermute x13, starting transfers between devices, left(): lax.ppermute(x, 'seq', [(ring[(i + 1) % peers], ring[i]) for i in range(p...  7.11 us
    pallas_call x2, Pallas kernels, prepare(): pl.pallas_call(functools.partial(prepare_kernel, len(tables), len(arrays)...  6.06 us
    ppermute x3, waiting for transfers between devices, shards(): arrived = lax.ppermute(squares, 'seq', pairs)  5.56 us
    ppermute x3, starting transfers between devices, shards(): arrived = lax.ppermute(squares, 'seq', pairs)  3.69 us
  transfers between devices with their start and end apart: 32, of which 21 were waited for; matrix products, arithmetic and copies ran while one was open for 0% of the time, Pallas kernels for 20%

profile of v3, /device:TPU:0, one launch (start us, length us, event | category | flops | bytes accessed | tf_op | source)
XLA Modules:
  0.0 87.3 jit_solution(554837951197170827)
XLA Ops:
  0.6 3.1 %collective-permute-start = (bf16[8,4,5120]{2,1,0:T(4,128)(2,1)}, bf16[8,4,5120]{2,1,0:T(4,128)(2,1)S(1)}, u32[]{:S(2)}, u32[]{:S(2)}) collective-permute-start(bf16[8,4,5120]{2,1,0:T(4,128)(2,1)} %x_ref.3), channel_id=1, source_target_pairs={{4,8},{8,12},{12,14},{14,10},{10,6},{6,2},{2,0},{0,4},{5,9},{9,13}... | collective-permute-start | bytes 983048 | tf_op jit(solution)/shard_map/ppermute | solution.py:357
  3.8 4.7 %shard_map.140 = (f32[8,5120]{1,0:T(8,128)S(1)}, f32[8,5120]{1,0:T(8,128)S(1)}, bf16[5120,512]{1,0:T(8,128)(2,1)S(1)}, bf16[5120,512]{1,0:T(8,128)(2,1)S(1)}) custom-call(s32[8]{0:T(128)} %level_in.2, f32[50,5120]{1,0:T(8,128)} %refs_0_.3, f32[50,5120]{1,0:T(8,128)} %refs_1_.1, bf16[5120,512]{1,0:T(8,128)(2,1)} %refs_2_.1, bf16[5120,512]{1,0:T(8,128)(2,1)} %refs_3_.1), custom_call_target="tpu_custom_call" | custom-call | flops 1000 | bytes 12533760 | tf_op jit(solution)/shard_map/pallas_call | solution.py:65
  8.5 3.1 %collective-permute-done.refs_1_ = bf16[8,4,5120]{2,1,0:T(4,128)(2,1)S(1)} collective-permute-done((bf16[8,4,5120]{2,1,0:T(4,128)(2,1)}, bf16[8,4,5120]{2,1,0:T(4,128)(2,1)S(1)}, u32[]{:S(2)}, u32[]{:S(2)}) %collective-permute-start) | collective-permute-done | bytes 327712 | tf_op jit(solution)/shard_map/ppermute | solution.py:357
  11.6 1.5 %collective-permute-done.1.refs_2_ = bf16[8,4,5120]{2,1,0:T(4,128)(2,1)S(1)} collective-permute-done((bf16[8,4,5120]{2,1,0:T(4,128)(2,1)}, bf16[8,4,5120]{2,1,0:T(4,128)(2,1)S(1)}, u32[]{:S(2)}, u32[]{:S(2)}) %collective-permute-start.1) | collective-permute-done | bytes 327712 | tf_op jit(solution)/shard_map/ppermute | solution.py:360
  13.2 1.6 %collective-permute-start.2 = (bf16[4,4,5120]{2,1,0:T(4,128)(2,1)S(1)}, bf16[4,4,5120]{2,1,0:T(4,128)(2,1)S(1)}, u32[]{:S(2)}, u32[]{:S(2)}) collective-permute-start(bf16[4,4,5120]{2,1,0:T(4,128)(2,1)S(1)} %get-tuple-element.177), channel_id=1, source_target_pairs={{4,8},{8,12},{12,14},{14,10},{10,6},{6,2},{2,0},{0,4},{5,9},{9,13}... | collective-permute-start | bytes 491528 | tf_op jit(solution)/shard_map/ppermute | solution.py:357
  15.8 1.7 %collective-permute-start.6 = (bf16[4,4,5120]{2,1,0:T(4,128)(2,1)S(1)}, bf16[4,4,5120]{2,1,0:T(4,128)(2,1)S(1)}, u32[]{:S(2)}, u32[]{:S(2)}) collective-permute-start(bf16[4,4,5120]{2,1,0:T(4,128)(2,1)S(1)} %get-tuple-element.176), channel_id=1, source_target_pairs={{4,8},{8,12},{12,14},{14,10},{10,6},{6,2},{2,0},{0,4},{5,9},{9,13}... | collective-permute-start | bytes 491528 | tf_op jit(solution)/shard_map/ppermute | solution.py:357
  17.5 2.6 %shard_map.141 = (f32[96,512]{1,0:T(8,128)S(1)}, f32[96,512]{1,0:T(8,128)S(1)}, f32[2,256]{1,0:T(2,128)S(1)}, bf16[96,5120]{1,0:T(8,128)(2,1)S(1)}) custom-call(bf16[8,4,5120]{2,1,0:T(4,128)(2,1)S(1)} %copy-done, bf16[8,4,5120]{2,1,0:T(4,128)(2,1)S(1)} %collective-permute-done.refs_1_, bf16[8,4,5120]{2,1,0:T(4,128)(2,1)S(1)} %collective-permute-done.1.refs_2_, ...), custom_call_target="tpu_custom_call" | custom-call | flops 1006632960 | bytes 13174784 | tf_op jit(solution)/shard_map/pallas_call | solution.py:23
  20.2 1.2 %collective-permute-done.3.refs_2_ = bf16[4,4,5120]{2,1,0:T(4,128)(2,1)S(1)} collective-permute-done((bf16[4,4,5120]{2,1,0:T(4,128)(2,1)S(1)}, bf16[4,4,5120]{2,1,0:T(4,128)(2,1)S(1)}, u32[]{:S(2)}, u32[]{:S(2)}) %collective-permute-start.3) | collective-permute-done | bytes 163872 | tf_op jit(solution)/shard_map/ppermute | solution.py:360
  21.3 1.6 %collective-permute-start.4 = (bf16[4,4,5120]{2,1,0:T(4,128)(2,1)S(1)}, bf16[4,4,5120]{2,1,0:T(4,128)(2,1)S(1)}, u32[]{:S(2)}, u32[]{:S(2)}) collective-permute-start(bf16[4,4,5120]{2,1,0:T(4,128)(2,1)S(1)} %collective-permute-done.2.refs_0_), channel_id=1, source_target_pairs={{4,8},{8,12},{12,14},{14,10},{10,6},{6,2},{2,0},{0,4},{5,9},{9,13}... | collective-permute-start | bytes 491528 | tf_op jit(solution)/shard_map/ppermute | solution.py:357
  23.4 1.0 %collective-permute-done.7.refs_3_ = bf16[4,4,5120]{2,1,0:T(4,128)(2,1)S(1)} collective-permute-done((bf16[4,4,5120]{2,1,0:T(4,128)(2,1)S(1)}, bf16[4,4,5120]{2,1,0:T(4,128)(2,1)S(1)}, u32[]{:S(2)}, u32[]{:S(2)}) %collective-permute-start.7) | collective-permute-done | bytes 163872 | tf_op jit(solution)/shard_map/ppermute | solution.py:360
  24.8 1.6 %collective-permute-start.9 = (bf16[4,4,5120]{2,1,0:T(4,128)(2,1)S(1)}, bf16[4,4,5120]{2,1,0:T(4,128)(2,1)S(1)}, u32[]{:S(2)}, u32[]{:S(2)}) collective-permute-start(bf16[4,4,5120]{2,1,0:T(4,128)(2,1)S(1)} %collective-permute-done.6.refs_1_), channel_id=1, source_target_pairs={{4,8},{8,12},{12,14},{14,10},{10,6},{6,2},{2,0},{0,4},{5,9},{9,13}... | collective-permute-start | bytes 491528 | tf_op jit(solution)/shard_map/ppermute | solution.py:357
  26.4 2.4 %shard_map.142 = (f32[64,512]{1,0:T(8,128)S(1)}, f32[64,512]{1,0:T(8,128)S(1)}, f32[2,256]{1,0:T(2,128)S(1)}, bf16[64,5120]{1,0:T(8,128)(2,1)S(1)}) custom-call(bf16[4,4,5120]{2,1,0:T(4,128)(2,1)S(1)} %collective-permute-done.2.refs_0_, bf16[4,4,5120]{2,1,0:T(4,128)(2,1)S(1)} %collective-permute-done.6.refs_1_, ...), custom_call_target="tpu_custom_call" | custom-call | flops 671088640 | bytes 12388352 | tf_op jit(solution)/shard_map/pallas_call | solution.py:23
  28.8 1.7 %collective-permute-start.8 = (bf16[4,4,5120]{2,1,0:T(4,128)(2,1)S(1)}, bf16[4,4,5120]{2,1,0:T(4,128)(2,1)S(1)}, u32[]{:S(2)}, u32[]{:S(2)}) collective-permute-start(bf16[4,4,5120]{2,1,0:T(4,128)(2,1)S(1)} %collective-permute-done.4.refs_0_), channel_id=1, source_target_pairs={{4,8},{8,12},{12,14},{14,10},{10,6},{6,2},{2,0},{0,4},{5,9},{9,13}... | collective-permute-start | bytes 491528 | tf_op jit(solution)/shard_map/ppermute | solution.py:357
  31.2 2.4 %shard_map.143 = (f32[64,512]{1,0:T(8,128)S(1)}, f32[64,512]{1,0:T(8,128)S(1)}, f32[2,256]{1,0:T(2,128)S(1)}, bf16[64,5120]{1,0:T(8,128)(2,1)S(1)}) custom-call(bf16[4,4,5120]{2,1,0:T(4,128)(2,1)S(1)} %collective-permute-done.4.refs_0_, bf16[4,4,5120]{2,1,0:T(4,128)(2,1)S(1)} %collective-permute-done.9.refs_1_, ...), custom_call_target="tpu_custom_call" | custom-call | flops 671088640 | bytes 12388352 | tf_op jit(solution)/shard_map/pallas_call | solution.py:23
  34.2 1.9 %collective-permute-done.11.refs_1_ = bf16[4,4,5120]{2,1,0:T(4,128)(2,1)S(1)} collective-permute-done((bf16[4,4,5120]{2,1,0:T(4,128)(2,1)S(1)}, bf16[4,4,5120]{2,1,0:T(4,128)(2,1)S(1)}, u32[]{:S(2)}, u32[]{:S(2)}) %collective-permute-start.11) | collective-permute-done | bytes 163872 | tf_op jit(solution)/shard_map/ppermute | solution.py:360
  36.1 2.2 %shard_map.144 = (f32[32,512]{1,0:T(8,128)S(1)}, f32[32,512]{1,0:T(8,128)S(1)}, f32[2,256]{1,0:T(2,128)S(1)}, bf16[32,5120]{1,0:T(8,128)(2,1)S(1)}) custom-call(bf16[4,4,5120]{2,1,0:T(4,128)(2,1)S(1)} %collective-permute-done.8.refs_0_, bf16[4,4,5120]{2,1,0:T(4,128)(2,1)S(1)} %collective-permute-done.11.refs_1_, ...), custom_call_target="tpu_custom_call" | custom-call | flops 335544320 | bytes 11601920 | tf_op jit(solution)/shard_map/pallas_call | solution.py:23
  38.4 1.1 %collective-permute-done.12 = f32[1,256]{1,0:T(1,128)S(1)} collective-permute-done((f32[1,256]{1,0:T(1,128)S(1)}, f32[1,256]{1,0:T(1,128)S(1)}, u32[]{:S(2)}, u32[]{:S(2)}) %collective-permute-start.12) | collective-permute-done | bytes 1056 | tf_op jit(solution)/shard_map/ppermute | solution.py:364
  39.6 1.6 %shard_map.145 = (bf16[256,512]{1,0:T(8,128)(2,1)S(1)}, bf16[2,256,512]{2,1,0:T(8,128)(2,1)S(1)}) custom-call(f32[96,512]{1,0:T(8,128)S(1)} %get-tuple-element.132.refs_0_, f32[64,512]{1,0:T(8,128)S(1)} %get-tuple-element.133.refs_1_, f32[64,512]{1,0:T(8,128)S(1)} %get-tuple-element.134.refs_2_, f32[32,512]{1,0:T(8,128)S(1)} %get-tuple-element.135.refs_3_, ...), custom_call_target="tpu_custom_call" | custom-call | flops 1342177280 | bytes 9703424 | tf_op jit(solution)/shard_map/pallas_call | solution.py:23
  41.9 3.2 %collective-permute-done.13 = f32[3,256]{1,0:T(4,128)S(1)} collective-permute-done((f32[3,256]{1,0:T(4,128)S(1)}, f32[3,256]{1,0:T(4,128)S(1)}, u32[]{:S(2)}, u32[]{:S(2)}) %collective-permute-start.13) | collective-permute-done | bytes 3104 | tf_op jit(solution)/shard_map/ppermute | solution.py:417
  45.1 1.4 %collective-permute-start.14 = (f32[3,256]{1,0:T(4,128)S(1)}, f32[3,256]{1,0:T(4,128)S(1)}, u32[]{:S(2)}, u32[]{:S(2)}) collective-permute-start(f32[3,256]{1,0:T(4,128)S(1)} %fusion), channel_id=1, source_target_pairs={{0,4},{2,6},{4,0},{6,2},{8,12},{10,14},{12,8},{14,10},{1,5},{3,7},... | collective-permute-start | bytes 9224 | tf_op jit(solution)/shard_map/ppermute | solution.py:417
  46.5 1.3 %shard_map.147.gate_ref = f32[8,5120]{1,0:T(8,128)S(1)} custom-call(s32[8]{0:T(128)} %level_in.2, f32[50,5120]{1,0:T(8,128)} %refs_0_.5), custom_call_target="tpu_custom_call" | custom-call | flops 1000 | bytes 1024000 | tf_op jit(solution)/shard_map/pallas_call | solution.py:65
  47.8 0.9 %collective-permute-done.14 = f32[3,256]{1,0:T(4,128)S(1)} collective-permute-done((f32[3,256]{1,0:T(4,128)S(1)}, f32[3,256]{1,0:T(4,128)S(1)}, u32[]{:S(2)}, u32[]{:S(2)}) %collective-permute-start.14) | collective-permute-done | bytes 3104 | tf_op jit(solution)/shard_map/ppermute | solution.py:417
  48.8 1.9 %collective-permute-start.16 = (f32[3,256]{1,0:T(4,128)S(1)}, f32[3,256]{1,0:T(4,128)S(1)}, u32[]{:S(2)}, u32[]{:S(2)}) collective-permute-start(f32[3,256]{1,0:T(4,128)S(1)} %add.22), channel_id=1, source_target_pairs={{0,8},{2,10},{4,12},{6,14},{8,0},{10,2},{12,4},{14,6},{1,9},{3,11}... | collective-permute-start | bytes 9224 | tf_op jit(solution)/shard_map/ppermute | solution.py:417
  50.6 1.2 %shard_map.146 = (f32[4,256,512]{2,1,0:T(8,128)S(1)}, bf16[512,512]{1,0:T(8,128)(2,1)S(1)}) custom-call(s32[8]{0:T(128)S(1)} %copy-done.4, bf16[256,512]{1,0:T(8,128)(2,1)S(1)} %get-tuple-element.148.q_ref, bf16[2,256,512]{2,1,0:T(8,128)(2,1)S(1)} %get-tuple-element.149.refs_0_, bf16[2,256,512]{2,1,0:T(8,128)(2,1)S(1)} %collective-permute-done.15.refs_1_), custom_call_target="tpu_custom_call" | custom-call | flops 134217728 | bytes 3932192 | tf_op jit(solution)/shard_map/pallas_call | solution.py:23
  51.8 1.5 %collective-permute-done.16 = f32[3,256]{1,0:T(4,128)S(1)} collective-permute-done((f32[3,256]{1,0:T(4,128)S(1)}, f32[3,256]{1,0:T(4,128)S(1)}, u32[]{:S(2)}, u32[]{:S(2)}) %collective-permute-start.16) | collective-permute-done | bytes 3104 | tf_op jit(solution)/shard_map/ppermute | solution.py:417
  53.3 1.1 %shard_map.148.att_ref = bf16[256,512]{1,0:T(8,128)(2,1)S(1)} custom-call(f32[4,256,512]{2,1,0:T(8,128)S(1)} %get-tuple-element.155.scores_ref, bf16[512,512]{1,0:T(8,128)(2,1)S(1)} %get-tuple-element.156.values_ref, f32[3,256]{1,0:T(4,128)S(1)} %add.23.sq_ref), custom_call_target="tpu_custom_call" | custom-call | flops 134217728 | bytes 2886656 | tf_op jit(solution)/shard_map/pallas_call | solution.py:23
  54.4 1.0 %shard_map.150 = (bf16[16,5120]{1,0:T(8,128)(2,1)S(1)}, bf16[16,5120]{1,0:T(8,128)(2,1)S(1)}) custom-call(bf16[256,512]{1,0:T(8,128)(2,1)S(1)} %shard_map.148.att_ref, bf16[512,5120]{1,0:T(8,128)(2,1)S(1)} %bitcast.4), custom_call_target="tpu_custom_call" | custom-call | flops 167772160 | bytes 5832704 | tf_op jit(solution)/shard_map/pallas_call | solution.py:23
  55.4 1.3 %collective-permute-start.17 = (bf16[16,5120]{1,0:T(8,128)(2,1)S(1)}, bf16[16,5120]{1,0:T(8,128)(2,1)S(1)}, u32[]{:S(2)}, u32[]{:S(2)}) collective-permute-start(bf16[16,5120]{1,0:T(8,128)(2,1)S(1)} %get-tuple-element.162), channel_id=1, source_target_pairs={{4,8},{8,12},{12,14},{14,10},{10,6},{6,2},{2,0},{0,4},{5,9},{9,13}... | collective-permute-start | bytes 491528 | tf_op jit(solution)/shard_map/ppermute | solution.py:357
  56.7 0.7 collective-permute-start.27
  57.4 1.4 %shard_map.149 = (bf16[16,5120]{1,0:T(8,128)(2,1)S(1)}, bf16[16,5120]{1,0:T(8,128)(2,1)S(1)}, bf16[16,5120]{1,0:T(8,128)(2,1)S(1)}, bf16[16,5120]{1,0:T(8,128)(2...) custom-call(bf16[256,512]{1,0:T(8,128)(2,1)S(1)} %shard_map.148.att_, ...), custom_call_target="tpu_custom_call" | custom-call | flops 1174405120 | bytes 7798784 | tf_op jit(solution)/shard_map/pallas_call | solution.py:23
  59.3 3.0 %collective-permute-done.17.arrived_ref = bf16[16,5120]{1,0:T(8,128)(2,1)S(1)} collective-permute-done((bf16[16,5120]{1,0:T(8,128)(2,1)S(1)}, bf16[16,5120]{1,0:T(8,128)(2,1)S(1)}, u32[]{:S(2)}, u32[]{:S(2)}) %collective-permute-start.17) | collective-permute-done | bytes 163872 | tf_op jit(solution)/shard_map/ppermute | solution.py:357
  62.3 1.4 %collective-permute-start.18 = (bf16[16,5120]{1,0:T(8,128)(2,1)S(1)}, bf16[16,5120]{1,0:T(8,128)(2,1)S(1)}, u32[]{:S(2)}, u32[]{:S(2)}) collective-permute-start(bf16[16,5120]{1,0:T(8,128)(2,1)S(1)} %shard_map.151), channel_id=1, source_target_pairs={{4,8},{8,12},{12,14},{14,10},{10,6},{6,2},{2,0},{0,4},{5,9},{9,13}... | collective-permute-start | bytes 491528 | tf_op jit(solution)/shard_map/ppermute | solution.py:357
  63.7 1.1 %collective-permute-start.24 = (bf16[16,5120]{1,0:T(8,128)(2,1)S(1)}, bf16[16,5120]{1,0:T(8,128)(2,1)S(1)}, u32[]{:S(2)}, u32[]{:S(2)}) collective-permute-start(bf16[16,5120]{1,0:T(8,128)(2,1)S(1)} %get-tuple-element.169), channel_id=1, source_target_pairs={{4,8},{8,12},{12,14},{14,10},{10,6},{6,2},{2,0},{0,4},{5,9},{9,13}... | collective-permute-start | bytes 491528 | tf_op jit(solution)/shard_map/ppermute | solution.py:357
  64.9 1.0 %collective-permute-start.28 = (bf16[16,5120]{1,0:T(8,128)(2,1)S(1)}, bf16[16,5120]{1,0:T(8,128)(2,1)S(1)}, u32[]{:S(2)}, u32[]{:S(2)}) collective-permute-start(bf16[16,5120]{1,0:T(8,128)(2,1)S(1)} %shard_map.158), channel_id=1, source_target_pairs={{8,4},{12,8},{14,12},{10,14},{6,10},{2,6},{0,2},{4,0},{9,5},{13,9}... | collective-permute-start | bytes 491528 | tf_op jit(solution)/shard_map/ppermute | solution.py:360
  67.1 2.4 %collective-permute-done.18.arrived_ref = bf16[16,5120]{1,0:T(8,128)(2,1)S(1)} collective-permute-done((bf16[16,5120]{1,0:T(8,128)(2,1)S(1)}, bf16[16,5120]{1,0:T(8,128)(2,1)S(1)}, u32[]{:S(2)}, u32[]{:S(2)}) %collective-permute-start.18) | collective-permute-done | bytes 163872 | tf_op jit(solution)/shard_map/ppermute | solution.py:357
  69.5 1.4 %collective-permute-start.19 = (bf16[16,5120]{1,0:T(8,128)(2,1)S(1)}, bf16[16,5120]{1,0:T(8,128)(2,1)S(1)}, u32[]{:S(2)}, u32[]{:S(2)}) collective-permute-start(bf16[16,5120]{1,0:T(8,128)(2,1)S(1)} %shard_map.152), channel_id=1, source_target_pairs={{4,8},{8,12},{12,14},{14,10},{10,6},{6,2},{2,0},{0,4},{5,9},{9,13}... | collective-permute-start | bytes 491528 | tf_op jit(solution)/shard_map/ppermute | solution.py:357
  70.9 2.1 %collective-permute-done.24.arrived_ref = bf16[16,5120]{1,0:T(8,128)(2,1)S(1)} collective-permute-done((bf16[16,5120]{1,0:T(8,128)(2,1)S(1)}, bf16[16,5120]{1,0:T(8,128)(2,1)S(1)}, u32[]{:S(2)}, u32[]{:S(2)}) %collective-permute-start.24) | collective-permute-done | bytes 163872 | tf_op jit(solution)/shard_map/ppermute | solution.py:357
  73.0 1.4 %collective-permute-start.25 = (bf16[16,5120]{1,0:T(8,128)(2,1)S(1)}, bf16[16,5120]{1,0:T(8,128)(2,1)S(1)}, u32[]{:S(2)}, u32[]{:S(2)}) collective-permute-start(bf16[16,5120]{1,0:T(8,128)(2,1)S(1)} %shard_map.156), channel_id=1, source_target_pairs={{4,8},{8,12},{12,14},{14,10},{10,6},{6,2},{2,0},{0,4},{5,9},{9,13}... | collective-permute-start | bytes 491528 | tf_op jit(solution)/shard_map/ppermute | solution.py:357
  74.4 0.7 collective-permute-start.29
  75.3 0.8 collective-permute-start.23
  76.6 1.4 %collective-permute-start.20 = (bf16[16,5120]{1,0:T(8,128)(2,1)S(1)}, bf16[16,5120]{1,0:T(8,128)(2,1)S(1)}, u32[]{:S(2)}, u32[]{:S(2)}) collective-permute-start(bf16[16,5120]{1,0:T(8,128)(2,1)S(1)} %shard_map.153), channel_id=1, source_target_pairs={{4,8},{8,12},{12,14},{14,10},{10,6},{6,2},{2,0},{0,4},{5,9},{9,13}... | collective-permute-start | bytes 491528 | tf_op jit(solution)/shard_map/ppermute | solution.py:357
  78.1 1.3 %collective-permute-done.25.arrived_ref = bf16[16,5120]{1,0:T(8,128)(2,1)S(1)} collective-permute-done((bf16[16,5120]{1,0:T(8,128)(2,1)S(1)}, bf16[16,5120]{1,0:T(8,128)(2,1)S(1)}, u32[]{:S(2)}, u32[]{:S(2)}) %collective-permute-start.25) | collective-permute-done | bytes 163872 | tf_op jit(solution)/shard_map/ppermute | solution.py:357
  79.4 1.4 %collective-permute-start.26 = (bf16[16,5120]{1,0:T(8,128)(2,1)S(1)}, bf16[16,5120]{1,0:T(8,128)(2,1)S(1)}, u32[]{:S(2)}, u32[]{:S(2)}) collective-permute-start(bf16[16,5120]{1,0:T(8,128)(2,1)S(1)} %shard_map.157), channel_id=1, source_target_pairs={{4,8},{8,12},{12,14},{14,10},{10,6},{6,2},{2,0},{0,4},{5,9},{9,13}... | collective-permute-start | bytes 491528 | tf_op jit(solution)/shard_map/ppermute | solution.py:357
  80.8 0.8 collective-permute-start.30
  82.7 1.3 %collective-permute-start.31 = (bf16[4,5120]{1,0:T(4,128)(2,1)}, bf16[4,5120]{1,0:T(4,128)(2,1)S(1)}, u32[]{:S(2)}, u32[]{:S(2)}) collective-permute-start(bf16[4,5120]{1,0:T(4,128)(2,1)} %shard_map.162), channel_id=1, source_target_pairs={{1,0},{3,2},{5,4},{7,6},{9,8},{11,10},{13,12},{15,14},{17,16},{19,... | collective-permute-start | bytes 122888 | tf_op jit(solution)/shard_map/ppermute | solution.py:445
  84.0 0.8 collective-permute-done.26.refs_4_
  84.8 1.4 %collective-permute-done.30.refs_5_ = bf16[16,5120]{1,0:T(8,128)(2,1)S(1)} collective-permute-done((bf16[16,5120]{1,0:T(8,128)(2,1)S(1)}, bf16[16,5120]{1,0:T(8,128)(2,1)S(1)}, u32[]{:S(2)}, u32[]{:S(2)}) %collective-permute-start.30) | collective-permute-done | bytes 163872 | tf_op jit(solution)/shard_map/ppermute | solution.py:360
  86.6 0.7 shard_map.163
  (68 shorter events, 8.3 us)
Async XLA Ops:
  0.6 16.9 %copy-start = (bf16[8,4,5120]{2,1,0:T(4,128)(2,1)S(1)}, bf16[8,4,5120]{2,1,0:T(4,128)(2,1)}, u32[]{:S(2)}) copy-start(bf16[8,4,5120]{2,1,0:T(4,128)(2,1)} %x_ref.3) | copy-start | bytes 983044
  0.6 11.0 %collective-permute-start = (bf16[8,4,5120]{2,1,0:T(4,128)(2,1)}, bf16[8,4,5120]{2,1,0:T(4,128)(2,1)S(1)}, u32[]{:S(2)}, u32[]{:S(2)}) collective-permute-start(bf16[8,4,5120]{2,1,0:T(4,128)(2,1)} %x_ref.3), channel_id=1, source_target_pairs={{4,8},{8,12},{12,14},{14,10},{10,6},{6,2},{2,0},{0,4},{5,9},{9,13}... | collective-permute-start | bytes 983048 | tf_op jit(solution)/shard_map/ppermute | solution.py:357
  3.7 9.4 %collective-permute-start.1 = (bf16[8,4,5120]{2,1,0:T(4,128)(2,1)}, bf16[8,4,5120]{2,1,0:T(4,128)(2,1)S(1)}, u32[]{:S(2)}, u32[]{:S(2)}) collective-permute-start(bf16[8,4,5120]{2,1,0:T(4,128)(2,1)} %x_ref.3), channel_id=1, source_target_pairs={{8,4},{12,8},{14,12},{10,14},{6,10},{2,6},{0,2},{4,0},{9,5},{13,9}... | collective-permute-start | bytes 983048 | tf_op jit(solution)/shard_map/ppermute | solution.py:360
  13.2 6.9 %collective-permute-start.2 = (bf16[4,4,5120]{2,1,0:T(4,128)(2,1)S(1)}, bf16[4,4,5120]{2,1,0:T(4,128)(2,1)S(1)}, u32[]{:S(2)}, u32[]{:S(2)}) collective-permute-start(bf16[4,4,5120]{2,1,0:T(4,128)(2,1)S(1)} %get-tuple-element.177), channel_id=1, source_target_pairs={{4,8},{8,12},{12,14},{14,10},{10,6},{6,2},{2,0},{0,4},{5,9},{9,13}... | collective-permute-start | bytes 491528 | tf_op jit(solution)/shard_map/ppermute | solution.py:357
  15.0 6.3 %collective-permute-start.3 = (bf16[4,4,5120]{2,1,0:T(4,128)(2,1)S(1)}, bf16[4,4,5120]{2,1,0:T(4,128)(2,1)S(1)}, u32[]{:S(2)}, u32[]{:S(2)}) collective-permute-start(bf16[4,4,5120]{2,1,0:T(4,128)(2,1)S(1)} %get-tuple-element.175), channel_id=1, source_target_pairs={{8,4},{12,8},{14,12},{10,14},{6,10},{2,6},{0,2},{4,0},{9,5},{13,9}... | collective-permute-start | bytes 491528 | tf_op jit(solution)/shard_map/ppermute | solution.py:360
  15.5 8.8 %collective-permute-start.7 = (bf16[4,4,5120]{2,1,0:T(4,128)(2,1)S(1)}, bf16[4,4,5120]{2,1,0:T(4,128)(2,1)S(1)}, u32[]{:S(2)}, u32[]{:S(2)}) collective-permute-start(bf16[4,4,5120]{2,1,0:T(4,128)(2,1)S(1)} %get-tuple-element.174), channel_id=1, source_target_pairs={{8,4},{12,8},{14,12},{10,14},{6,10},{2,6},{0,2},{4,0},{9,5},{13,9}... | collective-permute-start | bytes 491528 | tf_op jit(solution)/shard_map/ppermute | solution.py:360
  15.8 9.0 %collective-permute-start.6 = (bf16[4,4,5120]{2,1,0:T(4,128)(2,1)S(1)}, bf16[4,4,5120]{2,1,0:T(4,128)(2,1)S(1)}, u32[]{:S(2)}, u32[]{:S(2)}) collective-permute-start(bf16[4,4,5120]{2,1,0:T(4,128)(2,1)S(1)} %get-tuple-element.176), channel_id=1, source_target_pairs={{4,8},{8,12},{12,14},{14,10},{10,6},{6,2},{2,0},{0,4},{5,9},{9,13}... | collective-permute-start | bytes 491528 | tf_op jit(solution)/shard_map/ppermute | solution.py:357
  21.3 7.5 %collective-permute-start.4 = (bf16[4,4,5120]{2,1,0:T(4,128)(2,1)S(1)}, bf16[4,4,5120]{2,1,0:T(4,128)(2,1)S(1)}, u32[]{:S(2)}, u32[]{:S(2)}) collective-permute-start(bf16[4,4,5120]{2,1,0:T(4,128)(2,1)S(1)} %collective-permute-done.2.refs_0_), channel_id=1, source_target_pairs={{4,8},{8,12},{12,14},{14,10},{10,6},{6,2},{2,0},{0,4},{5,9},{9,13}... | collective-permute-start | bytes 491528 | tf_op jit(solution)/shard_map/ppermute | solution.py:357
  22.9 5.9 %collective-permute-start.5 = (bf16[4,4,5120]{2,1,0:T(4,128)(2,1)S(1)}, bf16[4,4,5120]{2,1,0:T(4,128)(2,1)S(1)}, u32[]{:S(2)}, u32[]{:S(2)}) collective-permute-start(bf16[4,4,5120]{2,1,0:T(4,128)(2,1)S(1)} %collective-permute-done.3.refs_2_), channel_id=1, source_target_pairs={{8,4},{12,8},{14,12},{10,14},{6,10},{2,6},{0,2},{4,0},{9,5},{13,9}... | collective-permute-start | bytes 491528 | tf_op jit(solution)/shard_map/ppermute | solution.py:360
  24.3 6.4 %collective-permute-start.10 = (bf16[4,4,5120]{2,1,0:T(4,128)(2,1)S(1)}, bf16[4,4,5120]{2,1,0:T(4,128)(2,1)S(1)}, u32[]{:S(2)}, u32[]{:S(2)}) collective-permute-start(bf16[4,4,5120]{2,1,0:T(4,128)(2,1)S(1)} %collective-permute-done.7.refs_3_), channel_id=1, source_target_pairs={{8,4},{12,8},{14,12},{10,14},{6,10},{2,6},{0,2},{4,0},{9,5},{13,9}... | collective-permute-start | bytes 491528 | tf_op jit(solution)/shard_map/ppermute | solution.py:360
  24.8 6.4 %collective-permute-start.9 = (bf16[4,4,5120]{2,1,0:T(4,128)(2,1)S(1)}, bf16[4,4,5120]{2,1,0:T(4,128)(2,1)S(1)}, u32[]{:S(2)}, u32[]{:S(2)}) collective-permute-start(bf16[4,4,5120]{2,1,0:T(4,128)(2,1)S(1)} %collective-permute-done.6.refs_1_), channel_id=1, source_target_pairs={{4,8},{8,12},{12,14},{14,10},{10,6},{6,2},{2,0},{0,4},{5,9},{9,13}... | collective-permute-start | bytes 491528 | tf_op jit(solution)/shard_map/ppermute | solution.py:357
  28.8 5.4 %collective-permute-start.8 = (bf16[4,4,5120]{2,1,0:T(4,128)(2,1)S(1)}, bf16[4,4,5120]{2,1,0:T(4,128)(2,1)S(1)}, u32[]{:S(2)}, u32[]{:S(2)}) collective-permute-start(bf16[4,4,5120]{2,1,0:T(4,128)(2,1)S(1)} %collective-permute-done.4.refs_0_), channel_id=1, source_target_pairs={{4,8},{8,12},{12,14},{14,10},{10,6},{6,2},{2,0},{0,4},{5,9},{9,13}... | collective-permute-start | bytes 491528 | tf_op jit(solution)/shard_map/ppermute | solution.py:357
  30.8 5.3 %collective-permute-start.11 = (bf16[4,4,5120]{2,1,0:T(4,128)(2,1)S(1)}, bf16[4,4,5120]{2,1,0:T(4,128)(2,1)S(1)}, u32[]{:S(2)}, u32[]{:S(2)}) collective-permute-start(bf16[4,4,5120]{2,1,0:T(4,128)(2,1)S(1)} %collective-permute-done.10.refs_3_), channel_id=1, source_target_pairs={{8,4},{12,8},{14,12},{10,14},{6,10},{2,6},{0,2},{4,0},{9,5},{13,9}... | collective-permute-start | bytes 491528 | tf_op jit(solution)/shard_map/ppermute | solution.py:360
  34.2 5.4 %slice-start.2 = ((s8[5242880]{0:T(1024)(128)(4,1)}), s8[4194304]{0:T(1024)(128)(4,1)S(1)}, s32[]{:S(2)}) async-start(s8[5242880]{0:T(1024)(128)(4,1)} %bitcast.5), calls=%async_computation.2 | async-start | bytes 8388608
  34.2 5.4 %slice-start.3 = ((s8[5242880]{0:T(1024)(128)(4,1)}), s8[1048576]{0:T(1024)(128)(4,1)S(1)}, s32[]{:S(2)}) async-start(s8[5242880]{0:T(1024)(128)(4,1)} %bitcast.5), calls=%async_computation.3 | async-start | bytes 2097152
  34.2 5.4 %copy-start.2 = (f32[512]{0:T(512)S(1)}, f32[512]{0:T(512)}, u32[]{:S(2)}) copy-start(f32[512]{0:T(512)} %param.24) | copy-start | bytes 6148
  34.2 5.4 %copy-start.3 = (f32[512]{0:T(512)S(1)}, f32[512]{0:T(512)}, u32[]{:S(2)}) copy-start(f32[512]{0:T(512)} %param.25) | copy-start | bytes 6148
  38.3 12.3 %copy-start.4 = (s32[8]{0:T(128)S(1)}, s32[8]{0:T(128)}, u32[]{:S(2)}) copy-start(s32[8]{0:T(128)} %start_ref.1) | copy-start | bytes 100
  38.3 1.2 %collective-permute-start.12 = (f32[1,256]{1,0:T(1,128)S(1)}, f32[1,256]{1,0:T(1,128)S(1)}, u32[]{:S(2)}, u32[]{:S(2)}) collective-permute-start(f32[1,256]{1,0:T(1,128)S(1)} %slice.20), channel_id=1, source_target_pairs={{0,1},{1,0},{2,3},{3,2},{4,5},{5,4},{6,7},{7,6},{8,9},{9,8},{10,11... | collective-permute-start | bytes 3080 | tf_op jit(solution)/shard_map/ppermute | solution.py:364
  39.6 14.8 %slice-start = ((s8[5242880]{0:T(1024)(128)(4,1)}), s8[4194304]{0:T(1024)(128)(4,1)S(1)}, s32[]{:S(2)}) async-start(s8[5242880]{0:T(1024)(128)(4,1)} %bitcast.3), calls=%async_computation | async-start | bytes 8388608
  39.6 14.8 %slice-start.1 = ((s8[5242880]{0:T(1024)(128)(4,1)}), s8[1048576]{0:T(1024)(128)(4,1)S(1)}, s32[]{:S(2)}) async-start(s8[5242880]{0:T(1024)(128)(4,1)} %bitcast.3), calls=%async_computation.1 | async-start | bytes 2097152
  41.2 7.5 %collective-permute-start.15 = (bf16[2,256,512]{2,1,0:T(8,128)(2,1)S(1)}, bf16[2,256,512]{2,1,0:T(8,128)(2,1)S(1)}, u32[]{:S(2)}, u32[]{:S(2)}) collective-permute-start(bf16[2,256,512]{2,1,0:T(8,128)(2,1)S(1)} %get-tuple-element.149.refs_0_), channel_id=1, source_target_pairs={{0,1},{1,0},{2,3},{3,2},{4,5},{5,4},{6,7},{7,6},{8,9},{9,8},{10,11... | collective-permute-start | bytes 1572872 | tf_op jit(solution)/shard_map/ppermute | solution.py:364
  41.5 3.6 %collective-permute-start.13 = (f32[3,256]{1,0:T(4,128)S(1)}, f32[3,256]{1,0:T(4,128)S(1)}, u32[]{:S(2)}, u32[]{:S(2)}) collective-permute-start(f32[3,256]{1,0:T(4,128)S(1)} %pad_maximum_fusion), channel_id=1, source_target_pairs={{0,2},{2,0},{4,6},{6,4},{8,10},{10,8},{12,14},{14,12},{1,3},{3,1},... | collective-permute-start | bytes 9224 | tf_op jit(solution)/shard_map/ppermute | solution.py:417
  45.1 3.7 %collective-permute-start.14 = (f32[3,256]{1,0:T(4,128)S(1)}, f32[3,256]{1,0:T(4,128)S(1)}, u32[]{:S(2)}, u32[]{:S(2)}) collective-permute-start(f32[3,256]{1,0:T(4,128)S(1)} %fusion), channel_id=1, source_target_pairs={{0,4},{2,6},{4,0},{6,2},{8,12},{10,14},{12,8},{14,10},{1,5},{3,7},... | collective-permute-start | bytes 9224 | tf_op jit(solution)/shard_map/ppermute | solution.py:417
  48.8 4.5 %collective-permute-start.16 = (f32[3,256]{1,0:T(4,128)S(1)}, f32[3,256]{1,0:T(4,128)S(1)}, u32[]{:S(2)}, u32[]{:S(2)}) collective-permute-start(f32[3,256]{1,0:T(4,128)S(1)} %add.22), channel_id=1, source_target_pairs={{0,8},{2,10},{4,12},{6,14},{8,0},{10,2},{12,4},{14,6},{1,9},{3,11}... | collective-permute-start | bytes 9224 | tf_op jit(solution)/shard_map/ppermute | solution.py:417
  55.4 6.9 %collective-permute-start.17 = (bf16[16,5120]{1,0:T(8,128)(2,1)S(1)}, bf16[16,5120]{1,0:T(8,128)(2,1)S(1)}, u32[]{:S(2)}, u32[]{:S(2)}) collective-permute-start(bf16[16,5120]{1,0:T(8,128)(2,1)S(1)} %get-tuple-element.162), channel_id=1, source_target_pairs={{4,8},{8,12},{12,14},{14,10},{10,6},{6,2},{2,0},{0,4},{5,9},{9,13}... | collective-permute-start | bytes 491528 | tf_op jit(solution)/shard_map/ppermute | solution.py:357
  56.7 29.8 %copy-start.1 = (bf16[1,4,5120]{2,1,0:T(4,128)(2,1)S(1)}, bf16[1,4,5120]{2,1,0:T(4,128)(2,1)}, u32[]{:S(2)}) copy-start(bf16[1,4,5120]{2,1,0:T(4,128)(2,1)} %fresh_ref.1) | copy-start | bytes 122884
  56.7 8.1 %collective-permute-start.27 = (bf16[16,5120]{1,0:T(8,128)(2,1)S(1)}, bf16[16,5120]{1,0:T(8,128)(2,1)S(1)}, u32[]{:S(2)}, u32[]{:S(2)}) collective-permute-start(bf16[16,5120]{1,0:T(8,128)(2,1)S(1)} %get-tuple-element.173), channel_id=1, source_target_pairs={{8,4},{12,8},{14,12},{10,14},{6,10},{2,6},{0,2},{4,0},{9,5},{13,9}... | collective-permute-start | bytes 491528 | tf_op jit(solution)/shard_map/ppermute | solution.py:360
  58.8 7.7 %collective-permute-start.21 = (bf16[16,5120]{1,0:T(8,128)(2,1)S(1)}, bf16[16,5120]{1,0:T(8,128)(2,1)S(1)}, u32[]{:S(2)}, u32[]{:S(2)}) collective-permute-start(bf16[16,5120]{1,0:T(8,128)(2,1)S(1)} %get-tuple-element.165), channel_id=1, source_target_pairs={{8,4},{12,8},{14,12},{10,14},{6,10},{2,6},{0,2},{4,0},{9,5},{13,9}... | collective-permute-start | bytes 491528 | tf_op jit(solution)/shard_map/ppermute | solution.py:360
  62.3 7.1 %collective-permute-start.18 = (bf16[16,5120]{1,0:T(8,128)(2,1)S(1)}, bf16[16,5120]{1,0:T(8,128)(2,1)S(1)}, u32[]{:S(2)}, u32[]{:S(2)}) collective-permute-start(bf16[16,5120]{1,0:T(8,128)(2,1)S(1)} %shard_map.151), channel_id=1, source_target_pairs={{4,8},{8,12},{12,14},{14,10},{10,6},{6,2},{2,0},{0,4},{5,9},{9,13}... | collective-permute-start | bytes 491528 | tf_op jit(solution)/shard_map/ppermute | solution.py:357
  63.7 9.2 %collective-permute-start.24 = (bf16[16,5120]{1,0:T(8,128)(2,1)S(1)}, bf16[16,5120]{1,0:T(8,128)(2,1)S(1)}, u32[]{:S(2)}, u32[]{:S(2)}) collective-permute-start(bf16[16,5120]{1,0:T(8,128)(2,1)S(1)} %get-tuple-element.169), channel_id=1, source_target_pairs={{4,8},{8,12},{12,14},{14,10},{10,6},{6,2},{2,0},{0,4},{5,9},{9,13}... | collective-permute-start | bytes 491528 | tf_op jit(solution)/shard_map/ppermute | solution.py:357
  64.9 9.5 %collective-permute-start.28 = (bf16[16,5120]{1,0:T(8,128)(2,1)S(1)}, bf16[16,5120]{1,0:T(8,128)(2,1)S(1)}, u32[]{:S(2)}, u32[]{:S(2)}) collective-permute-start(bf16[16,5120]{1,0:T(8,128)(2,1)S(1)} %shard_map.158), channel_id=1, source_target_pairs={{8,4},{12,8},{14,12},{10,14},{6,10},{2,6},{0,2},{4,0},{9,5},{13,9}... | collective-permute-start | bytes 491528 | tf_op jit(solution)/shard_map/ppermute | solution.py:360
  66.6 8.7 %collective-permute-start.22 = (bf16[16,5120]{1,0:T(8,128)(2,1)S(1)}, bf16[16,5120]{1,0:T(8,128)(2,1)S(1)}, u32[]{:S(2)}, u32[]{:S(2)}) collective-permute-start(bf16[16,5120]{1,0:T(8,128)(2,1)S(1)} %shard_map.154), channel_id=1, source_target_pairs={{8,4},{12,8},{14,12},{10,14},{6,10},{2,6},{0,2},{4,0},{9,5},{13,9}... | collective-permute-start | bytes 491528 | tf_op jit(solution)/shard_map/ppermute | solution.py:360
  69.5 7.1 %collective-permute-start.19 = (bf16[16,5120]{1,0:T(8,128)(2,1)S(1)}, bf16[16,5120]{1,0:T(8,128)(2,1)S(1)}, u32[]{:S(2)}, u32[]{:S(2)}) collective-permute-start(bf16[16,5120]{1,0:T(8,128)(2,1)S(1)} %shard_map.152), channel_id=1, source_target_pairs={{4,8},{8,12},{12,14},{14,10},{10,6},{6,2},{2,0},{0,4},{5,9},{9,13}... | collective-permute-start | bytes 491528 | tf_op jit(solution)/shard_map/ppermute | solution.py:357
  73.0 6.4 %collective-permute-start.25 = (bf16[16,5120]{1,0:T(8,128)(2,1)S(1)}, bf16[16,5120]{1,0:T(8,128)(2,1)S(1)}, u32[]{:S(2)}, u32[]{:S(2)}) collective-permute-start(bf16[16,5120]{1,0:T(8,128)(2,1)S(1)} %shard_map.156), channel_id=1, source_target_pairs={{4,8},{8,12},{12,14},{14,10},{10,6},{6,2},{2,0},{0,4},{5,9},{9,13}... | collective-permute-start | bytes 491528 | tf_op jit(solution)/shard_map/ppermute | solution.py:357
  74.4 6.3 %collective-permute-start.29 = (bf16[16,5120]{1,0:T(8,128)(2,1)S(1)}, bf16[16,5120]{1,0:T(8,128)(2,1)S(1)}, u32[]{:S(2)}, u32[]{:S(2)}) collective-permute-start(bf16[16,5120]{1,0:T(8,128)(2,1)S(1)} %shard_map.159), channel_id=1, source_target_pairs={{8,4},{12,8},{14,12},{10,14},{6,10},{2,6},{0,2},{4,0},{9,5},{13,9}... | collective-permute-start | bytes 491528 | tf_op jit(solution)/shard_map/ppermute | solution.py:360
  75.3 6.3 %collective-permute-start.23 = (bf16[16,5120]{1,0:T(8,128)(2,1)S(1)}, bf16[16,5120]{1,0:T(8,128)(2,1)S(1)}, u32[]{:S(2)}, u32[]{:S(2)}) collective-permute-start(bf16[16,5120]{1,0:T(8,128)(2,1)S(1)} %shard_map.155), channel_id=1, source_target_pairs={{8,4},{12,8},{14,12},{10,14},{6,10},{2,6},{0,2},{4,0},{9,5},{13,9}... | collective-permute-start | bytes 491528 | tf_op jit(solution)/shard_map/ppermute | solution.py:360
  76.6 5.4 %collective-permute-start.20 = (bf16[16,5120]{1,0:T(8,128)(2,1)S(1)}, bf16[16,5120]{1,0:T(8,128)(2,1)S(1)}, u32[]{:S(2)}, u32[]{:S(2)}) collective-permute-start(bf16[16,5120]{1,0:T(8,128)(2,1)S(1)} %shard_map.153), channel_id=1, source_target_pairs={{4,8},{8,12},{12,14},{14,10},{10,6},{6,2},{2,0},{0,4},{5,9},{9,13}... | collective-permute-start | bytes 491528 | tf_op jit(solution)/shard_map/ppermute | solution.py:357
  79.4 5.4 %collective-permute-start.26 = (bf16[16,5120]{1,0:T(8,128)(2,1)S(1)}, bf16[16,5120]{1,0:T(8,128)(2,1)S(1)}, u32[]{:S(2)}, u32[]{:S(2)}) collective-permute-start(bf16[16,5120]{1,0:T(8,128)(2,1)S(1)} %shard_map.157), channel_id=1, source_target_pairs={{4,8},{8,12},{12,14},{14,10},{10,6},{6,2},{2,0},{0,4},{5,9},{9,13}... | collective-permute-start | bytes 491528 | tf_op jit(solution)/shard_map/ppermute | solution.py:357
  80.8 5.4 %collective-permute-start.30 = (bf16[16,5120]{1,0:T(8,128)(2,1)S(1)}, bf16[16,5120]{1,0:T(8,128)(2,1)S(1)}, u32[]{:S(2)}, u32[]{:S(2)}) collective-permute-start(bf16[16,5120]{1,0:T(8,128)(2,1)S(1)} %shard_map.160), channel_id=1, source_target_pairs={{8,4},{12,8},{14,12},{10,14},{6,10},{2,6},{0,2},{4,0},{9,5},{13,9}... | collective-permute-start | bytes 491528 | tf_op jit(solution)/shard_map/ppermute | solution.py:360
  82.7 3.9 %collective-permute-start.31 = (bf16[4,5120]{1,0:T(4,128)(2,1)}, bf16[4,5120]{1,0:T(4,128)(2,1)S(1)}, u32[]{:S(2)}, u32[]{:S(2)}) collective-permute-start(bf16[4,5120]{1,0:T(4,128)(2,1)} %shard_map.162), channel_id=1, source_target_pairs={{1,0},{3,2},{5,4},{7,6},{9,8},{11,10},{13,12},{15,14},{17,16},{19,... | collective-permute-start | bytes 122888 | tf_op jit(solution)/shard_map/ppermute | solution.py:445

commit v4 on v3

--- a/solution.py
+++ b/solution.py
@@ -217,45 +217,45 @@
     )
 
 
-def attend_kernel(ring, inner, offsets, scores_ref, values_ref, sq_ref, out_ref):
-    heads, rows, columns = scores_ref.shape
+def attend_kernel(ring, inner, first, offsets, scores_ref, values_ref, sq_ref, out_ref):
+    heads, total, columns = scores_ref.shape
+    rows = out_ref.shape[0]
     block = rows // len(offsets)
     inverse_q_row = lax.rsqrt(sq_ref[0:1, :] / inner + epsilon)
     parts = [unplace(inverse_q_row, row_of(ring, offset, block), block) for offset in offsets]
     inverse_q = parts[0] if len(parts) == 1 else jnp.concatenate(parts, axis=0)
-    parts = [lax.rsqrt(sq_ref[1 + i : 2 + i, :] / inner + epsilon) for i in range(columns // rows)]
+    parts = [lax.rsqrt(sq_ref[1 + i : 2 + i, :] / inner + epsilon) for i in range(columns // total)]
     inverse_k = parts[0] if len(parts) == 1 else jnp.concatenate(parts, axis=1)
     for head in range(heads):
         lanes = slice(head * HD, (head + 1) * HD)
-        scores = scores_ref[head] * inverse_q * inverse_k
+        scores = scores_ref[head, first : first + rows, :] * inverse_q * inverse_k
         lifted = jnp.exp(scores - jnp.max(scores, axis=1, keepdims=True))
         weights = (lifted * (1.0 / jnp.sum(lifted, axis=1, keepdims=True))).astype(jnp.bfloat16)
         out = jnp.dot(weights, values_ref[:, lanes], preferred_element_type=jnp.float32)
         out_ref[:, lanes] = out.astype(jnp.bfloat16)
 
 
-def attend(scores, values, offsets, ring, squares, inner):
-    rows, local = scores.shape[1], values.shape[1]
-    return call(
-        functools.partial(attend_kernel, ring, inner, tuple(offsets)),
+def attend(scores, values, first, offsets, ring, squares, inner):
+    rows, local = scores.shape[1] // len(ring) * len(offsets), values.shape[1]
+    return call(
+        functools.partial(attend_kernel, ring, inner, first, tuple(offsets)),
         [scores, values, squares],
         [like((rows, local))],
         2 * rows * values.shape[0] * local,
     )[0]
 
 
-def partial_kernel(row, att_ref, w_ref, *outs):
-    rows = sum(ref.shape[0] for ref in outs)
-    out = jnp.dot(att_ref[row : row + rows, :], w_ref[...], preferred_element_type=jnp.float32)
+def partial_kernel(att_ref, w_ref, *outs):
+    out = jnp.dot(att_ref[...], w_ref[...], preferred_element_type=jnp.float32)
     row = 0
     for ref in outs:
         ref[...] = out[row : row + ref.shape[0]].astype(jnp.bfloat16)
         row += ref.shape[0]
 
 
-def partials(att, row, w_out, sizes):
-    return call(
-        functools.partial(partial_kernel, row),
+def partials(att, w_out, sizes):
+    return call(
+        partial_kernel,
         [att, w_out],
         [like((size, w_out.shape[1])) for size in sizes],
         2 * sum(sizes) * w_out.size,
@@ -290,28 +290,12 @@
     return call(first_kernel, [x, gate_rows, *parts], [like(x.shape[1:])], 4 * x.size)[0]
 
 
-def others_kernel(counts, x_ref, gate_ref, *refs):
+def others_kernel(counts, sections, x_ref, gate_ref, handed_ref, fresh_ref, *refs):
     parts, out_ref = refs[:-1], refs[-1]
     frames, tokens, _ = x_ref.shape
     half = frames // 2
     out_ref[: half - 1] = updated(1, half - 1, tokens, x_ref, gate_ref, parts[: counts[0]])
-    out_ref[half - 1 :] = updated(half, half, 0, x_ref, gate_ref, parts[counts[0] :])
-
-
-def other_frames(x, gate_rows, near, later):
-    frames, tokens, width = x.shape
-    counts = (len(near), len(later))
-    return call(
-        functools.partial(others_kernel, counts),
-        [x, gate_rows, *near, *later],
-        [like((frames - 1, tokens, width))],
-        4 * x.size,
-    )[0]
-
-
-def join_kernel(sections, rest_ref, handed_ref, fresh_ref, out_ref):
-    frames = out_ref.shape[0]
-    out_ref[: frames - 1] = rest_ref[...]
+    out_ref[half - 1 : frames - 1] = updated(half, half, 0, x_ref, gate_ref, parts[counts[0] :])
     newest = lax.axis_index("segment") == sections - 1
 
     @pl.when(newest)
@@ -323,9 +307,13 @@
         out_ref[frames - 1] = handed_ref[...]
 
 
-def join(sections, rest, handed, fresh):
-    shape = (rest.shape[0] + 1, *rest.shape[1:])
-    return call(functools.partial(join_kernel, sections), [rest, handed, fresh], [like(shape)], 1000)[0]
+def next_queue(x, gate_rows, handed, fresh, near, later, sections):
+    return call(
+        functools.partial(others_kernel, (len(near), len(later)), sections),
+        [x, gate_rows, handed, fresh, *near, *later],
+        [like(x.shape)],
+        4 * x.size,
+    )[0]
 
 
 def shards(
@@ -359,11 +347,16 @@
     def left(x):
         return lax.ppermute(x, "seq", [(ring[(i + 1) % peers], ring[i]) for i in range(peers)])
 
-    def from_sections(x):
+    def from_sections(x, pairs=None):
         if sections == 2:
-            return [lax.ppermute(x, "segment", [(0, 1), (1, 0)])]
-        up = [(i, i + 1) for i in range(sections - 1)]
-        return [lax.ppermute(x, "segment", route) for route in (up, [(j, i) for i, j in up])]
+            routes = [[(0, 1), (1, 0)]]
+        else:
+            up = [(i, i + 1) for i in range(sections - 1)]
+            routes = [up, [(j, i) for i, j in up]]
+        if pairs is None:
+            return [lax.ppermute(x, "segment", route) for route in routes]
+        joint = [[(i * sections + k, j * sections + l) for i, j in pairs for k, l in route] for route in routes]
+        return [lax.ppermute(x, ("seq", "segment"), route) for route in joint]
 
     groups, offsets = [], []
 
@@ -372,67 +365,65 @@
         offsets.append(list(dict.fromkeys(offset for _, offset, _ in blocks)))
         return out
 
-    halves = ((0, half_frames), (half_frames, frames))
+    halves = (queue_frames[:half_frames], queue_frames[half_frames:])
+    firsts = (0, half_frames)
     waiting = [(queue_frames, 0, 0)]
-    if far > 1:
-        arrived = right(queue_frames), left(queue_frames)
-    else:
-        arrived = right(queue_frames[:half_frames]), left(queue_frames[half_frames:])
-    prepared = prepare(
-        slot_level,
-        [shift_table, scale_table],
-        [w_query, w_key],
-    )
-    arrived, prepared = after(arrived, prepared)
-    shift_rows, scale_rows, *weights = prepared
-    if far > 1:
-        waiting += [(arrived[0], peers - 1, 0), (arrived[1], 1, 0)]
-        streams = [[x[lo:hi] for lo, hi in halves] for x in arrived]
-    else:
-        waiting += [(arrived[0], far, 0), (arrived[1], far, half_frames)]
-    for step in range(2, far + 1):
+    to_right, to_left = list(halves), list(halves)
+    for step in range(1, far + 1):
+        lead = right(to_right[0]), left(to_left[1])
         if step < far:
-            moved = [[right(streams[0][i]), left(streams[1][i])] for i in range(2)]
+            lag = right(to_right[1]), left(to_left[0])
+        if step == 1:
+            prepared = prepare(slot_level, [shift_table, scale_table], [w_query, w_key])
+            lead, prepared = after(lead, prepared)
+            shift_rows, scale_rows, *weights = prepared
         else:
-            moved = [[right(streams[0][0])], [left(streams[1][1])]]
-        group = projected(waiting)
-        moved[0], group = after(moved[0], group)
-        groups.append(group)
+            group = projected(waiting)
+            lead, group = after(lead, group)
+            groups.append(group)
+            waiting = []
         if step < far:
-            streams = [[moved[0][i], moved[1][i]] for i in range(2)]
-            waiting = [(x, offset, first) for i, offset in ((0, peers - step), (1, step)) for x, (first, _) in zip(streams[i], halves)]
+            to_right, to_left = [lead[0], lag[0]], [lag[1], lead[1]]
+            for blocks, offset in ((to_right, peers - step), (to_left, step)):
+                waiting += [(x, offset, first) for x, first in zip(blocks, firsts)]
         else:
-            waiting = [(moved[0][0], far, 0), (moved[1][0], far, half_frames)]
+            waiting += [(x, far, first) for x, first in zip(lead, firsts)]
     groups.append(projected(waiting))
     offsets = sum(offsets, [])
 
-    squares = functools.reduce(jnp.add, [group[2] for group in groups])
-    other_squares, groups = after(from_sections(squares[1:2]), groups)
-    squares = jnp.concatenate([squares, *other_squares], axis=0)
-    queries, kv = finish_projection(groups, w_value, query_gain[None], key_gain[None])
-    other_kv = from_sections(kv)
+    own = functools.reduce(jnp.add, [group[2] for group in groups])
     distance = 1
     while distance < peers:
         pairs = [(i, i ^ distance) for i in range(peers)]
-        arrived = lax.ppermute(squares, "seq", pairs)
         if distance == 1:
-            arrived, (queries, kv) = after(arrived, (queries, kv))
-        elif distance == 2:
-            arrived, other_kv = after(arrived, other_kv)
-        squares = squares + arrived
+            arrived = lax.ppermute(own, "seq", pairs)
+            near = from_sections(own[1:2])
+            away = from_sections(own[1:2], pairs)
+            arrived, near, away, groups = lax.optimization_barrier((arrived, near, away, groups))
+            own = jnp.concatenate([own + arrived] + [x + y for x, y in zip(near, away)], axis=0)
+        else:
+            arrived = lax.ppermute(own, "seq", pairs)
+            if distance == 2:
+                queries, kv = finish_projection(groups, w_value, query_gain[None], key_gain[None])
+                arrived, (queries, kv) = after(arrived, (queries, kv))
+                other_kv = from_sections(kv)
+            own = own + arrived
         distance *= 2
+    squares = own
     scores, all_values = raw_scores(
         queries, [kv, *other_kv], offsets, ring, window_start, (frames, tokens, sections)
     )
     slot_level, _ = after(slot_level, kv)
     (gate_rows,) = prepare(slot_level, [gate_table], [])
     squares, scores, all_values, gate_rows = lax.optimization_barrier((squares, scores, all_values, gate_rows))
-    att = attend(scores, all_values, offsets, ring, squares, inner)
+
+    def attended(first, last):
+        return attend(scores, all_values, first * rows, offsets[first:last], ring, squares, inner)
 
     half_rows = rows // 2
-    sends = partials(att, offsets.index(far) * rows, w_out, [half_rows] * 2)
+    sends = partials(attended(peers - 1, peers), w_out, [half_rows] * 2)
     from_left, from_right = [right(sends[0]), None], [None, left(sends[1])]
-    out = partials(att, 0, w_out, [half_rows] * (2 * peers - 2))
+    out = partials(attended(0, peers - 1), w_out, [half_rows] * (2 * peers - 2))
     own = {offset: out[2 * i : 2 * i + 2] for i, offset in enumerate(offsets[:-1])}
     for step in range(far - 1, 0, -1):
         for to_right, to_left in ((1, 0), (0, 1)):
@@ -443,8 +434,10 @@
     )
     first = first_frame(queue_frames, gate_rows, near)
     handed = lax.ppermute(first, "segment", [(i, i - 1) for i in range(1, sections)])
-    rest = other_frames(queue_frames, gate_rows, near, later)
-    return (join(sections, rest, handed, fresh_frames), first[None, None])
+    return (
+        next_queue(queue_frames, gate_rows, handed, fresh_frames, near, later, sections),
+        first[None, None],
+    )
 
 
 def ring_order(mesh):

time: 87.5 us -> 83.5 us (0.954)
  waiting for transfers between devices: 28.8 us -> 17.9 us
  starting transfers between devices: 33.1 us -> 38.8 us
  local copies, waits for them, and re-layouts: 0.27 us -> 1.16 us
    ppermute x13 -> x14, waiting for transfers between devices: 14.1 us -> 7.3 us  [right(): lax.ppermute(x, 'seq', [(ring[i], ring[(i + 1) % peers]) for i in range(p...]
    ppermute x5 -> x6, waiting for transfers between devices: 6.71 us -> 2.07 us  [the longest x1 1.31 us: from_sections(): return [lax.ppermute(x, ('seq', 'segment'), route) for route in joint]]
    ppermute x13 -> x14, starting transfers between devices: 7.11 us -> 11.4 us  [left(): lax.ppermute(x, 'seq', [(ring[(i + 1) % peers], ring[i]) for i in range(p...]
    ppermute x5 -> x6, starting transfers between devices: 4 us -> 7.04 us  [the longest x3 5.34 us: shards(): arrived = lax.ppermute(own, 'seq', pairs)]
    ppermute x13 -> x14, starting transfers between devices: 20.7 us -> 19 us  [right(): lax.ppermute(x, 'seq', [(ring[i], ring[(i + 1) % peers]) for i in range(p...]
    ppermute x1, waiting for transfers between devices: 0.01 us -> 1.7 us  [shards(): lax.ppermute(first, 'segment', [(i, i - 1) for i in range(1, sections)])]
    ppermute x13 -> x14, waiting for transfers between devices: 7.96 us -> 6.82 us  [left(): lax.ppermute(x, 'seq', [(ring[(i + 1) % peers], ring[i]) for i in range(p...]
    slice x3 -> x2, local copies, waits for them, and re-layouts: 0.23 us -> 1.12 us  [the longest x1 1.11 us: shards(): halves = (queue_frames[:half_frames], queue_frames[half_frames:])]
  transfers between devices with their start and end apart: 32 -> 35, of which waited for: 21 -> 18; matrix products, arithmetic and copies ran while one was open for 0% -> 0% of each run, Pallas kernels for 20% -> 22%
where the time goes in v4:
time: 83.5 us; the launch traced here: 83.3 us
  starting transfers between devices  38.8 us (46%)
  Pallas kernels  24.5 us (29%)
  waiting for transfers between devices  17.9 us (21%)
  local copies, waits for them, and re-layouts  1.16 us (1%)
  between operations  0.91 us (1%)
    ppermute x14, starting transfers between devices, right(): lax.ppermute(x, 'seq', [(ring[i], ring[(i + 1) % peers]) for i in range(p...  19 us
    pallas_call x22, Pallas kernels, call(): pl.pallas_call(kernel, in_specs=[SCALARS] * scalars + [WHOLE] * (len(ins)...  18.5 us
    ppermute x14, starting transfers between devices, left(): lax.ppermute(x, 'seq', [(ring[(i + 1) % peers], ring[i]) for i in range(p...  11.4 us
    ppermute x14, waiting for transfers between devices, right(): lax.ppermute(x, 'seq', [(ring[i], ring[(i + 1) % peers]) for i in range(p...  7.3 us
    ppermute x14, waiting for transfers between devices, left(): lax.ppermute(x, 'seq', [(ring[(i + 1) % peers], ring[i]) for i in range(p...  6.82 us
    pallas_call x2, Pallas kernels, prepare(): pl.pallas_call(functools.partial(prepare_kernel, len(tables), len(arrays)...  6.06 us
    ppermute x3, starting transfers between devices, shards(): arrived = lax.ppermute(own, 'seq', pairs)  5.34 us
    ppermute x1, waiting for transfers between devices, shards(): lax.ppermute(first, 'segment', [(i, i - 1) for i in range(1, sections)])  1.7 us
  transfers between devices with their start and end apart: 35, of which 18 were waited for; matrix products, arithmetic and copies ran while one was open for 0% of the time, Pallas kernels for 22%

profile of v4, /device:TPU:0, one launch (start us, length us, event | category | flops | bytes accessed | tf_op | source)
XLA Modules:
  0.0 83.3 jit_solution(17181480983001220512)
XLA Ops:
  0.6 1.1 %fusion.1 = (bf16[4,4,5120]{2,1,0:T(4,128)(2,1)S(1)}, bf16[4,4,5120]{2,1,0:T(4,128)(2,1)S(1)}) fusion(bf16[8,4,5120]{2,1,0:T(4,128)(2,1)} %x_ref.3), kind=kLoop, calls=%fused_computation.3 | loop fusion | bytes 655360 | tf_op jit(solution)/shard_map/slice | solution.py:368
  1.7 3.1 %collective-permute-start = (bf16[4,4,5120]{2,1,0:T(4,128)(2,1)S(1)}, bf16[4,4,5120]{2,1,0:T(4,128)(2,1)S(1)}, u32[]{:S(2)}, u32[]{:S(2)}) collective-permute-start(bf16[4,4,5120]{2,1,0:T(4,128)(2,1)S(1)} %get-tuple-element.177), channel_id=1, source_target_pairs={{4,8},{8,12},{12,14},{14,10},{10,6},{6,2},{2,0},{0,4},{5,9},{9,13}... | collective-permute-start | bytes 491528 | tf_op jit(solution)/shard_map/ppermute | solution.py:345
  4.9 2.0 %collective-permute-start.4 = (bf16[4,4,5120]{2,1,0:T(4,128)(2,1)S(1)}, bf16[4,4,5120]{2,1,0:T(4,128)(2,1)S(1)}, u32[]{:S(2)}, u32[]{:S(2)}) collective-permute-start(bf16[4,4,5120]{2,1,0:T(4,128)(2,1)S(1)} %get-tuple-element.176), channel_id=1, source_target_pairs={{4,8},{8,12},{12,14},{14,10},{10,6},{6,2},{2,0},{0,4},{5,9},{9,13}... | collective-permute-start | bytes 491528 | tf_op jit(solution)/shard_map/ppermute | solution.py:345
  6.9 4.7 %shard_map.140 = (f32[8,5120]{1,0:T(8,128)S(1)}, f32[8,5120]{1,0:T(8,128)S(1)}, bf16[5120,512]{1,0:T(8,128)(2,1)S(1)}, bf16[5120,512]{1,0:T(8,128)(2,1)S(1)}) custom-call(s32[8]{0:T(128)} %level_in.2, f32[50,5120]{1,0:T(8,128)} %refs_0_.3, f32[50,5120]{1,0:T(8,128)} %refs_1_.1, bf16[5120,512]{1,0:T(8,128)(2,1)} %refs_2_.1, bf16[5120,512]{1,0:T(8,128)(2,1)} %refs_3_.1), custom_call_target="tpu_custom_call" | custom-call | flops 1000 | bytes 12533760 | tf_op jit(solution)/shard_map/pallas_call | solution.py:65
  11.9 1.8 %collective-permute-start.2 = (bf16[4,4,5120]{2,1,0:T(4,128)(2,1)S(1)}, bf16[4,4,5120]{2,1,0:T(4,128)(2,1)S(1)}, u32[]{:S(2)}, u32[]{:S(2)}) collective-permute-start(bf16[4,4,5120]{2,1,0:T(4,128)(2,1)S(1)} %collective-permute-done.refs_1_), channel_id=1, source_target_pairs={{4,8},{8,12},{12,14},{14,10},{10,6},{6,2},{2,0},{0,4},{5,9},{9,13}... | collective-permute-start | bytes 491528 | tf_op jit(solution)/shard_map/ppermute | solution.py:345
  14.0 1.8 %collective-permute-start.8 = (bf16[4,4,5120]{2,1,0:T(4,128)(2,1)S(1)}, bf16[4,4,5120]{2,1,0:T(4,128)(2,1)S(1)}, u32[]{:S(2)}, u32[]{:S(2)}) collective-permute-start(bf16[4,4,5120]{2,1,0:T(4,128)(2,1)S(1)} %collective-permute-done.4.refs_2_), channel_id=1, source_target_pairs={{4,8},{8,12},{12,14},{14,10},{10,6},{6,2},{2,0},{0,4},{5,9},{9,13}... | collective-permute-start | bytes 491528 | tf_op jit(solution)/shard_map/ppermute | solution.py:345
  16.0 2.7 %shard_map.141 = (f32[96,512]{1,0:T(8,128)S(1)}, f32[96,512]{1,0:T(8,128)S(1)}, f32[2,256]{1,0:T(2,128)S(1)}, bf16[96,5120]{1,0:T(8,128)(2,1)S(1)}) custom-call(bf16[8,4,5120]{2,1,0:T(4,128)(2,1)S(1)} %copy-done, bf16[4,4,5120]{2,1,0:T(4,128)(2,1)S(1)} %collective-permute-done.refs_1_, bf16[4,4,5120]{2,1,0:T(4,128)(2,1)S(1)} %collective-permute-done.4.refs_2_, ...), custom_call_target="tpu_custom_call" | custom-call | flops 1006632960 | bytes 13174784 | tf_op jit(solution)/shard_map/pallas_call | solution.py:23
  18.7 1.4 %collective-permute-done.3.refs_3_ = bf16[4,4,5120]{2,1,0:T(4,128)(2,1)S(1)} collective-permute-done((bf16[4,4,5120]{2,1,0:T(4,128)(2,1)S(1)}, bf16[4,4,5120]{2,1,0:T(4,128)(2,1)S(1)}, u32[]{:S(2)}, u32[]{:S(2)}) %collective-permute-start.3) | collective-permute-done | bytes 163872 | tf_op jit(solution)/shard_map/ppermute | solution.py:348
  20.0 1.6 %collective-permute-start.6 = (bf16[4,4,5120]{2,1,0:T(4,128)(2,1)S(1)}, bf16[4,4,5120]{2,1,0:T(4,128)(2,1)S(1)}, u32[]{:S(2)}, u32[]{:S(2)}) collective-permute-start(bf16[4,4,5120]{2,1,0:T(4,128)(2,1)S(1)} %collective-permute-done.2.refs_0_), channel_id=1, source_target_pairs={{4,8},{8,12},{12,14},{14,10},{10,6},{6,2},{2,0},{0,4},{5,9},{9,13}... | collective-permute-start | bytes 491528 | tf_op jit(solution)/shard_map/ppermute | solution.py:345
  22.0 1.6 %collective-permute-start.12 = (bf16[4,4,5120]{2,1,0:T(4,128)(2,1)S(1)}, bf16[4,4,5120]{2,1,0:T(4,128)(2,1)S(1)}, u32[]{:S(2)}, u32[]{:S(2)}) collective-permute-start(bf16[4,4,5120]{2,1,0:T(4,128)(2,1)S(1)} %collective-permute-done.8.refs_1_), channel_id=1, source_target_pairs={{4,8},{8,12},{12,14},{14,10},{10,6},{6,2},{2,0},{0,4},{5,9},{9,13}... | collective-permute-start | bytes 491528 | tf_op jit(solution)/shard_map/ppermute | solution.py:345
  23.6 0.4 collective-permute-start.13
  24.1 2.4 %shard_map.142 = (f32[64,512]{1,0:T(8,128)S(1)}, f32[64,512]{1,0:T(8,128)S(1)}, f32[2,256]{1,0:T(2,128)S(1)}, bf16[64,5120]{1,0:T(8,128)(2,1)S(1)}) custom-call(bf16[4,4,5120]{2,1,0:T(4,128)(2,1)S(1)} %collective-permute-done.2.refs_0_, bf16[4,4,5120]{2,1,0:T(4,128)(2,1)S(1)} %collective-permute-done.8.refs_1_, ...), custom_call_target="tpu_custom_call" | custom-call | flops 671088640 | bytes 12388352 | tf_op jit(solution)/shard_map/pallas_call | solution.py:23
  26.5 0.5 collective-permute-done.7.refs_3_
  27.0 1.6 %collective-permute-start.10 = (bf16[4,4,5120]{2,1,0:T(4,128)(2,1)S(1)}, bf16[4,4,5120]{2,1,0:T(4,128)(2,1)S(1)}, u32[]{:S(2)}, u32[]{:S(2)}) collective-permute-start(bf16[4,4,5120]{2,1,0:T(4,128)(2,1)S(1)} %collective-permute-done.6.refs_0_), channel_id=1, source_target_pairs={{4,8},{8,12},{12,14},{14,10},{10,6},{6,2},{2,0},{0,4},{5,9},{9,13}... | collective-permute-start | bytes 491528 | tf_op jit(solution)/shard_map/ppermute | solution.py:345
  29.1 1.6 %collective-permute-done.13.refs_2_ = bf16[4,4,5120]{2,1,0:T(4,128)(2,1)S(1)} collective-permute-done((bf16[4,4,5120]{2,1,0:T(4,128)(2,1)S(1)}, bf16[4,4,5120]{2,1,0:T(4,128)(2,1)S(1)}, u32[]{:S(2)}, u32[]{:S(2)}) %collective-permute-start.13) | collective-permute-done | bytes 163872 | tf_op jit(solution)/shard_map/ppermute | solution.py:348
  30.6 2.4 %shard_map.143 = (f32[64,512]{1,0:T(8,128)S(1)}, f32[64,512]{1,0:T(8,128)S(1)}, f32[2,256]{1,0:T(2,128)S(1)}, bf16[64,5120]{1,0:T(8,128)(2,1)S(1)}) custom-call(bf16[4,4,5120]{2,1,0:T(4,128)(2,1)S(1)} %collective-permute-done.6.refs_0_, bf16[4,4,5120]{2,1,0:T(4,128)(2,1)S(1)} %collective-permute-done.12.refs_1_, ...), custom_call_target="tpu_custom_call" | custom-call | flops 671088640 | bytes 12388352 | tf_op jit(solution)/shard_map/pallas_call | solution.py:23
  33.1 0.8 %collective-permute-done.11.refs_1_ = bf16[4,4,5120]{2,1,0:T(4,128)(2,1)S(1)} collective-permute-done((bf16[4,4,5120]{2,1,0:T(4,128)(2,1)S(1)}, bf16[4,4,5120]{2,1,0:T(4,128)(2,1)S(1)}, u32[]{:S(2)}, u32[]{:S(2)}) %collective-permute-start.11) | collective-permute-done | bytes 163872 | tf_op jit(solution)/shard_map/ppermute | solution.py:348
  33.9 2.2 %shard_map.144 = (f32[32,512]{1,0:T(8,128)S(1)}, f32[32,512]{1,0:T(8,128)S(1)}, f32[2,256]{1,0:T(2,128)S(1)}, bf16[32,5120]{1,0:T(8,128)(2,1)S(1)}) custom-call(bf16[4,4,5120]{2,1,0:T(4,128)(2,1)S(1)} %collective-permute-done.10.refs_0_, bf16[4,4,5120]{2,1,0:T(4,128)(2,1)S(1)} %collective-permute-done.11.refs_1_, ...), custom_call_target="tpu_custom_call" | custom-call | flops 335544320 | bytes 11601920 | tf_op jit(solution)/shard_map/pallas_call | solution.py:23
  36.2 0.5 collective-permute-start.14
  36.7 1.7 %collective-permute-start.16 = (f32[1,256]{1,0:T(1,128)S(1)}, f32[1,256]{1,0:T(1,128)S(1)}, u32[]{:S(2)}, u32[]{:S(2)}) collective-permute-start(f32[1,256]{1,0:T(1,128)S(1)} %slice.13), channel_id=1, source_target_pairs={{0,3},{1,2},{2,1},{3,0},{4,7},{5,6},{6,5},{7,4},{8,11},{9,10},{10,... | collective-permute-start | bytes 3080 | tf_op jit(solution)/shard_map/ppermute | solution.py:359
  38.4 1.3 %collective-permute-done.16 = f32[1,256]{1,0:T(1,128)S(1)} collective-permute-done((f32[1,256]{1,0:T(1,128)S(1)}, f32[1,256]{1,0:T(1,128)S(1)}, u32[]{:S(2)}, u32[]{:S(2)}) %collective-permute-start.16) | collective-permute-done | bytes 1056 | tf_op jit(solution)/shard_map/ppermute | solution.py:359
  39.8 1.7 %collective-permute-start.17 = (f32[3,256]{1,0:T(4,128)S(1)}, f32[3,256]{1,0:T(4,128)S(1)}, u32[]{:S(2)}, u32[]{:S(2)}) collective-permute-start(f32[3,256]{1,0:T(4,128)S(1)} %pad_maximum_fusion), channel_id=1, source_target_pairs={{0,4},{2,6},{4,0},{6,2},{8,12},{10,14},{12,8},{14,10},{1,5},{3,7},... | collective-permute-start | bytes 9224 | tf_op jit(solution)/shard_map/ppermute | solution.py:405
  41.6 1.6 %shard_map.145 = (bf16[256,512]{1,0:T(8,128)(2,1)S(1)}, bf16[2,256,512]{2,1,0:T(8,128)(2,1)S(1)}) custom-call(f32[96,512]{1,0:T(8,128)S(1)} %get-tuple-element.136.refs_0_, f32[64,512]{1,0:T(8,128)S(1)} %get-tuple-element.137.refs_1_, f32[64,512]{1,0:T(8,128)S(1)} %get-tuple-element.138.refs_2_, f32[32,512]{1,0:T(8,128)S(1)} %get-tuple-element.139.refs_3_, ...), custom_call_target="tpu_custom_call" | custom-call | flops 1342177280 | bytes 9703424 | tf_op jit(solution)/shard_map/pallas_call | solution.py:23
  43.5 3.1 %collective-permute-start.18 = (f32[3,256]{1,0:T(4,128)S(1)}, f32[3,256]{1,0:T(4,128)S(1)}, u32[]{:S(2)}, u32[]{:S(2)}) collective-permute-start(f32[3,256]{1,0:T(4,128)S(1)} %fusion), channel_id=1, source_target_pairs={{0,8},{2,10},{4,12},{6,14},{8,0},{10,2},{12,4},{14,6},{1,9},{3,11}... | collective-permute-start | bytes 9224 | tf_op jit(solution)/shard_map/ppermute | solution.py:405
  46.7 1.3 %shard_map.147.gate_ref = f32[8,5120]{1,0:T(8,128)S(1)} custom-call(s32[8]{0:T(128)} %level_in.2, f32[50,5120]{1,0:T(8,128)} %refs_0_.5), custom_call_target="tpu_custom_call" | custom-call | flops 1000 | bytes 1024000 | tf_op jit(solution)/shard_map/pallas_call | solution.py:65
  48.3 1.2 %shard_map.146 = (f32[4,256,512]{2,1,0:T(8,128)S(1)}, bf16[512,512]{1,0:T(8,128)(2,1)S(1)}) custom-call(s32[8]{0:T(128)S(1)} %copy-done.4, bf16[256,512]{1,0:T(8,128)(2,1)S(1)} %get-tuple-element.151.q_ref, bf16[2,256,512]{2,1,0:T(8,128)(2,1)S(1)} %get-tuple-element.152.refs_0_, bf16[2,256,512]{2,1,0:T(8,128)(2,1)S(1)} %collective-permute-done.19.refs_1_), custom_call_target="tpu_custom_call" | custom-call | flops 134217728 | bytes 3932192 | tf_op jit(solution)/shard_map/pallas_call | solution.py:23
  49.5 0.5 shard_map.150.att_ref
  50.0 1.0 %shard_map.151 = (bf16[16,5120]{1,0:T(8,128)(2,1)S(1)}, bf16[16,5120]{1,0:T(8,128)(2,1)S(1)}) custom-call(bf16[32,512]{1,0:T(8,128)(2,1)S(1)} %shard_map.150.att_ref, bf16[512,5120]{1,0:T(8,128)(2,1)S(1)} %bitcast.4), custom_call_target="tpu_custom_call" | custom-call | flops 167772160 | bytes 5603328 | tf_op jit(solution)/shard_map/pallas_call | solution.py:23
  51.0 1.5 %collective-permute-start.20 = (bf16[16,5120]{1,0:T(8,128)(2,1)S(1)}, bf16[16,5120]{1,0:T(8,128)(2,1)S(1)}, u32[]{:S(2)}, u32[]{:S(2)}) collective-permute-start(bf16[16,5120]{1,0:T(8,128)(2,1)S(1)} %get-tuple-element.164), channel_id=1, source_target_pairs={{4,8},{8,12},{12,14},{14,10},{10,6},{6,2},{2,0},{0,4},{5,9},{9,13}... | collective-permute-start | bytes 491528 | tf_op jit(solution)/shard_map/ppermute | solution.py:345
  52.5 0.6 collective-permute-start.31
  53.0 1.0 %shard_map.148.att_ref = bf16[224,512]{1,0:T(8,128)(2,1)S(1)} custom-call(f32[4,256,512]{2,1,0:T(8,128)S(1)} %get-tuple-element.157.scores_ref, bf16[512,512]{1,0:T(8,128)(2,1)S(1)} %get-tuple-element.158.values_ref, f32[3,256]{1,0:T(4,128)S(1)} %add.27.sq_ref), custom_call_target="tpu_custom_call" | custom-call | flops 117440512 | bytes 2853888 | tf_op jit(solution)/shard_map/pallas_call | solution.py:23
  54.1 1.4 %shard_map.149 = (bf16[16,5120]{1,0:T(8,128)(2,1)S(1)}, bf16[16,5120]{1,0:T(8,128)(2,1)S(1)}, bf16[16,5120]{1,0:T(8,128)(2,1)S(1)}, bf16[16,5120]{1,0:T(8,128)(2...) custom-call(bf16[224,512]{1,0:T(8,128)(2,1)S(1)} %shard_map.148.att_, ...), custom_call_target="tpu_custom_call" | custom-call | flops 1174405120 | bytes 7766016 | tf_op jit(solution)/shard_map/pallas_call | solution.py:23
  55.4 1.5 %collective-permute-start.24 = (bf16[16,5120]{1,0:T(8,128)(2,1)S(1)}, bf16[16,5120]{1,0:T(8,128)(2,1)S(1)}, u32[]{:S(2)}, u32[]{:S(2)}) collective-permute-start(bf16[16,5120]{1,0:T(8,128)(2,1)S(1)} %get-tuple-element.167), channel_id=1, source_target_pairs={{8,4},{12,8},{14,12},{10,14},{6,10},{2,6},{0,2},{4,0},{9,5},{13,9}... | collective-permute-start | bytes 491528 | tf_op jit(solution)/shard_map/ppermute | solution.py:348
  57.1 0.9 %collective-permute-start.21 = (bf16[16,5120]{1,0:T(8,128)(2,1)S(1)}, bf16[16,5120]{1,0:T(8,128)(2,1)S(1)}, u32[]{:S(2)}, u32[]{:S(2)}) collective-permute-start(bf16[16,5120]{1,0:T(8,128)(2,1)S(1)} %shard_map.152), channel_id=1, source_target_pairs={{4,8},{8,12},{12,14},{14,10},{10,6},{6,2},{2,0},{0,4},{5,9},{9,13}... | collective-permute-start | bytes 491528 | tf_op jit(solution)/shard_map/ppermute | solution.py:345
  58.0 2.0 %collective-permute-start.28 = (bf16[16,5120]{1,0:T(8,128)(2,1)S(1)}, bf16[16,5120]{1,0:T(8,128)(2,1)S(1)}, u32[]{:S(2)}, u32[]{:S(2)}) collective-permute-start(bf16[16,5120]{1,0:T(8,128)(2,1)S(1)} %get-tuple-element.171), channel_id=1, source_target_pairs={{4,8},{8,12},{12,14},{14,10},{10,6},{6,2},{2,0},{0,4},{5,9},{9,13}... | collective-permute-start | bytes 491528 | tf_op jit(solution)/shard_map/ppermute | solution.py:345
  60.1 2.0 %collective-permute-done.24.arrived_ref = bf16[16,5120]{1,0:T(8,128)(2,1)S(1)} collective-permute-done((bf16[16,5120]{1,0:T(8,128)(2,1)S(1)}, bf16[16,5120]{1,0:T(8,128)(2,1)S(1)}, u32[]{:S(2)}, u32[]{:S(2)}) %collective-permute-start.24) | collective-permute-done | bytes 163872 | tf_op jit(solution)/shard_map/ppermute | solution.py:348
  62.2 1.9 %collective-permute-start.25 = (bf16[16,5120]{1,0:T(8,128)(2,1)S(1)}, bf16[16,5120]{1,0:T(8,128)(2,1)S(1)}, u32[]{:S(2)}, u32[]{:S(2)}) collective-permute-start(bf16[16,5120]{1,0:T(8,128)(2,1)S(1)} %shard_map.155), channel_id=1, source_target_pairs={{8,4},{12,8},{14,12},{10,14},{6,10},{2,6},{0,2},{4,0},{9,5},{13,9}... | collective-permute-start | bytes 491528 | tf_op jit(solution)/shard_map/ppermute | solution.py:348
  64.7 3.0 %collective-permute-done.28.arrived_ref = bf16[16,5120]{1,0:T(8,128)(2,1)S(1)} collective-permute-done((bf16[16,5120]{1,0:T(8,128)(2,1)S(1)}, bf16[16,5120]{1,0:T(8,128)(2,1)S(1)}, u32[]{:S(2)}, u32[]{:S(2)}) %collective-permute-start.28) | collective-permute-done | bytes 163872 | tf_op jit(solution)/shard_map/ppermute | solution.py:345
  67.9 2.1 %collective-permute-start.33 = (bf16[16,5120]{1,0:T(8,128)(2,1)S(1)}, bf16[16,5120]{1,0:T(8,128)(2,1)S(1)}, u32[]{:S(2)}, u32[]{:S(2)}) collective-permute-start(bf16[16,5120]{1,0:T(8,128)(2,1)S(1)} %shard_map.161), channel_id=1, source_target_pairs={{8,4},{12,8},{14,12},{10,14},{6,10},{2,6},{0,2},{4,0},{9,5},{13,9}... | collective-permute-start | bytes 491528 | tf_op jit(solution)/shard_map/ppermute | solution.py:348
  70.0 1.5 %collective-permute-start.26 = (bf16[16,5120]{1,0:T(8,128)(2,1)S(1)}, bf16[16,5120]{1,0:T(8,128)(2,1)S(1)}, u32[]{:S(2)}, u32[]{:S(2)}) collective-permute-start(bf16[16,5120]{1,0:T(8,128)(2,1)S(1)} %shard_map.156), channel_id=1, source_target_pairs={{8,4},{12,8},{14,12},{10,14},{6,10},{2,6},{0,2},{4,0},{9,5},{13,9}... | collective-permute-start | bytes 491528 | tf_op jit(solution)/shard_map/ppermute | solution.py:348
  71.6 0.6 collective-permute-start.23
  72.2 2.7 %collective-permute-done.29.arrived_ref = bf16[16,5120]{1,0:T(8,128)(2,1)S(1)} collective-permute-done((bf16[16,5120]{1,0:T(8,128)(2,1)S(1)}, bf16[16,5120]{1,0:T(8,128)(2,1)S(1)}, u32[]{:S(2)}, u32[]{:S(2)}) %collective-permute-start.29) | collective-permute-done | bytes 163872 | tf_op jit(solution)/shard_map/ppermute | solution.py:345
  75.2 2.0 %collective-permute-start.34 = (bf16[16,5120]{1,0:T(8,128)(2,1)S(1)}, bf16[16,5120]{1,0:T(8,128)(2,1)S(1)}, u32[]{:S(2)}, u32[]{:S(2)}) collective-permute-start(bf16[16,5120]{1,0:T(8,128)(2,1)S(1)} %shard_map.162), channel_id=1, source_target_pairs={{8,4},{12,8},{14,12},{10,14},{6,10},{2,6},{0,2},{4,0},{9,5},{13,9}... | collective-permute-start | bytes 491528 | tf_op jit(solution)/shard_map/ppermute | solution.py:348
  77.2 1.1 %collective-permute-done.23.refs_1_ = bf16[16,5120]{1,0:T(8,128)(2,1)S(1)} collective-permute-done((bf16[16,5120]{1,0:T(8,128)(2,1)S(1)}, bf16[16,5120]{1,0:T(8,128)(2,1)S(1)}, u32[]{:S(2)}, u32[]{:S(2)}) %collective-permute-start.23) | collective-permute-done | bytes 163872 | tf_op jit(solution)/shard_map/ppermute | solution.py:345
  78.2 0.7 shard_map.157
  78.9 1.3 %collective-permute-start.27 = (bf16[4,5120]{1,0:T(4,128)(2,1)}, bf16[4,5120]{1,0:T(4,128)(2,1)S(1)}, u32[]{:S(2)}, u32[]{:S(2)}) collective-permute-start(bf16[4,5120]{1,0:T(4,128)(2,1)} %shard_map.157), channel_id=1, source_target_pairs={{1,0},{3,2},{5,4},{7,6},{9,8},{11,10},{13,12},{15,14},{17,16},{19,... | collective-permute-start | bytes 122888 | tf_op jit(solution)/shard_map/ppermute | solution.py:436
  80.5 1.7 %collective-permute-done.27.handed_ref = bf16[4,5120]{1,0:T(4,128)(2,1)S(1)} collective-permute-done((bf16[4,5120]{1,0:T(4,128)(2,1)}, bf16[4,5120]{1,0:T(4,128)(2,1)S(1)}, u32[]{:S(2)}, u32[]{:S(2)}) %collective-permute-start.27) | collective-permute-done | bytes 40992 | tf_op jit(solution)/shard_map/ppermute | solution.py:436
  82.2 1.1 %shard_map.163 = bf16[8,4,5120]{2,1,0:T(4,128)(2,1)} custom-call(bf16[8,4,5120]{2,1,0:T(4,128)(2,1)S(1)} %copy-done, f32[8,5120]{1,0:T(8,128)S(1)} %shard_map.147.gate_ref, bf16[4,5120]{1,0:T(4,128)(2,1)S(1)} %collective-permute-done.27.handed_ref, bf16[1,4,5120]{2,1,0:T(4,128)(2,1)S(1)} %copy-done.1, bf16[16,5120]{1,0:T(8,128)(2,1)S(1)} %get-tuple-element.160.refs_0_, ...), custom_call_target="tpu_custom_call" | custom-call | flops 655360 | bytes 1884160 | tf_op jit(solution)/shard_map/pallas_call | solution.py:23
  (74 shorter events, 4.3 us)
Async XLA Ops:
  1.7 9.9 %collective-permute-start = (bf16[4,4,5120]{2,1,0:T(4,128)(2,1)S(1)}, bf16[4,4,5120]{2,1,0:T(4,128)(2,1)S(1)}, u32[]{:S(2)}, u32[]{:S(2)}) collective-permute-start(bf16[4,4,5120]{2,1,0:T(4,128)(2,1)S(1)} %get-tuple-element.177), channel_id=1, source_target_pairs={{4,8},{8,12},{12,14},{14,10},{10,6},{6,2},{2,0},{0,4},{5,9},{9,13}... | collective-permute-start | bytes 491528 | tf_op jit(solution)/shard_map/ppermute | solution.py:345
  4.8 11.1 %copy-start = (bf16[8,4,5120]{2,1,0:T(4,128)(2,1)S(1)}, bf16[8,4,5120]{2,1,0:T(4,128)(2,1)}, u32[]{:S(2)}) copy-start(bf16[8,4,5120]{2,1,0:T(4,128)(2,1)} %x_ref.3) | copy-start | bytes 983044
  4.9 7.1 %collective-permute-start.1 = (bf16[4,4,5120]{2,1,0:T(4,128)(2,1)S(1)}, bf16[4,4,5120]{2,1,0:T(4,128)(2,1)S(1)}, u32[]{:S(2)}, u32[]{:S(2)}) collective-permute-start(bf16[4,4,5120]{2,1,0:T(4,128)(2,1)S(1)} %get-tuple-element.176), channel_id=1, source_target_pairs={{8,4},{12,8},{14,12},{10,14},{6,10},{2,6},{0,2},{4,0},{9,5},{13,9}... | collective-permute-start | bytes 491528 | tf_op jit(solution)/shard_map/ppermute | solution.py:348
  4.9 9.1 %collective-permute-start.4 = (bf16[4,4,5120]{2,1,0:T(4,128)(2,1)S(1)}, bf16[4,4,5120]{2,1,0:T(4,128)(2,1)S(1)}, u32[]{:S(2)}, u32[]{:S(2)}) collective-permute-start(bf16[4,4,5120]{2,1,0:T(4,128)(2,1)S(1)} %get-tuple-element.176), channel_id=1, source_target_pairs={{4,8},{8,12},{12,14},{14,10},{10,6},{6,2},{2,0},{0,4},{5,9},{9,13}... | collective-permute-start | bytes 491528 | tf_op jit(solution)/shard_map/ppermute | solution.py:345
  6.9 8.9 %collective-permute-start.5 = (bf16[4,4,5120]{2,1,0:T(4,128)(2,1)S(1)}, bf16[4,4,5120]{2,1,0:T(4,128)(2,1)S(1)}, u32[]{:S(2)}, u32[]{:S(2)}) collective-permute-start(bf16[4,4,5120]{2,1,0:T(4,128)(2,1)S(1)} %get-tuple-element.177), channel_id=1, source_target_pairs={{8,4},{12,8},{14,12},{10,14},{6,10},{2,6},{0,2},{4,0},{9,5},{13,9}... | collective-permute-start | bytes 491528 | tf_op jit(solution)/shard_map/ppermute | solution.py:348
  11.9 6.7 %collective-permute-start.2 = (bf16[4,4,5120]{2,1,0:T(4,128)(2,1)S(1)}, bf16[4,4,5120]{2,1,0:T(4,128)(2,1)S(1)}, u32[]{:S(2)}, u32[]{:S(2)}) collective-permute-start(bf16[4,4,5120]{2,1,0:T(4,128)(2,1)S(1)} %collective-permute-done.refs_1_), channel_id=1, source_target_pairs={{4,8},{8,12},{12,14},{14,10},{10,6},{6,2},{2,0},{0,4},{5,9},{9,13}... | collective-permute-start | bytes 491528 | tf_op jit(solution)/shard_map/ppermute | solution.py:345
  13.7 6.3 %collective-permute-start.3 = (bf16[4,4,5120]{2,1,0:T(4,128)(2,1)S(1)}, bf16[4,4,5120]{2,1,0:T(4,128)(2,1)S(1)}, u32[]{:S(2)}, u32[]{:S(2)}) collective-permute-start(bf16[4,4,5120]{2,1,0:T(4,128)(2,1)S(1)} %collective-permute-done.1.refs_4_), channel_id=1, source_target_pairs={{8,4},{12,8},{14,12},{10,14},{6,10},{2,6},{0,2},{4,0},{9,5},{13,9}... | collective-permute-start | bytes 491528 | tf_op jit(solution)/shard_map/ppermute | solution.py:348
  14.0 8.1 %collective-permute-start.8 = (bf16[4,4,5120]{2,1,0:T(4,128)(2,1)S(1)}, bf16[4,4,5120]{2,1,0:T(4,128)(2,1)S(1)}, u32[]{:S(2)}, u32[]{:S(2)}) collective-permute-start(bf16[4,4,5120]{2,1,0:T(4,128)(2,1)S(1)} %collective-permute-done.4.refs_2_), channel_id=1, source_target_pairs={{4,8},{8,12},{12,14},{14,10},{10,6},{6,2},{2,0},{0,4},{5,9},{9,13}... | collective-permute-start | bytes 491528 | tf_op jit(solution)/shard_map/ppermute | solution.py:345
  15.8 7.9 %collective-permute-start.9 = (bf16[4,4,5120]{2,1,0:T(4,128)(2,1)S(1)}, bf16[4,4,5120]{2,1,0:T(4,128)(2,1)S(1)}, u32[]{:S(2)}, u32[]{:S(2)}) collective-permute-start(bf16[4,4,5120]{2,1,0:T(4,128)(2,1)S(1)} %collective-permute-done.5.refs_3_), channel_id=1, source_target_pairs={{8,4},{12,8},{14,12},{10,14},{6,10},{2,6},{0,2},{4,0},{9,5},{13,9}... | collective-permute-start | bytes 491528 | tf_op jit(solution)/shard_map/ppermute | solution.py:348
  20.0 6.5 %collective-permute-start.6 = (bf16[4,4,5120]{2,1,0:T(4,128)(2,1)S(1)}, bf16[4,4,5120]{2,1,0:T(4,128)(2,1)S(1)}, u32[]{:S(2)}, u32[]{:S(2)}) collective-permute-start(bf16[4,4,5120]{2,1,0:T(4,128)(2,1)S(1)} %collective-permute-done.2.refs_0_), channel_id=1, source_target_pairs={{4,8},{8,12},{12,14},{14,10},{10,6},{6,2},{2,0},{0,4},{5,9},{9,13}... | collective-permute-start | bytes 491528 | tf_op jit(solution)/shard_map/ppermute | solution.py:345
  21.6 5.4 %collective-permute-start.7 = (bf16[4,4,5120]{2,1,0:T(4,128)(2,1)S(1)}, bf16[4,4,5120]{2,1,0:T(4,128)(2,1)S(1)}, u32[]{:S(2)}, u32[]{:S(2)}) collective-permute-start(bf16[4,4,5120]{2,1,0:T(4,128)(2,1)S(1)} %collective-permute-done.3.refs_3_), channel_id=1, source_target_pairs={{8,4},{12,8},{14,12},{10,14},{6,10},{2,6},{0,2},{4,0},{9,5},{13,9}... | collective-permute-start | bytes 491528 | tf_op jit(solution)/shard_map/ppermute | solution.py:348
  22.0 7.0 %collective-permute-start.12 = (bf16[4,4,5120]{2,1,0:T(4,128)(2,1)S(1)}, bf16[4,4,5120]{2,1,0:T(4,128)(2,1)S(1)}, u32[]{:S(2)}, u32[]{:S(2)}) collective-permute-start(bf16[4,4,5120]{2,1,0:T(4,128)(2,1)S(1)} %collective-permute-done.8.refs_1_), channel_id=1, source_target_pairs={{4,8},{8,12},{12,14},{14,10},{10,6},{6,2},{2,0},{0,4},{5,9},{9,13}... | collective-permute-start | bytes 491528 | tf_op jit(solution)/shard_map/ppermute | solution.py:345
  23.6 7.0 %collective-permute-start.13 = (bf16[4,4,5120]{2,1,0:T(4,128)(2,1)S(1)}, bf16[4,4,5120]{2,1,0:T(4,128)(2,1)S(1)}, u32[]{:S(2)}, u32[]{:S(2)}) collective-permute-start(bf16[4,4,5120]{2,1,0:T(4,128)(2,1)S(1)} %collective-permute-done.9.refs_2_), channel_id=1, source_target_pairs={{8,4},{12,8},{14,12},{10,14},{6,10},{2,6},{0,2},{4,0},{9,5},{13,9}... | collective-permute-start | bytes 491528 | tf_op jit(solution)/shard_map/ppermute | solution.py:348
  24.1 17.5 %slice-start.2 = ((s8[5242880]{0:T(1024)(128)(4,1)}), s8[4194304]{0:T(1024)(128)(4,1)S(1)}, s32[]{:S(2)}) async-start(s8[5242880]{0:T(1024)(128)(4,1)} %bitcast.5), calls=%async_computation.2 | async-start | bytes 8388608
  27.0 14.5 %slice-start.3 = ((s8[5242880]{0:T(1024)(128)(4,1)}), s8[1048576]{0:T(1024)(128)(4,1)S(1)}, s32[]{:S(2)}) async-start(s8[5242880]{0:T(1024)(128)(4,1)} %bitcast.5), calls=%async_computation.3 | async-start | bytes 2097152
  27.0 6.0 %collective-permute-start.10 = (bf16[4,4,5120]{2,1,0:T(4,128)(2,1)S(1)}, bf16[4,4,5120]{2,1,0:T(4,128)(2,1)S(1)}, u32[]{:S(2)}, u32[]{:S(2)}) collective-permute-start(bf16[4,4,5120]{2,1,0:T(4,128)(2,1)S(1)} %collective-permute-done.6.refs_0_), channel_id=1, source_target_pairs={{4,8},{8,12},{12,14},{14,10},{10,6},{6,2},{2,0},{0,4},{5,9},{9,13}... | collective-permute-start | bytes 491528 | tf_op jit(solution)/shard_map/ppermute | solution.py:345
  28.6 5.3 %collective-permute-start.11 = (bf16[4,4,5120]{2,1,0:T(4,128)(2,1)S(1)}, bf16[4,4,5120]{2,1,0:T(4,128)(2,1)S(1)}, u32[]{:S(2)}, u32[]{:S(2)}) collective-permute-start(bf16[4,4,5120]{2,1,0:T(4,128)(2,1)S(1)} %collective-permute-done.7.refs_3_), channel_id=1, source_target_pairs={{8,4},{12,8},{14,12},{10,14},{6,10},{2,6},{0,2},{4,0},{9,5},{13,9}... | collective-permute-start | bytes 491528 | tf_op jit(solution)/shard_map/ppermute | solution.py:348
  33.9 7.6 %copy-start.2 = (f32[512]{0:T(512)S(1)}, f32[512]{0:T(512)}, u32[]{:S(2)}) copy-start(f32[512]{0:T(512)} %param.24) | copy-start | bytes 6148
  33.9 7.6 %copy-start.3 = (f32[512]{0:T(512)S(1)}, f32[512]{0:T(512)}, u32[]{:S(2)}) copy-start(f32[512]{0:T(512)} %param.25) | copy-start | bytes 6148
  36.1 12.1 %copy-start.4 = (s32[8]{0:T(128)S(1)}, s32[8]{0:T(128)}, u32[]{:S(2)}) copy-start(s32[8]{0:T(128)} %start_ref.1) | copy-start | bytes 100
  36.2 3.7 %collective-permute-start.14 = (f32[2,256]{1,0:T(2,128)S(1)}, f32[2,256]{1,0:T(2,128)S(1)}, u32[]{:S(2)}, u32[]{:S(2)}) collective-permute-start(f32[2,256]{1,0:T(2,128)S(1)} %add_add_fusion), channel_id=1, source_target_pairs={{0,2},{2,0},{4,6},{6,4},{8,10},{10,8},{12,14},{14,12},{1,3},{3,1},... | collective-permute-start | bytes 6152 | tf_op jit(solution)/shard_map/ppermute | solution.py:399
  36.7 1.7 %collective-permute-start.15 = (f32[1,256]{1,0:T(1,128)S(1)}, f32[1,256]{1,0:T(1,128)S(1)}, u32[]{:S(2)}, u32[]{:S(2)}) collective-permute-start(f32[1,256]{1,0:T(1,128)S(1)} %slice.13), channel_id=1, source_target_pairs={{0,1},{1,0},{2,3},{3,2},{4,5},{5,4},{6,7},{7,6},{8,9},{9,8},{10,11... | collective-permute-start | bytes 3080 | tf_op jit(solution)/shard_map/ppermute | solution.py:357
  36.7 3.0 %collective-permute-start.16 = (f32[1,256]{1,0:T(1,128)S(1)}, f32[1,256]{1,0:T(1,128)S(1)}, u32[]{:S(2)}, u32[]{:S(2)}) collective-permute-start(f32[1,256]{1,0:T(1,128)S(1)} %slice.13), channel_id=1, source_target_pairs={{0,3},{1,2},{2,1},{3,0},{4,7},{5,6},{6,5},{7,4},{8,11},{9,10},{10,... | collective-permute-start | bytes 3080 | tf_op jit(solution)/shard_map/ppermute | solution.py:359
  39.8 3.7 %collective-permute-start.17 = (f32[3,256]{1,0:T(4,128)S(1)}, f32[3,256]{1,0:T(4,128)S(1)}, u32[]{:S(2)}, u32[]{:S(2)}) collective-permute-start(f32[3,256]{1,0:T(4,128)S(1)} %pad_maximum_fusion), channel_id=1, source_target_pairs={{0,4},{2,6},{4,0},{6,2},{8,12},{10,14},{12,8},{14,10},{1,5},{3,7},... | collective-permute-start | bytes 9224 | tf_op jit(solution)/shard_map/ppermute | solution.py:405
  41.5 8.4 %slice-start = ((s8[5242880]{0:T(1024)(128)(4,1)}), s8[4194304]{0:T(1024)(128)(4,1)S(1)}, s32[]{:S(2)}) async-start(s8[5242880]{0:T(1024)(128)(4,1)} %bitcast.3), calls=%async_computation | async-start | bytes 8388608
  41.6 8.4 %slice-start.1 = ((s8[5242880]{0:T(1024)(128)(4,1)}), s8[1048576]{0:T(1024)(128)(4,1)S(1)}, s32[]{:S(2)}) async-start(s8[5242880]{0:T(1024)(128)(4,1)} %bitcast.3), calls=%async_computation.1 | async-start | bytes 2097152
  43.5 4.8 %collective-permute-start.19 = (bf16[2,256,512]{2,1,0:T(8,128)(2,1)S(1)}, bf16[2,256,512]{2,1,0:T(8,128)(2,1)S(1)}, u32[]{:S(2)}, u32[]{:S(2)}) collective-permute-start(bf16[2,256,512]{2,1,0:T(8,128)(2,1)S(1)} %get-tuple-element.152.refs_0_), channel_id=1, source_target_pairs={{0,1},{1,0},{2,3},{3,2},{4,5},{5,4},{6,7},{7,6},{8,9},{9,8},{10,11... | collective-permute-start | bytes 1572872 | tf_op jit(solution)/shard_map/ppermute | solution.py:357
  43.5 4.7 %collective-permute-start.18 = (f32[3,256]{1,0:T(4,128)S(1)}, f32[3,256]{1,0:T(4,128)S(1)}, u32[]{:S(2)}, u32[]{:S(2)}) collective-permute-start(f32[3,256]{1,0:T(4,128)S(1)} %fusion), channel_id=1, source_target_pairs={{0,8},{2,10},{4,12},{6,14},{8,0},{10,2},{12,4},{14,6},{1,9},{3,11}... | collective-permute-start | bytes 9224 | tf_op jit(solution)/shard_map/ppermute | solution.py:405
  51.0 6.1 %collective-permute-start.20 = (bf16[16,5120]{1,0:T(8,128)(2,1)S(1)}, bf16[16,5120]{1,0:T(8,128)(2,1)S(1)}, u32[]{:S(2)}, u32[]{:S(2)}) collective-permute-start(bf16[16,5120]{1,0:T(8,128)(2,1)S(1)} %get-tuple-element.164), channel_id=1, source_target_pairs={{4,8},{8,12},{12,14},{14,10},{10,6},{6,2},{2,0},{0,4},{5,9},{9,13}... | collective-permute-start | bytes 491528 | tf_op jit(solution)/shard_map/ppermute | solution.py:345
  52.5 7.6 %collective-permute-start.31 = (bf16[16,5120]{1,0:T(8,128)(2,1)S(1)}, bf16[16,5120]{1,0:T(8,128)(2,1)S(1)}, u32[]{:S(2)}, u32[]{:S(2)}) collective-permute-start(bf16[16,5120]{1,0:T(8,128)(2,1)S(1)} %get-tuple-element.175), channel_id=1, source_target_pairs={{8,4},{12,8},{14,12},{10,14},{6,10},{2,6},{0,2},{4,0},{9,5},{13,9}... | collective-permute-start | bytes 491528 | tf_op jit(solution)/shard_map/ppermute | solution.py:348
  54.0 28.2 %copy-start.1 = (bf16[1,4,5120]{2,1,0:T(4,128)(2,1)S(1)}, bf16[1,4,5120]{2,1,0:T(4,128)(2,1)}, u32[]{:S(2)}) copy-start(bf16[1,4,5120]{2,1,0:T(4,128)(2,1)} %fresh_ref.1) | copy-start | bytes 122884
  55.4 6.7 %collective-permute-start.24 = (bf16[16,5120]{1,0:T(8,128)(2,1)S(1)}, bf16[16,5120]{1,0:T(8,128)(2,1)S(1)}, u32[]{:S(2)}, u32[]{:S(2)}) collective-permute-start(bf16[16,5120]{1,0:T(8,128)(2,1)S(1)} %get-tuple-element.167), channel_id=1, source_target_pairs={{8,4},{12,8},{14,12},{10,14},{6,10},{2,6},{0,2},{4,0},{9,5},{13,9}... | collective-permute-start | bytes 491528 | tf_op jit(solution)/shard_map/ppermute | solution.py:348
  57.1 7.1 %collective-permute-start.21 = (bf16[16,5120]{1,0:T(8,128)(2,1)S(1)}, bf16[16,5120]{1,0:T(8,128)(2,1)S(1)}, u32[]{:S(2)}, u32[]{:S(2)}) collective-permute-start(bf16[16,5120]{1,0:T(8,128)(2,1)S(1)} %shard_map.152), channel_id=1, source_target_pairs={{4,8},{8,12},{12,14},{14,10},{10,6},{6,2},{2,0},{0,4},{5,9},{9,13}... | collective-permute-start | bytes 491528 | tf_op jit(solution)/shard_map/ppermute | solution.py:345
  58.0 9.8 %collective-permute-start.28 = (bf16[16,5120]{1,0:T(8,128)(2,1)S(1)}, bf16[16,5120]{1,0:T(8,128)(2,1)S(1)}, u32[]{:S(2)}, u32[]{:S(2)}) collective-permute-start(bf16[16,5120]{1,0:T(8,128)(2,1)S(1)} %get-tuple-element.171), channel_id=1, source_target_pairs={{4,8},{8,12},{12,14},{14,10},{10,6},{6,2},{2,0},{0,4},{5,9},{9,13}... | collective-permute-start | bytes 491528 | tf_op jit(solution)/shard_map/ppermute | solution.py:345
  60.1 7.8 %collective-permute-start.32 = (bf16[16,5120]{1,0:T(8,128)(2,1)S(1)}, bf16[16,5120]{1,0:T(8,128)(2,1)S(1)}, u32[]{:S(2)}, u32[]{:S(2)}) collective-permute-start(bf16[16,5120]{1,0:T(8,128)(2,1)S(1)} %shard_map.160), channel_id=1, source_target_pairs={{8,4},{12,8},{14,12},{10,14},{6,10},{2,6},{0,2},{4,0},{9,5},{13,9}... | collective-permute-start | bytes 491528 | tf_op jit(solution)/shard_map/ppermute | solution.py:348
  62.2 7.8 %collective-permute-start.25 = (bf16[16,5120]{1,0:T(8,128)(2,1)S(1)}, bf16[16,5120]{1,0:T(8,128)(2,1)S(1)}, u32[]{:S(2)}, u32[]{:S(2)}) collective-permute-start(bf16[16,5120]{1,0:T(8,128)(2,1)S(1)} %shard_map.155), channel_id=1, source_target_pairs={{8,4},{12,8},{14,12},{10,14},{6,10},{2,6},{0,2},{4,0},{9,5},{13,9}... | collective-permute-start | bytes 491528 | tf_op jit(solution)/shard_map/ppermute | solution.py:348
  64.3 7.3 %collective-permute-start.22 = (bf16[16,5120]{1,0:T(8,128)(2,1)S(1)}, bf16[16,5120]{1,0:T(8,128)(2,1)S(1)}, u32[]{:S(2)}, u32[]{:S(2)}) collective-permute-start(bf16[16,5120]{1,0:T(8,128)(2,1)S(1)} %shard_map.153), channel_id=1, source_target_pairs={{4,8},{8,12},{12,14},{14,10},{10,6},{6,2},{2,0},{0,4},{5,9},{9,13}... | collective-permute-start | bytes 491528 | tf_op jit(solution)/shard_map/ppermute | solution.py:345
  67.8 7.1 %collective-permute-start.29 = (bf16[16,5120]{1,0:T(8,128)(2,1)S(1)}, bf16[16,5120]{1,0:T(8,128)(2,1)S(1)}, u32[]{:S(2)}, u32[]{:S(2)}) collective-permute-start(bf16[16,5120]{1,0:T(8,128)(2,1)S(1)} %shard_map.158), channel_id=1, source_target_pairs={{4,8},{8,12},{12,14},{14,10},{10,6},{6,2},{2,0},{0,4},{5,9},{9,13}... | collective-permute-start | bytes 491528 | tf_op jit(solution)/shard_map/ppermute | solution.py:345
  67.9 7.2 %collective-permute-start.33 = (bf16[16,5120]{1,0:T(8,128)(2,1)S(1)}, bf16[16,5120]{1,0:T(8,128)(2,1)S(1)}, u32[]{:S(2)}, u32[]{:S(2)}) collective-permute-start(bf16[16,5120]{1,0:T(8,128)(2,1)S(1)} %shard_map.161), channel_id=1, source_target_pairs={{8,4},{12,8},{14,12},{10,14},{6,10},{2,6},{0,2},{4,0},{9,5},{13,9}... | collective-permute-start | bytes 491528 | tf_op jit(solution)/shard_map/ppermute | solution.py:348
  70.0 7.1 %collective-permute-start.26 = (bf16[16,5120]{1,0:T(8,128)(2,1)S(1)}, bf16[16,5120]{1,0:T(8,128)(2,1)S(1)}, u32[]{:S(2)}, u32[]{:S(2)}) collective-permute-start(bf16[16,5120]{1,0:T(8,128)(2,1)S(1)} %shard_map.156), channel_id=1, source_target_pairs={{8,4},{12,8},{14,12},{10,14},{6,10},{2,6},{0,2},{4,0},{9,5},{13,9}... | collective-permute-start | bytes 491528 | tf_op jit(solution)/shard_map/ppermute | solution.py:348
  71.6 6.6 %collective-permute-start.23 = (bf16[16,5120]{1,0:T(8,128)(2,1)S(1)}, bf16[16,5120]{1,0:T(8,128)(2,1)S(1)}, u32[]{:S(2)}, u32[]{:S(2)}) collective-permute-start(bf16[16,5120]{1,0:T(8,128)(2,1)S(1)} %shard_map.154), channel_id=1, source_target_pairs={{4,8},{8,12},{12,14},{14,10},{10,6},{6,2},{2,0},{0,4},{5,9},{9,13}... | collective-permute-start | bytes 491528 | tf_op jit(solution)/shard_map/ppermute | solution.py:345
  75.0 5.4 %collective-permute-start.30 = (bf16[16,5120]{1,0:T(8,128)(2,1)S(1)}, bf16[16,5120]{1,0:T(8,128)(2,1)S(1)}, u32[]{:S(2)}, u32[]{:S(2)}) collective-permute-start(bf16[16,5120]{1,0:T(8,128)(2,1)S(1)} %shard_map.159), channel_id=1, source_target_pairs={{4,8},{8,12},{12,14},{14,10},{10,6},{6,2},{2,0},{0,4},{5,9},{9,13}... | collective-permute-start | bytes 491528 | tf_op jit(solution)/shard_map/ppermute | solution.py:345
  75.2 5.4 %collective-permute-start.34 = (bf16[16,5120]{1,0:T(8,128)(2,1)S(1)}, bf16[16,5120]{1,0:T(8,128)(2,1)S(1)}, u32[]{:S(2)}, u32[]{:S(2)}) collective-permute-start(bf16[16,5120]{1,0:T(8,128)(2,1)S(1)} %shard_map.162), channel_id=1, source_target_pairs={{8,4},{12,8},{14,12},{10,14},{6,10},{2,6},{0,2},{4,0},{9,5},{13,9}... | collective-permute-start | bytes 491528 | tf_op jit(solution)/shard_map/ppermute | solution.py:348
  78.9 3.3 %collective-permute-start.27 = (bf16[4,5120]{1,0:T(4,128)(2,1)}, bf16[4,5120]{1,0:T(4,128)(2,1)S(1)}, u32[]{:S(2)}, u32[]{:S(2)}) collective-permute-start(bf16[4,5120]{1,0:T(4,128)(2,1)} %shard_map.157), channel_id=1, source_target_pairs={{1,0},{3,2},{5,4},{7,6},{9,8},{11,10},{13,12},{15,14},{17,16},{19,... | collective-permute-start | bytes 122888 | tf_op jit(solution)/shard_map/ppermute | solution.py:436
